TPU v7x, 32 devices: a whole 2x2x4 slice. The times are simulated.
32 devices in a mesh: case: 2 (over y), brick: 4 (over z), sect: 2 (over x), slab: 2 (over core).
Axes of the slice: x: 2, y: 2, z: 4, core: 2. Of those that a mesh axis runs over, the one named last changes fastest.
Arguments:
- geometry: bfloat16 [64, 32, 32, 128], P(None, ('case', 'brick'), ('sect', 'slab')), parts along dimension 1, may hold values from -6 to 6
- conv_kernels: bfloat16 [1, 3, 3, 3, 64, 64], replicated, may hold values from -0.15625 to 0.15625
- point_place: float32 [3, 8192], P(None, ('case', 'brick', 'sect', 'slab')), parts along dimension 1, may hold values from 0 to 1
- point_attr: bfloat16 [8192, 64], P(('case', 'brick', 'sect', 'slab')), parts along dimension 0, may hold values from -6 to 6
- destination: int32 [8192, 1], P(('case', 'brick', 'sect', 'slab')), parts along dimension 0, may hold values from 0 to 7; in each aligned block of 256 rows (0 to 255, 256 to 511, ...) at most 40 rows name the same one
- dense_first: bfloat16 [2, 128, 512], replicated, may hold values from -1 to 1
- dense_middle: bfloat16 [2, 3, 512, 512], replicated, may hold values from -0.5 to 0.5
- dense_last: bfloat16 [2, 4, 512], replicated, may hold values from -0.25 to 0.25
Outputs:
- prediction: float32 [4, 10240], P(None, ('case', 'brick', 'sect', 'slab')), parts along dimension 1
There are 2 independent parts, one for each index of `case`. A program takes and returns all parts, laid end to end along the dimension named above; an argument that names none is the same for every part. Nothing has to cross between parts.
Inputs may be any that keep to these rules, and one draw needn't show every extreme that they name: A destination names a brick index and a sect index as brick * 2 + sect; its sect index fixes the point's section. No destination is named by more than 40 of the points of one device, and some device names some destination exactly 40 times.
All inputs are finite; a program needn't handle non-finite values.
Results may differ from a plain program's by a relative error of at most 0.0075.
Values may be sent and summed in bfloat16 or wider, within the bound.
No kernel may reach another device: no remote copies, remote signals or barrier semaphores. Data moves between devices by JAX's collectives and lax.ppermute only.
A program may use at most 64 MiB of HBM per device.

v0:
```python
import jax
import jax.numpy as jnp
from jax import lax
from jax.sharding import PartitionSpec as P


def extended(array, sides, width):
    for axis, dim in sides:
        size, length = (lax.axis_size(axis), array.shape[dim])
        up = [(i, (i + 1) % size) for i in range(size - 1)]
        down = [(j, i) for i, j in up]
        last = lax.slice_in_dim(array, length - width, length, axis=dim)
        leading = lax.slice_in_dim(array, 0, width, axis=dim)
        before = lax.ppermute(last, axis, up)
        after = lax.ppermute(leading, axis, down)
        array = jnp.concatenate([before, array, after], axis=dim)
    return array


def convolve(features_now, kernel):
    response = lax.conv_general_dilated(
        features_now[None],
        kernel,
        (1, 1, 1),
        ((0, 0), (0, 0), (1, 1)),
        dimension_numbers=("NCDHW", "DHWIO", "NCDHW"),
        preferred_element_type=jnp.float32,
    )
    return response[0]


def hat(offset):
    return jnp.maximum(0.0, 1.0 - jnp.abs(offset))


def network(table_rows, first_weights, middle_weights, last_weights):
    activity = jax.nn.gelu(
        jnp.dot(table_rows, first_weights, preferred_element_type=jnp.float32), approximate=True
    ).astype(jnp.bfloat16)
    for ordinal in range(middle_weights.shape[0]):
        activity = jax.nn.gelu(
            jnp.dot(activity, middle_weights[ordinal], preferred_element_type=jnp.float32),
            approximate=True,
        ).astype(jnp.bfloat16)
    return lax.dot_general(
        last_weights, activity, (((1,), (1,)), ((), ())), preferred_element_type=jnp.float32
    )


def on_device(
    geometry,
    conv_kernels,
    point_place,
    point_attr,
    destination,
    dense_first,
    dense_middle,
    dense_last,
):
    channels, span_x, span_y, span_z = geometry.shape
    features_now = geometry
    padded = extended(features_now, (("brick", 1), (("sect", "slab"), 2)), 1)
    response = convolve(padded, conv_kernels[0])
    features_now = (
        features_now.astype(jnp.float32) + jax.nn.gelu(response, approximate=True)
    ).astype(jnp.bfloat16)
    latent = extended(features_now, (("brick", 1), (("sect", "slab"), 2)), 1)
    extent_x = latent.shape[1]
    extent_y = latent.shape[2]
    count = point_place.shape[1]
    local_x = point_place[0] * span_x
    local_y = point_place[1] * span_y
    local_z = point_place[2] * span_z
    weight_x = hat(local_x[None, :] - (jnp.arange(extent_x, dtype=jnp.float32) - 0.5)[:, None])
    weight_y = hat(local_y[None, :] - (jnp.arange(extent_y, dtype=jnp.float32) - 0.5)[:, None])
    weight_z = hat(
        local_z[None, :] - (jnp.arange(span_z, dtype=jnp.float32) + 0.5)[:, None]
    ).astype(jnp.bfloat16)
    block_size = min(512, count)
    block_count = count // block_size
    flat_latent = latent.reshape(channels * extent_x * extent_y, span_z)

    def split_blocks(table):
        return table.reshape(table.shape[0], block_count, block_size).transpose(1, 0, 2)

    def sample(pieces):
        part_z, part_x, part_y = pieces
        partial_sum = jnp.dot(flat_latent, part_z, preferred_element_type=jnp.float32).reshape(
            channels, extent_x, extent_y, block_size
        )
        return jnp.einsum(
            "cxyp,xp,yp->pc", partial_sum, part_x, part_y, precision=lax.Precision.HIGHEST
        )

    sampled = lax.map(
        sample, (split_blocks(weight_z), split_blocks(weight_x), split_blocks(weight_y))
    )
    feature = sampled.reshape(count, channels).astype(jnp.bfloat16)
    table_rows = jnp.concatenate([feature, point_attr], axis=1)
    brick_count = lax.axis_size("brick")
    sect_count = lax.axis_size("sect")
    targets_all = brick_count * sect_count
    capacity = 5 * count // (4 * targets_all)
    target = destination[:, 0]
    onehot = (target[:, None] == jnp.arange(targets_all, dtype=jnp.int32)[None, :]).astype(
        jnp.int32
    )
    before = jnp.cumsum(onehot, axis=0) - onehot
    arrival = jnp.sum(before * onehot, axis=1)
    slot_index = target * capacity + arrival
    upper = target % sect_count >= sect_count // 2
    surface_value = network(table_rows, dense_first[0], dense_middle[0], dense_last[0])
    volume_value = network(table_rows, dense_first[1], dense_middle[1], dense_last[1])
    chosen = jnp.where(upper[None, :], volume_value, surface_value)
    outbox = (
        jnp.zeros((chosen.shape[0], targets_all * capacity), jnp.float32)
        .at[:, slot_index]
        .set(chosen)
    )
    prediction = lax.all_to_all(outbox, ("brick", "sect"), split_axis=1, concat_axis=1, tiled=True)
    return prediction


def solution(mesh):
    in_specs = (
        P(None, ("case", "brick"), ("sect", "slab"), None),
        P(),
        P(None, ("case", "brick", "sect", "slab")),
        P(("case", "brick", "sect", "slab"), None),
        P(("case", "brick", "sect", "slab"), None),
        P(),
        P(),
        P(),
    )
    out_specs = P(None, ("case", "brick", "sect", "slab"))
    return jax.shard_map(
        on_device, mesh=mesh, in_specs=in_specs, out_specs=out_specs, check_vma=False
    )
```

profile of v0, /device:TPU:0, one launch (start us, length us, event | category | flops | bytes accessed | tf_op | source)
XLA Modules:
  0.0 85.7 jit_solution(7794228538194470888)
XLA Ops:
  1.1 5.0 %collective-permute-start = (bf16[64,1,8,128]{3,0,2,1:T(8,128)(2,1)S(1)}, bf16[64,1,8,128]{3,0,2,1:T(8,128)(2,1)S(1)}, u32[]{:S(2)}, u32[]{:S(2)}) collective-permute-start(bf16[64,1,8,128]{3,0,2,1:T(8,128)(2,1)S(1)} %copy.73), channel_id=1, source_target_pairs={{0,4},{4,8},{8,12},{1,5},{5,9},{9,13},{2,6},{6,10},{10,14},{3,7},{... | collective-permute-start | bytes 393224 | tf_op jit(solution)/shard_map/ppermute | solution.py:14
  6.1 1.3 %collective-permute-start.1 = (bf16[64,1,8,128]{3,0,2,1:T(8,128)(2,1)S(1)}, bf16[64,1,8,128]{3,0,2,1:T(8,128)(2,1)S(1)}, u32[]{:S(2)}, u32[]{:S(2)}) collective-permute-start(bf16[64,1,8,128]{3,0,2,1:T(8,128)(2,1)S(1)} %copy.74), channel_id=1, source_target_pairs={{4,0},{8,4},{12,8},{5,1},{9,5},{13,9},{6,2},{10,6},{14,10},{7,3},{... | collective-permute-start | bytes 393224 | tf_op jit(solution)/shard_map/ppermute | solution.py:15
  10.7 1.3 %constant_dynamic-update-slice_fusion.1 = bf16[64,6,8,128]{3,0,2,1:T(8,128)(2,1)S(1)} fusion(bf16[64,6,8,128]{3,0,2,1:T(8,128)(2,1)S(1)} %constant_dynamic-update-slice_fusion.2, bf16[64,4,8,128]{3,2,1,0:T(8,128)(2,1)} %param.8), kind=kLoop, calls=%fused_computation.156 | loop fusion | bytes 1048576
  13.0 1.3 %collective-permute-start.2 = (bf16[64,6,1,128]{3,0,2,1:T(8,128)(2,1)S(1)}, bf16[64,6,1,128]{3,0,2,1:T(8,128)(2,1)S(1)}, u32[]{:S(2)}, u32[]{:S(2)}) collective-permute-start(bf16[64,6,1,128]{3,0,2,1:T(8,128)(2,1)S(1)} %get-tuple-element.26), channel_id=1, source_target_pairs={{0,1},{1,2},{2,3},{4,5},{5,6},{6,7},{8,9},{9,10},{10,11},{12,13},{... | collective-permute-start | bytes 294920 | tf_op jit(solution)/shard_map/ppermute | solution.py:14
  14.3 1.3 %collective-permute-start.3 = (bf16[64,6,1,128]{3,0,2,1:T(8,128)(2,1)S(1)}, bf16[64,6,1,128]{3,0,2,1:T(8,128)(2,1)S(1)}, u32[]{:S(2)}, u32[]{:S(2)}) collective-permute-start(bf16[64,6,1,128]{3,0,2,1:T(8,128)(2,1)S(1)} %get-tuple-element.28), channel_id=1, source_target_pairs={{1,0},{2,1},{3,2},{5,4},{6,5},{7,6},{9,8},{10,9},{11,10},{13,12},{... | collective-permute-start | bytes 294920 | tf_op jit(solution)/shard_map/ppermute | solution.py:15
  15.7 1.9 %copy.49 = bf16[64,4,8,128]{0,2,3,1:T(8,128)(2,1)} copy(bf16[64,4,8,128]{3,2,1,0:T(8,128)(2,1)S(1)} %copy-done.2) | data formatting | bytes 1048576 | tf_op args[0]
  17.6 1.7 %collective-permute-done.3 = bf16[64,6,1,128]{3,0,2,1:T(8,128)(2,1)S(1)} collective-permute-done((bf16[64,6,1,128]{3,0,2,1:T(8,128)(2,1)S(1)}, bf16[64,6,1,128]{3,0,2,1:T(8,128)(2,1)S(1)}, u32[]{:S(2)}, u32[]{:S(2)}) %collective-permute-start.3) | collective-permute-done | bytes 98336 | tf_op jit(solution)/shard_map/ppermute | solution.py:15
  20.5 2.1 %pad.clone = bf16[64,6,10,1,136]{0,4,2,1,3:T(8,128)(2,1)} pad(bf16[64,6,10,1,128]{0,4,2,1,3:T(8,128)(2,1)S(1)} %copy.71, bf16[]{:T(256)} %constant.40), padding=0_0x0_0x0_0x0_0x1_7 | pad | bytes 2027522 | tf_op jit(solution)/shard_map/broadcast_in_dim | solution.py:22
  22.6 3.6 %reshape.81 = bf16[64,6,10,1,8,17]{0,5,4,2,1,3:T(8,128)(2,1)S(1)} reshape(bf16[64,6,10,1,136]{0,4,2,1,3:T(8,128)(2,1)} %pad.clone) | data formatting | bytes 2088960 | tf_op jit(solution)/shard_map/conv_general_dilated | solution.py:21
  26.9 4.5 %fusion.17 = f32[4,8,8,17,64]{4,2,3,1,0:T(8,128)S(1)} fusion(bf16[64,6,10,1,7,2]{0,4,5,2,1,3:T(8,128)(2,1)S(1)} %slice.113, bf16[64,6,10,1,8,17]{0,4,5,2,1,3:T(8,128)(2,1)S(1)} %copy.55, pred[8,17]{0,1:T(8,128)(4,1)S(1)} %copy-done.7, bf16[1,3,3,3,64,64]{5,4,3,2,1,0:T(8,128)(2,1)S(1)} %copy-done), kind=kOutput, calls=%fused_computation.22 | convolution fusion | flops 966373376 | bytes 2487432 | tf_op jit(solution)/shard_map/conv_general_dilated | solution.py:21
  33.5 3.6 %collective-permute-start.4 = (bf16[64,1,8,128]{0,2,3,1:T(8,128)(2,1)S(1)}, bf16[64,1,8,128]{0,2,3,1:T(8,128)(2,1)S(1)}, u32[]{:S(2)}, u32[]{:S(2)}) collective-permute-start(bf16[64,1,8,128]{0,2,3,1:T(8,128)(2,1)S(1)} %get-tuple-element.17), channel_id=1, source_target_pairs={{0,4},{4,8},{8,12},{1,5},{5,9},{9,13},{2,6},{6,10},{10,14},{3,7},{... | collective-permute-start | bytes 393224 | tf_op jit(solution)/shard_map/ppermute | solution.py:14
  37.1 1.3 %collective-permute-start.5 = (bf16[64,1,8,128]{0,2,3,1:T(8,128)(2,1)S(1)}, bf16[64,1,8,128]{0,2,3,1:T(8,128)(2,1)S(1)}, u32[]{:S(2)}, u32[]{:S(2)}) collective-permute-start(bf16[64,1,8,128]{0,2,3,1:T(8,128)(2,1)S(1)} %get-tuple-element.24), channel_id=1, source_target_pairs={{4,0},{8,4},{12,8},{5,1},{9,5},{13,9},{6,2},{10,6},{14,10},{7,3},{... | collective-permute-start | bytes 393224 | tf_op jit(solution)/shard_map/ppermute | solution.py:15
  38.4 3.1 %collective-permute-done.4 = bf16[64,1,8,128]{0,2,3,1:T(8,128)(2,1)S(1)} collective-permute-done((bf16[64,1,8,128]{0,2,3,1:T(8,128)(2,1)S(1)}, bf16[64,1,8,128]{0,2,3,1:T(8,128)(2,1)S(1)}, u32[]{:S(2)}, u32[]{:S(2)}) %collective-permute-start.4) | collective-permute-done | bytes 131104 | tf_op jit(solution)/shard_map/ppermute | solution.py:14
  41.5 4.7 %collective-permute-done.5 = bf16[64,1,8,128]{0,2,3,1:T(8,128)(2,1)S(1)} collective-permute-done((bf16[64,1,8,128]{0,2,3,1:T(8,128)(2,1)S(1)}, bf16[64,1,8,128]{0,2,3,1:T(8,128)(2,1)S(1)}, u32[]{:S(2)}, u32[]{:S(2)}) %collective-permute-start.5) | collective-permute-done | bytes 131104 | tf_op jit(solution)/shard_map/ppermute | solution.py:15
  46.6 1.3 %fusion.191 = (bf16[64,6,1,128]{0,2,3,1:T(2,128)(2,1)}, bf16[64,6,1,128]{0,2,3,1:T(2,128)(2,1)S(1)}) fusion(bf16[64,6,8,128]{0,2,3,1:T(8,128)(2,1)S(1)} %pad_maximum_fusion), kind=kLoop, calls=%fused_computation.205 | loop fusion | bytes 393216 | tf_op jit(solution)/shard_map/slice | solution.py:12
  47.8 4.4 %collective-permute-start.6 = (bf16[64,6,1,128]{0,2,3,1:T(2,128)(2,1)}, bf16[64,6,1,128]{0,2,3,1:T(2,128)(2,1)}, u32[]{:S(2)}, u32[]{:S(2)}) collective-permute-start(bf16[64,6,1,128]{0,2,3,1:T(2,128)(2,1)} %get-tuple-element.15), channel_id=1, source_target_pairs={{0,1},{1,2},{2,3},{4,5},{5,6},{6,7},{8,9},{9,10},{10,11},{12,13},{... | collective-permute-start | bytes 294920 | tf_op jit(solution)/shard_map/ppermute | solution.py:14
  52.3 1.5 %collective-permute-start.7 = (bf16[64,6,1,128]{0,2,3,1:T(2,128)(2,1)S(1)}, bf16[64,6,1,128]{0,2,3,1:T(2,128)(2,1)}, u32[]{:S(2)}, u32[]{:S(2)}) collective-permute-start(bf16[64,6,1,128]{0,2,3,1:T(2,128)(2,1)S(1)} %get-tuple-element.16), channel_id=1, source_target_pairs={{1,0},{2,1},{3,2},{5,4},{6,5},{7,6},{9,8},{10,9},{11,10},{13,12},{... | collective-permute-start | bytes 294920 | tf_op jit(solution)/shard_map/ppermute | solution.py:15
  58.1 1.7 %fusion.42 = bf16[256,512]{1,0:T(8,128)(2,1)S(1)} fusion(bf16[2,3,512,512]{3,2,1,0:T(8,128)(2,1)} %param.14, bf16[2,128,512]{2,1,0:T(8,128)(2,1)S(1)} %copy-done.4, bf16[256,64]{0,1:T(8,128)(2,1)S(1)} %copy-done.5, bf16[256,64]{0,1:T(8,128)(2,1)S(1)} %multiply_reduce_fusion), kind=kOutput, calls=%fused_computation.55 | convolution fusion | flops 170262528 | bytes 983040 | tf_op jit(solution)/shard_map/dot_general | solution.py:42
  59.8 1.7 %fusion.75 = bf16[256,512]{1,0:T(8,128)(2,1)S(1)} fusion(bf16[2,3,512,512]{3,2,1,0:T(8,128)(2,1)} %param.14, bf16[2,128,512]{2,1,0:T(8,128)(2,1)S(1)} %copy-done.4, bf16[256,64]{0,1:T(8,128)(2,1)S(1)} %copy-done.5, bf16[256,64]{0,1:T(8,128)(2,1)S(1)} %multiply_reduce_fusion), kind=kOutput, calls=%fused_computation.88 | convolution fusion | flops 170262528 | bytes 983040 | tf_op jit(solution)/shard_map/dot_general | solution.py:42
  61.5 1.4 %fusion.50 = bf16[256,512]{1,0:T(8,128)(2,1)S(1)} fusion(bf16[256,512]{1,0:T(8,128)(2,1)S(1)} %fusion.42, bf16[2,3,512,512]{3,2,1,0:T(8,128)(2,1)} %param.14), kind=kOutput, calls=%fused_computation.63 | convolution fusion | flops 135397376 | bytes 1048576 | tf_op jit(solution)/shard_map/dot_general | solution.py:42
  63.0 1.4 %fusion.83 = bf16[256,512]{1,0:T(8,128)(2,1)S(1)} fusion(bf16[256,512]{1,0:T(8,128)(2,1)S(1)} %fusion.75, bf16[2,3,512,512]{3,2,1,0:T(8,128)(2,1)} %param.14), kind=kOutput, calls=%fused_computation.96 | convolution fusion | flops 135397376 | bytes 1048576 | tf_op jit(solution)/shard_map/dot_general | solution.py:42
  64.5 1.6 %fusion.108 = f32[256,4]{0,1:T(4,128)S(1)} fusion(bf16[256,512]{1,0:T(8,128)(2,1)S(1)} %fusion.50, bf16[2,3,512,512]{3,2,1,0:T(8,128)(2,1)} %param.14, bf16[2,4,512]{2,1,0:T(4,128)(2,1)S(1)} %copy-done.6), kind=kOutput, calls=%fused_computation.112 | convolution fusion | flops 136445952 | bytes 794624 | tf_op jit(solution)/shard_map/dot_general | solution.py:45
  66.0 1.6 %convolution_select_fusion = f32[256,4]{0,1:T(4,128)S(1)} fusion(f32[256,4]{0,1:T(4,128)S(1)} %fusion.108, bf16[256,512]{1,0:T(8,128)(2,1)S(1)} %fusion.83, bf16[2,3,512,512]{3,2,1,0:T(8,128)(2,1)} %param.14, bf16[2,4,512]{2,1,0:T(4,128)(2,1)S(1)} %copy-done.6, pred[256]{0:T(512)(128)(4,1)S(1)} %fusion.164), kind=kOutput, calls=%fused_computation.24 | convolution fusion | flops 136446976 | bytes 799232 | tf_op jit(solution)/shard_map/dot_general | solution.py:45
  69.2 14.6 %all_to_all.12 = f32[8,1,160]{2,1,0:T(1,128)S(1)} all-to-all(f32[8,1,160]{2,1,0:T(1,128)S(1)} %reshape.105), channel_id=1, replica_groups=mesh['case'=2,'brick'=4,'sect'=2,'slab'=2] {'brick','sect'}, dimensions={0} | all-to-all | bytes 10240 | tf_op jit(solution)/shard_map/all_to_all | solution.py:120
  (64 shorter events, 17.7 us)
Async XLA Ops:
  0.0 26.6 %copy-start = (bf16[1,3,3,3,64,64]{5,4,3,2,1,0:T(8,128)(2,1)S(1)}, bf16[1,3,3,3,64,64]{5,4,3,2,1,0:T(8,128)(2,1)}, u32[]{:S(2)}) copy-start(bf16[1,3,3,3,64,64]{5,4,3,2,1,0:T(8,128)(2,1)} %param.9) | copy-start | bytes 663556
  0.0 15.7 %copy-start.2 = (bf16[64,4,8,128]{3,2,1,0:T(8,128)(2,1)S(1)}, bf16[64,4,8,128]{3,2,1,0:T(8,128)(2,1)}, u32[]{:S(2)}) copy-start(bf16[64,4,8,128]{3,2,1,0:T(8,128)(2,1)} %param.8) | copy-start | bytes 1572868
  0.0 15.6 %copy-start.3 = (s32[256,1]{0,1:T(1,128)S(1)}, s32[256,1]{0,1:T(1,128)}, u32[]{:S(2)}) copy-start(s32[256,1]{0,1:T(1,128)} %param.12) | copy-start | bytes 3076
  1.1 9.6 %collective-permute-start = (bf16[64,1,8,128]{3,0,2,1:T(8,128)(2,1)S(1)}, bf16[64,1,8,128]{3,0,2,1:T(8,128)(2,1)S(1)}, u32[]{:S(2)}, u32[]{:S(2)}) collective-permute-start(bf16[64,1,8,128]{3,0,2,1:T(8,128)(2,1)S(1)} %copy.73), channel_id=1, source_target_pairs={{0,4},{4,8},{8,12},{1,5},{5,9},{9,13},{2,6},{6,10},{10,14},{3,7},{... | collective-permute-start | bytes 393224 | tf_op jit(solution)/shard_map/ppermute | solution.py:14
  6.1 6.9 %collective-permute-start.1 = (bf16[64,1,8,128]{3,0,2,1:T(8,128)(2,1)S(1)}, bf16[64,1,8,128]{3,0,2,1:T(8,128)(2,1)S(1)}, u32[]{:S(2)}, u32[]{:S(2)}) collective-permute-start(bf16[64,1,8,128]{3,0,2,1:T(8,128)(2,1)S(1)} %copy.74), channel_id=1, source_target_pairs={{4,0},{8,4},{12,8},{5,1},{9,5},{13,9},{6,2},{10,6},{14,10},{7,3},{... | collective-permute-start | bytes 393224 | tf_op jit(solution)/shard_map/ppermute | solution.py:15
  13.0 4.5 %collective-permute-start.2 = (bf16[64,6,1,128]{3,0,2,1:T(8,128)(2,1)S(1)}, bf16[64,6,1,128]{3,0,2,1:T(8,128)(2,1)S(1)}, u32[]{:S(2)}, u32[]{:S(2)}) collective-permute-start(bf16[64,6,1,128]{3,0,2,1:T(8,128)(2,1)S(1)} %get-tuple-element.26), channel_id=1, source_target_pairs={{0,1},{1,2},{2,3},{4,5},{5,6},{6,7},{8,9},{9,10},{10,11},{12,13},{... | collective-permute-start | bytes 294920 | tf_op jit(solution)/shard_map/ppermute | solution.py:14
  14.3 4.9 %collective-permute-start.3 = (bf16[64,6,1,128]{3,0,2,1:T(8,128)(2,1)S(1)}, bf16[64,6,1,128]{3,0,2,1:T(8,128)(2,1)S(1)}, u32[]{:S(2)}, u32[]{:S(2)}) collective-permute-start(bf16[64,6,1,128]{3,0,2,1:T(8,128)(2,1)S(1)} %get-tuple-element.28), channel_id=1, source_target_pairs={{1,0},{2,1},{3,2},{5,4},{6,5},{7,6},{9,8},{10,9},{11,10},{13,12},{... | collective-permute-start | bytes 294920 | tf_op jit(solution)/shard_map/ppermute | solution.py:15
  26.2 0.7 copy-start.7
  31.4 1.2 %copy-start.1 = (bf16[64,4,8,128]{0,2,3,1:T(8,128)(2,1)S(1)}, bf16[64,4,8,128]{0,2,3,1:T(8,128)(2,1)}, u32[]{:S(2)}) copy-start(bf16[64,4,8,128]{0,2,3,1:T(8,128)(2,1)} %copy.49) | copy-start | bytes 1572868
  33.5 8.0 %collective-permute-start.4 = (bf16[64,1,8,128]{0,2,3,1:T(8,128)(2,1)S(1)}, bf16[64,1,8,128]{0,2,3,1:T(8,128)(2,1)S(1)}, u32[]{:S(2)}, u32[]{:S(2)}) collective-permute-start(bf16[64,1,8,128]{0,2,3,1:T(8,128)(2,1)S(1)} %get-tuple-element.17), channel_id=1, source_target_pairs={{0,4},{4,8},{8,12},{1,5},{5,9},{9,13},{2,6},{6,10},{10,14},{3,7},{... | collective-permute-start | bytes 393224 | tf_op jit(solution)/shard_map/ppermute | solution.py:14
  37.1 9.1 %collective-permute-start.5 = (bf16[64,1,8,128]{0,2,3,1:T(8,128)(2,1)S(1)}, bf16[64,1,8,128]{0,2,3,1:T(8,128)(2,1)S(1)}, u32[]{:S(2)}, u32[]{:S(2)}) collective-permute-start(bf16[64,1,8,128]{0,2,3,1:T(8,128)(2,1)S(1)} %get-tuple-element.24), channel_id=1, source_target_pairs={{4,0},{8,4},{12,8},{5,1},{9,5},{13,9},{6,2},{10,6},{14,10},{7,3},{... | collective-permute-start | bytes 393224 | tf_op jit(solution)/shard_map/ppermute | solution.py:15
  47.8 6.9 %collective-permute-start.6 = (bf16[64,6,1,128]{0,2,3,1:T(2,128)(2,1)}, bf16[64,6,1,128]{0,2,3,1:T(2,128)(2,1)}, u32[]{:S(2)}, u32[]{:S(2)}) collective-permute-start(bf16[64,6,1,128]{0,2,3,1:T(2,128)(2,1)} %get-tuple-element.15), channel_id=1, source_target_pairs={{0,1},{1,2},{2,3},{4,5},{5,6},{6,7},{8,9},{9,10},{10,11},{12,13},{... | collective-permute-start | bytes 294920 | tf_op jit(solution)/shard_map/ppermute | solution.py:14
  52.3 3.7 %collective-permute-start.7 = (bf16[64,6,1,128]{0,2,3,1:T(2,128)(2,1)S(1)}, bf16[64,6,1,128]{0,2,3,1:T(2,128)(2,1)}, u32[]{:S(2)}, u32[]{:S(2)}) collective-permute-start(bf16[64,6,1,128]{0,2,3,1:T(2,128)(2,1)S(1)} %get-tuple-element.16), channel_id=1, source_target_pairs={{1,0},{2,1},{3,2},{5,4},{6,5},{7,6},{9,8},{10,9},{11,10},{13,12},{... | collective-permute-start | bytes 294920 | tf_op jit(solution)/shard_map/ppermute | solution.py:15
  57.2 1.0 %copy-start.4 = (bf16[2,128,512]{2,1,0:T(8,128)(2,1)S(1)}, bf16[2,128,512]{2,1,0:T(8,128)(2,1)}, u32[]{:S(2)}) copy-start(bf16[2,128,512]{2,1,0:T(8,128)(2,1)} %param.13) | copy-start | bytes 786436
  57.2 0.9 %copy-start.5 = (bf16[256,64]{0,1:T(8,128)(2,1)S(1)}, bf16[256,64]{0,1:T(8,128)(2,1)}, u32[]{:S(2)}) copy-start(bf16[256,64]{0,1:T(8,128)(2,1)} %param.11) | copy-start | bytes 98308
  61.5 2.9 %copy-start.6 = (bf16[2,4,512]{2,1,0:T(4,128)(2,1)S(1)}, bf16[2,4,512]{2,1,0:T(4,128)(2,1)}, u32[]{:S(2)}) copy-start(bf16[2,4,512]{2,1,0:T(4,128)(2,1)} %param.15) | copy-start | bytes 24580
where the time goes:
time: 86.6 us; the launch traced here: 85.7 us
  local copies, waits for them, and re-layouts  20.8 us (24%)
  starting transfers between devices  19.7 us (23%)
  matrix products  14.8 us (17%)
  blocking collectives  14.6 us (17%)
  waiting for transfers between devices  10.5 us (12%)
  other arithmetic  5.07 us (6%)
    all_to_all x1, blocking collectives, on_device(): lax.all_to_all(outbox, ('brick', 'sect'), split_axis=1, concat_axis=1, ti...  14.6 us
    ppermute x4, starting transfers between devices, extended(): before = lax.ppermute(last, axis, up)  14.3 us
    ppermute x4, waiting for transfers between devices, extended(): after = lax.ppermute(leading, axis, down)  7.42 us
    dot_general x4, matrix products, network(): jnp.dot(activity, middle_weights[ordinal], preferred_element_type=jnp.flo...  6.26 us
    unnamed x25, local copies, waits for them, and re-layouts  5.7 us
    ppermute x4, starting transfers between devices, extended(): after = lax.ppermute(leading, axis, down)  5.34 us
    conv_general_dilated x1, matrix products, convolve(): lax.conv_general_dilated(features_now[None], kernel, (1, 1, 1), ((0, 0),...  4.51 us
    conv_general_dilated x4, local copies, waits for them, and re-layouts, convolve(): lax.conv_general_dilated(features_now[None], kernel, (1, 1, 1), ((0, 0),...  4.4 us
  transfers between devices with their start and end apart: 8, of which 5 were waited for; matrix products, arithmetic and copies ran while one was open for 10% of the time, Pallas kernels for 0%

commit v1 on v0

v1 whole, which is shorter than its diff:
```python
import jax
import jax.numpy as jnp
from jax import lax
from jax.experimental import pallas as pl
from jax.experimental.pallas import tpu as pltpu
from jax.sharding import PartitionSpec as P

F32 = jnp.float32
BF16 = jnp.bfloat16
HALO = 2


def hat(offset):
    return jnp.maximum(0.0, 1.0 - jnp.abs(offset))


def gelu(value):
    return jax.nn.gelu(value, approximate=True)


def iota(shape, axis):
    return lax.broadcasted_iota(jnp.int32, shape, axis)


def call(body, outs, scratch, name, n_smem=0, n_any=0):
    def run(*args):
        spaces = (
            [pltpu.SMEM] * n_smem
            + [pltpu.VMEM] * (len(args) - n_smem - n_any)
            + [pl.ANY] * n_any
        )
        return pl.pallas_call(
            body,
            out_shape=outs,
            in_specs=[pl.BlockSpec(memory_space=s) for s in spaces],
            out_specs=jax.tree.map(lambda _: pl.BlockSpec(memory_space=pltpu.VMEM), outs),
            scratch_shapes=scratch,
            name=name,
            compiler_params=pltpu.CompilerParams(vmem_limit_bytes=48 << 20),
        )(*args)

    return run


def columns_body(g_ref, own_ref, up_ref, down_ref):
    span_x = g_ref.shape[1]
    for x in range(span_x):
        layer = jnp.swapaxes(g_ref[:, x].astype(F32), 0, 1).astype(BF16)
        own_ref[x] = layer
        if x < HALO:
            down_ref[x] = layer
        if x >= span_x - HALO:
            up_ref[x - (span_x - HALO)] = layer


def edges_body(own_ref, before_ref, after_ref, right_ref, left_ref):
    span_x, span_y = own_ref.shape[:2]
    for ref, base, span in (
        (before_ref, 0, HALO),
        (own_ref, HALO, span_x),
        (after_ref, HALO + span_x, HALO),
    ):
        right_ref[base : base + span] = ref[:, span_y - HALO :]
        left_ref[base : base + span] = ref[:, :HALO]


def make_points_body(span_x, span_y, bricks, sects, capacity):
    def body(flags_ref, place_ref, dest_ref, attr_ref, first_ref, pick_ref, wz_ref, wxy_ref, pre_ref):
        count = place_ref.shape[1]
        span_z = wz_ref.shape[0]
        slots = pick_ref.shape[0]
        half = slots // 2
        local_x = place_ref[0:1, :] * span_x
        local_y = place_ref[1:2, :] * span_y
        local_z = place_ref[2:3, :] * span_z
        cell_z = iota((span_z, count), 0).astype(F32) + 0.5
        wz_ref[...] = hat(local_z - cell_z).astype(BF16)
        weight_y = []
        for y in range(span_y + 2):
            w = hat(local_y - (y - 0.5))
            if y == 0:
                w = w * flags_ref[2].astype(F32)
            if y == span_y + 1:
                w = w * flags_ref[3].astype(F32)
            weight_y.append(w)
        for x in range(span_x + 2):
            w = hat(local_x - (x - 0.5))
            if x == 0:
                w = w * flags_ref[0].astype(F32)
            if x == span_x + 1:
                w = w * flags_ref[1].astype(F32)
            for y in range(span_y + 2):
                row = x * (span_y + 2) + y
                wxy_ref[row : row + 1, :] = w * weight_y[y]
        along = jnp.broadcast_to(dest_ref[...].astype(F32), (count, count))
        earlier, later = iota((count, count), 0), iota((count, count), 1)
        row = jnp.sum(jnp.where(earlier == later, along, 0.0), axis=0, keepdims=True)
        same = jnp.where((along == row) & (earlier < later), 1.0, 0.0)
        arrival = jnp.sum(same, axis=0, keepdims=True).astype(jnp.int32)
        target = row.astype(jnp.int32)
        brick, sect = target // sects, target % sects
        slot = (sect * bricks + brick) * capacity + arrival
        pick = jnp.where(iota((slots, count), 0) == slot, 1.0, 0.0).astype(BF16)
        pick_ref[...] = pick
        attr = jnp.dot(pick, attr_ref[...], preferred_element_type=F32).astype(BF16)
        channels = first_ref.shape[1] - attr.shape[1]
        for s in range(2):
            pre_ref[s * half : (s + 1) * half] = jnp.dot(
                attr[s * half : (s + 1) * half], first_ref[s, channels:], preferred_element_type=F32
            )

    return body


def main_body(
    own_ref, before_ref, after_ref, right_ref, left_ref, kernel_ref,
    pick_ref, wz_ref, wxy_ref, pre_ref, first_ref, last_ref, middle_hbm,
    value_ref, shifted, latent, middle_ref, sem,
):
    span_x, span_y, channels, span_z = own_ref.shape
    wide_x, wide_y = span_x + 2 * HALO, span_y + 2 * HALO
    out_x, out_y = span_x + 2, span_y + 2
    fetch = pltpu.make_async_copy(middle_hbm, middle_ref, sem)
    fetch.start()
    lane = iota((channels, span_z), 1)

    def column(x, y):
        if y < HALO:
            return left_ref[x, y]
        if y >= HALO + span_y:
            return right_ref[x, y - HALO - span_y]
        if x < HALO:
            return before_ref[x, y - HALO]
        if x >= HALO + span_x:
            return after_ref[x - HALO - span_x, y - HALO]
        return own_ref[x - HALO, y - HALO]

    def put(x):
        for y in range(wide_y):
            tile = column(x, y)
            wide = tile.astype(F32)
            lower = jnp.where(lane == 0, 0.0, pltpu.roll(wide, 1, 1)).astype(BF16)
            upper = jnp.where(lane == span_z - 1, 0.0, pltpu.roll(wide, span_z - 1, 1)).astype(BF16)
            for e, piece in enumerate((lower, tile, upper)):
                base = (x * 3 + e) * channels
                shifted[base : base + channels, y * span_z : (y + 1) * span_z] = piece

    put(0)
    put(1)
    total = jnp.zeros((channels, wz_ref.shape[1]), F32)
    for x in range(out_x):
        put(x + 2)
        rows = shifted[x * 3 * channels : (x + 3) * 3 * channels, :]
        part = jnp.dot(kernel_ref[...], rows, preferred_element_type=F32)
        for y in range(out_y):
            response = sum(
                part[b * channels : (b + 1) * channels, (y + b) * span_z : (y + b + 1) * span_z]
                for b in range(3)
            )
            centre = column(x + 1, y + 1).astype(F32)
            latent[y * channels : (y + 1) * channels, :] = (centre + gelu(response)).astype(BF16)
        sampled = jnp.dot(latent[...], wz_ref[...], preferred_element_type=F32)
        for y in range(out_y):
            row = x * out_y + y
            total += sampled[y * channels : (y + 1) * channels] * wxy_ref[row : row + 1, :]
    feature = lax.dot_general(
        pick_ref[...], total.astype(BF16), (((1,), (1,)), ((), ())), preferred_element_type=F32
    ).astype(BF16)
    fetch.wait()
    half = feature.shape[0] // 2
    for s in range(2):
        span = slice(s * half, (s + 1) * half)
        act = gelu(
            jnp.dot(feature[span], first_ref[s, :channels], preferred_element_type=F32)
            + pre_ref[span]
        ).astype(BF16)
        for i in range(middle_ref.shape[1]):
            act = gelu(jnp.dot(act, middle_ref[s, i], preferred_element_type=F32)).astype(BF16)
        value_ref[s] = lax.dot_general(
            last_ref[s], act, (((1,), (1,)), ((), ())), preferred_element_type=F32
        )


def shift(array, axes, step):
    size = lax.axis_size(axes)
    pairs = [(i, i + step) for i in range(size) if 0 <= i + step < size]
    return lax.ppermute(array, axes, pairs)


def swap_blocks(blocks, axis, dim):
    size = blocks.shape[dim]
    me = lax.axis_index(axis)
    lead, tail = blocks.shape[:dim], blocks.shape[dim + 1 :]
    step = size // 2
    while step:
        bit = (me // step) % 2
        split = blocks.reshape(lead + (size // (2 * step), 2, step) + tail)
        at = dim + 1
        sent = lax.dynamic_index_in_dim(split, 1 - bit, at, False)
        kept = lax.dynamic_index_in_dim(split, bit, at, False)
        got = lax.ppermute(sent, axis, [(i, i ^ step) for i in range(size)])
        split = jnp.stack(
            [jnp.where(bit == 0, kept, got), jnp.where(bit == 0, got, kept)], axis=at
        )
        blocks = split.reshape(lead + (size,) + tail)
        step //= 2
    return blocks


def on_device(
    geometry,
    conv_kernels,
    point_place,
    point_attr,
    destination,
    dense_first,
    dense_middle,
    dense_last,
):
    channels, span_x, span_y, span_z = geometry.shape
    count = point_place.shape[1]
    hidden = dense_first.shape[2]
    bricks, sects = lax.axis_size("brick"), lax.axis_size("sect")
    capacity = 5 * count // (4 * bricks * sects)
    slots = bricks * sects * capacity
    outputs = dense_last.shape[1]
    lines = ("sect", "slab")
    brick, line = lax.axis_index("brick"), lax.axis_index(lines)
    flags = jnp.stack(
        [brick > 0, brick < bricks - 1, line > 0, line < lax.axis_size(lines) - 1]
    ).astype(jnp.int32)
    kernel = conv_kernels[0].transpose(1, 4, 0, 2, 3).reshape(3 * channels, 9 * channels)

    def block(*shape):
        return jax.ShapeDtypeStruct(shape, BF16)

    own, up, down = call(
        columns_body,
        [
            block(span_x, span_y, channels, span_z),
            block(HALO, span_y, channels, span_z),
            block(HALO, span_y, channels, span_z),
        ],
        [],
        "columns",
    )(geometry)
    before = shift(up, "brick", 1)
    after = shift(down, "brick", -1)
    to_right, to_left = call(
        edges_body, [block(span_x + 2 * HALO, HALO, channels, span_z)] * 2, [], "edges"
    )(own, before, after)
    left = shift(to_right, lines, 1)
    right = shift(to_left, lines, -1)
    pick, wz, wxy, pre = call(
        make_points_body(span_x, span_y, bricks, sects, capacity),
        [
            block(slots, count),
            block(span_z, count),
            jax.ShapeDtypeStruct(((span_x + 2) * (span_y + 2), count), F32),
            jax.ShapeDtypeStruct((slots, hidden), F32),
        ],
        [],
        "points",
        n_smem=1,
    )(flags, point_place, destination, point_attr, dense_first)
    wide = (span_x + 2 * HALO) * 3 * channels
    value = call(
        main_body,
        jax.ShapeDtypeStruct((2, outputs, slots // 2), F32),
        [
            pltpu.VMEM((wide, (span_y + 2 * HALO) * span_z), BF16),
            pltpu.VMEM(((span_y + 2) * channels, span_z), BF16),
            pltpu.VMEM(dense_middle.shape, BF16),
            pltpu.SemaphoreType.DMA,
        ],
        "main",
        n_any=1,
    )(own, before, after, right, left, kernel, pick, wz, wxy, pre, dense_first, dense_last, dense_middle)
    value = value.transpose(1, 0, 2).reshape(outputs, sects, bricks, capacity)
    value = swap_blocks(value, "sect", 1)
    value = swap_blocks(value, "brick", 2)
    return value.transpose(0, 2, 1, 3).reshape(outputs, slots)


def solution(mesh):
    in_specs = (
        P(None, ("case", "brick"), ("sect", "slab"), None),
        P(),
        P(None, ("case", "brick", "sect", "slab")),
        P(("case", "brick", "sect", "slab"), None),
        P(("case", "brick", "sect", "slab"), None),
        P(),
        P(),
        P(),
    )
    out_specs = P(None, ("case", "brick", "sect", "slab"))
    return jax.shard_map(
        on_device, mesh=mesh, in_specs=in_specs, out_specs=out_specs, check_vma=False
    )
```

time: 86.6 us -> 55.7 us (0.64)
  matrix products: 14.8 us -> 0 us
  blocking collectives: 14.6 us -> 0 us
  Pallas kernels: 0 us -> 9.85 us
  local copies, waits for them, and re-layouts: 20.8 us -> 13.2 us
  other arithmetic: 5.07 us -> 0.15 us
  waiting for transfers between devices: 10.5 us -> 14.5 us
  starting transfers between devices: 19.7 us -> 17.3 us
    all_to_all x1 -> x0, blocking collectives: 14.6 us -> none  [on_device(): lax.all_to_all(outbox, ('brick', 'sect'), split_axis=1, concat_axis=1, ti...]
    dot_general x7 -> x0, matrix products: 10.2 us -> none  [the longest x4 6.26 us: network(): jnp.dot(activity, middle_weights[ordinal], preferred_element_type=jnp.flo...]
    pallas_call x0 -> x4, Pallas kernels: none -> 9.85 us  [run(): pl.pallas_call(body, out_shape=outs, in_specs=[pl.BlockSpec(memory_space=...]
    conv_general_dilated x1 -> x0, matrix products: 4.51 us -> none  [convolve(): lax.conv_general_dilated(features_now[None], kernel, (1, 1, 1), ((0, 0),...]
    conv_general_dilated x4 -> x0, local copies, waits for them, and re-layouts: 4.4 us -> none  [convolve(): lax.conv_general_dilated(features_now[None], kernel, (1, 1, 1), ((0, 0),...]
    ppermute x8 -> x7, waiting for transfers between devices: 10.5 us -> 14.5 us  [the longest x4 8.36 us: shift(): return lax.ppermute(array, axes, pairs)]
    reshape x0 -> x2, local copies, waits for them, and re-layouts: none -> 2.77 us  [the longest x1 2.08 us: on_device(): conv_kernels[0].transpose(1, 4, 0, 2, 3).reshape(3 * channels, 9 * channels)]
    slice x5 -> x0, local copies, waits for them, and re-layouts: 2.6 us -> none  [the longest x3 1.3 us: extended(): last = lax.slice_in_dim(array, length - width, length, axis=dim)]
  transfers between devices with their start and end apart: 8 -> 7, of which waited for: 5 -> 5; matrix products, arithmetic and copies ran while one was open for 10% -> 11% of each run, Pallas kernels for 0% -> 2%
where the time goes in v1:
time: 55.7 us; the launch traced here: 55.2 us
  starting transfers between devices  17.3 us (31%)
  waiting for transfers between devices  14.5 us (26%)
  local copies, waits for them, and re-layouts  13.2 us (24%)
  Pallas kernels  9.85 us (18%)
    ppermute x4, starting transfers between devices, shift(): return lax.ppermute(array, axes, pairs)  11.4 us
    pallas_call x4, Pallas kernels, run(): pl.pallas_call(body, out_shape=outs, in_specs=[pl.BlockSpec(memory_space=...  9.85 us
    ppermute x4, waiting for transfers between devices, shift(): return lax.ppermute(array, axes, pairs)  8.36 us
    unnamed x30, local copies, waits for them, and re-layouts  8.26 us
    ppermute x3, waiting for transfers between devices, swap_blocks(): got = lax.ppermute(sent, axis, [(i, i ^ step) for i in range(size)])  6.18 us
    ppermute x3, starting transfers between devices, swap_blocks(): got = lax.ppermute(sent, axis, [(i, i ^ step) for i in range(size)])  5.83 us
    reshape x1, local copies, waits for them, and re-layouts, on_device(): conv_kernels[0].transpose(1, 4, 0, 2, 3).reshape(3 * channels, 9 * channels)  2.08 us
    transpose x1, local copies, waits for them, and re-layouts, on_device(): conv_kernels[0].transpose(1, 4, 0, 2, 3).reshape(3 * channels, 9 * channels)  2.04 us
  transfers between devices with their start and end apart: 7, of which 5 were waited for; matrix products, arithmetic and copies ran while one was open for 11% of the time, Pallas kernels for 2%

profile of v1, /device:TPU:0, one launch (start us, length us, event | category | flops | bytes accessed | tf_op | source)
XLA Modules:
  0.0 55.2 jit_solution(9101609913181804057)
XLA Ops:
  0.0 1.1 %copy-done.9 = bf16[64,4,8,128]{3,2,1,0:T(8,128)(2,1)S(1)} copy-done((bf16[64,4,8,128]{3,2,1,0:T(8,128)(2,1)S(1)}, bf16[64,4,8,128]{3,2,1,0:T(8,128)(2,1)}, u32[]{:S(2)}) %copy-start.9) | copy-done | bytes 524312
  1.4 5.1 %collective-permute-start = (bf16[2,8,64,128]{3,2,1,0:T(8,128)(2,1)S(1)}, bf16[2,8,64,128]{3,2,1,0:T(8,128)(2,1)S(1)}, u32[]{:S(2)}, u32[]{:S(2)}) collective-permute-start(bf16[2,8,64,128]{3,2,1,0:T(8,128)(2,1)S(1)} %get-tuple-element.15), channel_id=1, source_target_pairs={{0,4},{4,8},{8,12},{1,5},{5,9},{9,13},{2,6},{6,10},{10,14},{3,7},{... | collective-permute-start | bytes 786440 | tf_op jit(solution)/shard_map/ppermute | solution.py:187
  6.5 1.3 %collective-permute-start.1 = (bf16[2,8,64,128]{3,2,1,0:T(8,128)(2,1)S(1)}, bf16[2,8,64,128]{3,2,1,0:T(8,128)(2,1)S(1)}, u32[]{:S(2)}, u32[]{:S(2)}) collective-permute-start(bf16[2,8,64,128]{3,2,1,0:T(8,128)(2,1)S(1)} %get-tuple-element.16), channel_id=1, source_target_pairs={{4,0},{8,4},{12,8},{5,1},{9,5},{13,9},{6,2},{10,6},{14,10},{7,3},{... | collective-permute-start | bytes 786440 | tf_op jit(solution)/shard_map/ppermute | solution.py:187
  7.8 4.2 %collective-permute-done.before_ref = bf16[2,8,64,128]{3,2,1,0:T(8,128)(2,1)S(1)} collective-permute-done((bf16[2,8,64,128]{3,2,1,0:T(8,128)(2,1)S(1)}, bf16[2,8,64,128]{3,2,1,0:T(8,128)(2,1)S(1)}, u32[]{:S(2)}, u32[]{:S(2)}) %collective-permute-start) | collective-permute-done | bytes 262176 | tf_op jit(solution)/shard_map/ppermute | solution.py:187
  12.0 4.1 %collective-permute-done.1.after_ref = bf16[2,8,64,128]{3,2,1,0:T(8,128)(2,1)S(1)} collective-permute-done((bf16[2,8,64,128]{3,2,1,0:T(8,128)(2,1)S(1)}, bf16[2,8,64,128]{3,2,1,0:T(8,128)(2,1)S(1)}, u32[]{:S(2)}, u32[]{:S(2)}) %collective-permute-start.1) | collective-permute-done | bytes 262176 | tf_op jit(solution)/shard_map/ppermute | solution.py:187
  16.1 0.9 %edges.1 = (bf16[8,2,64,128]{3,2,1,0:T(8,128)(2,1)}, bf16[8,2,64,128]{3,2,1,0:T(8,128)(2,1)}) custom-call(bf16[4,8,64,128]{3,2,1,0:T(8,128)(2,1)S(1)} %get-tuple-element.14.own_ref, bf16[2,8,64,128]{3,2,1,0:T(8,128)(2,1)S(1)} %collective-permute-done.before_ref, bf16[2,8,64,128]{3,2,1,0:T(8,128)(2,1)S(1)} %collective-permute-done.1.after_ref), custom_call_target="tpu_custom_call" | custom-call | tf_op jit(solution)/shard_map/edges/pallas_call | solution.py:32
  17.9 1.3 %collective-permute-start.2 = (bf16[8,2,64,128]{3,2,1,0:T(8,128)(2,1)}, bf16[8,2,64,128]{3,2,1,0:T(8,128)(2,1)}, u32[]{:S(2)}, u32[]{:S(2)}) collective-permute-start(bf16[8,2,64,128]{3,2,1,0:T(8,128)(2,1)} %get-tuple-element.17), channel_id=1, source_target_pairs={{1,0},{2,1},{3,2},{5,4},{6,5},{7,6},{9,8},{10,9},{11,10},{13,12},{... | collective-permute-start | bytes 786440 | tf_op jit(solution)/shard_map/ppermute | solution.py:187
  19.2 3.8 %collective-permute-start.3 = (bf16[8,2,64,128]{3,2,1,0:T(8,128)(2,1)}, bf16[8,2,64,128]{3,2,1,0:T(8,128)(2,1)}, u32[]{:S(2)}, u32[]{:S(2)}) collective-permute-start(bf16[8,2,64,128]{3,2,1,0:T(8,128)(2,1)} %get-tuple-element.18), channel_id=1, source_target_pairs={{0,1},{1,2},{2,3},{4,5},{5,6},{6,7},{8,9},{9,10},{10,11},{12,13},{... | collective-permute-start | bytes 786440 | tf_op jit(solution)/shard_map/ppermute | solution.py:187
  22.9 2.0 %copy.23 = bf16[3,64,3,3,64]{4,3,2,1,0:T(4,128)(2,1)} copy(bf16[3,64,3,3,64]{1,4,3,0,2:T(8,128)(2,1)} %bitcast.49) | data formatting | bytes 442368 | tf_op jit(solution)/shard_map/transpose | solution.py:232
  25.0 2.1 %reshape.17.kernel_ref = bf16[192,576]{1,0:T(8,128)(2,1)} reshape(bf16[3,64,3,3,64]{4,3,2,1,0:T(4,128)(2,1)} %copy.23) | data formatting | bytes 442368 | tf_op jit(solution)/shard_map/reshape | solution.py:232
  27.2 1.5 %copy.25.attr_ref = bf16[256,64]{1,0:T(8,128)(2,1)} copy(bf16[256,64]{0,1:T(8,128)(2,1)} %param.11) | data formatting | bytes 65536 | tf_op args[3]
  28.8 0.8 %copy-done.10 = bf16[256,64]{1,0:T(8,128)(2,1)S(1)} copy-done((bf16[256,64]{1,0:T(8,128)(2,1)S(1)}, bf16[256,64]{1,0:T(8,128)(2,1)}, u32[]{:S(2)}) %copy-start.10) | copy-done | bytes 32792
  29.6 1.1 %points.1 = (bf16[320,256]{1,0:T(8,128)(2,1)S(1)}, bf16[128,256]{1,0:T(8,128)(2,1)S(1)}, f32[60,256]{1,0:T(8,128)S(1)}, f32[320,512]{1,0:T(8,128)S(1)}) custom-call(s32[4]{0:T(128)S(1)} %add_convert_fusion.flags_ref, f32[3,256]{1,0:T(4,128)S(1)} %copy-done.12, s32[256,1]{1,0:T(8,128)S(1)} %copy.24.dest_ref, bf16[256,64]{1,0:T(8,128)(2,1)S(1)} %copy-done.10, ...), custom_call_target="tpu_custom_call" | custom-call | tf_op jit(solution)/shard_map/points/pallas_call | solution.py:32
  30.8 1.0 %copy-done.2 = bf16[4,8,64,128]{3,2,1,0:T(8,128)(2,1)S(1)} copy-done((bf16[4,8,64,128]{3,2,1,0:T(8,128)(2,1)S(1)}, bf16[4,8,64,128]{3,2,1,0:T(8,128)(2,1)}, u32[]{:S(2)}) %copy-start.2) | copy-done | bytes 524312
  31.8 0.9 %copy-done.5 = bf16[2,8,64,128]{3,2,1,0:T(8,128)(2,1)S(1)} copy-done((bf16[2,8,64,128]{3,2,1,0:T(8,128)(2,1)S(1)}, bf16[2,8,64,128]{3,2,1,0:T(8,128)(2,1)}, u32[]{:S(2)}) %copy-start.5) | copy-done | bytes 262168
  32.7 0.9 %copy-done.7 = bf16[2,8,64,128]{3,2,1,0:T(8,128)(2,1)S(1)} copy-done((bf16[2,8,64,128]{3,2,1,0:T(8,128)(2,1)S(1)}, bf16[2,8,64,128]{3,2,1,0:T(8,128)(2,1)}, u32[]{:S(2)}) %copy-start.7) | copy-done | bytes 262168
  33.7 0.9 %copy-done.8 = bf16[192,576]{1,0:T(8,128)(2,1)S(1)} copy-done((bf16[192,576]{1,0:T(8,128)(2,1)S(1)}, bf16[192,576]{1,0:T(8,128)(2,1)}, u32[]{:S(2)}) %copy-start.8) | copy-done | bytes 221208
  34.6 7.6 %main.1 = f32[2,4,160]{2,1,0:T(4,128)S(1)} custom-call(bf16[4,8,64,128]{3,2,1,0:T(8,128)(2,1)S(1)} %copy-done.2, bf16[2,8,64,128]{3,2,1,0:T(8,128)(2,1)S(1)} %copy-done.5, bf16[2,8,64,128]{3,2,1,0:T(8,128)(2,1)S(1)} %copy-done.7, bf16[8,2,64,128]{3,2,1,0:T(8,128)(2,1)} %collective-permute-done.2.right_ref, ...), custom_call_target="tpu_custom_call" | custom-call | tf_op jit(solution)/shard_map/main/pallas_call | solution.py:32
  42.3 1.6 %collective-permute-start.4 = (f32[4,1,1,4,40]{4,3,0,2,1:T(4,128)S(1)}, f32[4,1,1,4,40]{4,3,0,2,1:T(4,128)S(1)}, u32[]{:S(2)}, u32[]{:S(2)}) collective-permute-start(f32[4,1,1,4,40]{4,3,0,2,1:T(4,128)S(1)} %dynamic-slice_bitcast_fusion), channel_id=1, source_target_pairs={{0,2},{2,0},{1,3},{3,1},{4,6},{6,4},{5,7},{7,5},{8,10},{10,8},{9,1... | collective-permute-start | bytes 7688 | tf_op jit(solution)/shard_map/ppermute | solution.py:201
  43.9 2.1 %collective-permute-done.4 = f32[4,1,1,4,40]{4,3,0,2,1:T(4,128)S(1)} collective-permute-done((f32[4,1,1,4,40]{4,3,0,2,1:T(4,128)S(1)}, f32[4,1,1,4,40]{4,3,0,2,1:T(4,128)S(1)}, u32[]{:S(2)}, u32[]{:S(2)}) %collective-permute-start.4) | collective-permute-done | bytes 2592 | tf_op jit(solution)/shard_map/ppermute | solution.py:201
  46.0 2.6 %collective-permute-start.5 = (f32[4,2,1,2,40]{4,3,1,0,2:T(2,128)S(1)}, f32[4,2,1,2,40]{4,3,1,0,2:T(2,128)S(1)}, u32[]{:S(2)}, u32[]{:S(2)}) collective-permute-start(f32[4,2,1,2,40]{4,3,1,0,2:T(2,128)S(1)} %bitcast.53), channel_id=1, source_target_pairs={{0,8},{4,12},{8,0},{12,4},{1,9},{5,13},{9,1},{13,5},{2,10},{6,14},... | collective-permute-start | bytes 7688 | tf_op jit(solution)/shard_map/ppermute | solution.py:201
  48.7 2.0 %collective-permute-done.5 = f32[4,2,1,2,40]{4,3,1,0,2:T(2,128)S(1)} collective-permute-done((f32[4,2,1,2,40]{4,3,1,0,2:T(2,128)S(1)}, f32[4,2,1,2,40]{4,3,1,0,2:T(2,128)S(1)}, u32[]{:S(2)}, u32[]{:S(2)}) %collective-permute-start.5) | collective-permute-done | bytes 2592 | tf_op jit(solution)/shard_map/ppermute | solution.py:201
  50.7 1.6 %collective-permute-start.6 = (f32[4,2,2,1,40]{4,2,1,0,3:T(2,128)S(1)}, f32[4,2,2,1,40]{4,2,1,0,3:T(2,128)S(1)}, u32[]{:S(2)}, u32[]{:S(2)}) collective-permute-start(f32[4,2,2,1,40]{4,2,1,0,3:T(2,128)S(1)} %bitcast.54), channel_id=1, source_target_pairs={{0,4},{4,0},{8,12},{12,8},{1,5},{5,1},{9,13},{13,9},{2,6},{6,2},{1... | collective-permute-start | bytes 7688 | tf_op jit(solution)/shard_map/ppermute | solution.py:201
  52.3 2.1 %collective-permute-done.6 = f32[4,2,2,1,40]{4,2,1,0,3:T(2,128)S(1)} collective-permute-done((f32[4,2,2,1,40]{4,2,1,0,3:T(2,128)S(1)}, f32[4,2,2,1,40]{4,2,1,0,3:T(2,128)S(1)}, u32[]{:S(2)}, u32[]{:S(2)}) %collective-permute-start.6) | collective-permute-done | bytes 2592 | tf_op jit(solution)/shard_map/ppermute | solution.py:201
  (40 shorter events, 2.2 us)
Async XLA Ops:
  0.0 28.8 %copy-start.3 = (bf16[2,128,512]{2,1,0:T(8,128)(2,1)S(1)}, bf16[2,128,512]{2,1,0:T(8,128)(2,1)}, u32[]{:S(2)}) copy-start(bf16[2,128,512]{2,1,0:T(8,128)(2,1)} %first_ref.3) | copy-start | bytes 786436
  0.0 1.1 %copy-start.9 = (bf16[64,4,8,128]{3,2,1,0:T(8,128)(2,1)S(1)}, bf16[64,4,8,128]{3,2,1,0:T(8,128)(2,1)}, u32[]{:S(2)}) copy-start(bf16[64,4,8,128]{3,2,1,0:T(8,128)(2,1)} %g_ref.1) | copy-start | bytes 1572868
  1.1 26.0 %copy-start.13 = (s32[256,1]{0,1:T(1,128)S(1)}, s32[256,1]{0,1:T(1,128)}, u32[]{:S(2)}) copy-start(s32[256,1]{0,1:T(1,128)} %param.12) | copy-start | bytes 3076
  1.1 27.7 %copy-start.12 = (f32[3,256]{1,0:T(4,128)S(1)}, f32[3,256]{1,0:T(4,128)}, u32[]{:S(2)}) copy-start(f32[3,256]{1,0:T(4,128)} %place_ref.1) | copy-start | bytes 9220
  1.1 29.6 %copy-start = (bf16[2,3,512,512]{3,2,1,0:T(8,128)(2,1)S(1)}, bf16[2,3,512,512]{3,2,1,0:T(8,128)(2,1)}, u32[]{:S(2)}) copy-start(bf16[2,3,512,512]{3,2,1,0:T(8,128)(2,1)} %middle_hbm.1) | copy-start | bytes 9437188
  1.1 29.6 %copy-start.11 = (bf16[2,4,512]{2,1,0:T(4,128)(2,1)S(1)}, bf16[2,4,512]{2,1,0:T(4,128)(2,1)}, u32[]{:S(2)}) copy-start(bf16[2,4,512]{2,1,0:T(4,128)(2,1)} %last_ref.1) | copy-start | bytes 24580
  1.4 10.6 %collective-permute-start = (bf16[2,8,64,128]{3,2,1,0:T(8,128)(2,1)S(1)}, bf16[2,8,64,128]{3,2,1,0:T(8,128)(2,1)S(1)}, u32[]{:S(2)}, u32[]{:S(2)}) collective-permute-start(bf16[2,8,64,128]{3,2,1,0:T(8,128)(2,1)S(1)} %get-tuple-element.15), channel_id=1, source_target_pairs={{0,4},{4,8},{8,12},{1,5},{5,9},{9,13},{2,6},{6,10},{10,14},{3,7},{... | collective-permute-start | bytes 786440 | tf_op jit(solution)/shard_map/ppermute | solution.py:187
  6.5 9.7 %collective-permute-start.1 = (bf16[2,8,64,128]{3,2,1,0:T(8,128)(2,1)S(1)}, bf16[2,8,64,128]{3,2,1,0:T(8,128)(2,1)S(1)}, u32[]{:S(2)}, u32[]{:S(2)}) collective-permute-start(bf16[2,8,64,128]{3,2,1,0:T(8,128)(2,1)S(1)} %get-tuple-element.16), channel_id=1, source_target_pairs={{4,0},{8,4},{12,8},{5,1},{9,5},{13,9},{6,2},{10,6},{14,10},{7,3},{... | collective-permute-start | bytes 786440 | tf_op jit(solution)/shard_map/ppermute | solution.py:187
  12.0 5.1 %copy-start.4 = (bf16[2,8,64,128]{3,2,1,0:T(8,128)(2,1)}, bf16[2,8,64,128]{3,2,1,0:T(8,128)(2,1)S(1)}, u32[]{:S(2)}) copy-start(bf16[2,8,64,128]{3,2,1,0:T(8,128)(2,1)S(1)} %collective-permute-done.before_ref) | copy-start | bytes 786436
  16.1 1.7 %copy-start.6 = (bf16[2,8,64,128]{3,2,1,0:T(8,128)(2,1)}, bf16[2,8,64,128]{3,2,1,0:T(8,128)(2,1)S(1)}, u32[]{:S(2)}) copy-start(bf16[2,8,64,128]{3,2,1,0:T(8,128)(2,1)S(1)} %collective-permute-done.1.after_ref) | copy-start | bytes 786436
  17.1 0.8 %copy-start.1 = (bf16[4,8,64,128]{3,2,1,0:T(8,128)(2,1)}, bf16[4,8,64,128]{3,2,1,0:T(8,128)(2,1)S(1)}, u32[]{:S(2)}) copy-start(bf16[4,8,64,128]{3,2,1,0:T(8,128)(2,1)S(1)} %get-tuple-element.14.own_ref) | copy-start | bytes 1572868
  17.9 12.8 %collective-permute-start.2 = (bf16[8,2,64,128]{3,2,1,0:T(8,128)(2,1)}, bf16[8,2,64,128]{3,2,1,0:T(8,128)(2,1)}, u32[]{:S(2)}, u32[]{:S(2)}) collective-permute-start(bf16[8,2,64,128]{3,2,1,0:T(8,128)(2,1)} %get-tuple-element.17), channel_id=1, source_target_pairs={{1,0},{2,1},{3,2},{5,4},{6,5},{7,6},{9,8},{10,9},{11,10},{13,12},{... | collective-permute-start | bytes 786440 | tf_op jit(solution)/shard_map/ppermute | solution.py:187
  19.2 11.5 %collective-permute-start.3 = (bf16[8,2,64,128]{3,2,1,0:T(8,128)(2,1)}, bf16[8,2,64,128]{3,2,1,0:T(8,128)(2,1)}, u32[]{:S(2)}, u32[]{:S(2)}) collective-permute-start(bf16[8,2,64,128]{3,2,1,0:T(8,128)(2,1)} %get-tuple-element.18), channel_id=1, source_target_pairs={{0,1},{1,2},{2,3},{4,5},{5,6},{6,7},{8,9},{9,10},{10,11},{12,13},{... | collective-permute-start | bytes 786440 | tf_op jit(solution)/shard_map/ppermute | solution.py:187
  28.8 0.8 %copy-start.10 = (bf16[256,64]{1,0:T(8,128)(2,1)S(1)}, bf16[256,64]{1,0:T(8,128)(2,1)}, u32[]{:S(2)}) copy-start(bf16[256,64]{1,0:T(8,128)(2,1)} %copy.25.attr_ref) | copy-start | bytes 98308
  30.7 1.0 %copy-start.2 = (bf16[4,8,64,128]{3,2,1,0:T(8,128)(2,1)S(1)}, bf16[4,8,64,128]{3,2,1,0:T(8,128)(2,1)}, u32[]{:S(2)}) copy-start(bf16[4,8,64,128]{3,2,1,0:T(8,128)(2,1)} %copy-done.1) | copy-start | bytes 1572868
  31.8 0.9 %copy-start.5 = (bf16[2,8,64,128]{3,2,1,0:T(8,128)(2,1)S(1)}, bf16[2,8,64,128]{3,2,1,0:T(8,128)(2,1)}, u32[]{:S(2)}) copy-start(bf16[2,8,64,128]{3,2,1,0:T(8,128)(2,1)} %copy-done.4) | copy-start | bytes 786436
  32.7 0.9 %copy-start.7 = (bf16[2,8,64,128]{3,2,1,0:T(8,128)(2,1)S(1)}, bf16[2,8,64,128]{3,2,1,0:T(8,128)(2,1)}, u32[]{:S(2)}) copy-start(bf16[2,8,64,128]{3,2,1,0:T(8,128)(2,1)} %copy-done.6) | copy-start | bytes 786436
  33.7 0.9 %copy-start.8 = (bf16[192,576]{1,0:T(8,128)(2,1)S(1)}, bf16[192,576]{1,0:T(8,128)(2,1)}, u32[]{:S(2)}) copy-start(bf16[192,576]{1,0:T(8,128)(2,1)} %reshape.17.kernel_ref) | copy-start | bytes 663556
  42.3 3.7 %collective-permute-start.4 = (f32[4,1,1,4,40]{4,3,0,2,1:T(4,128)S(1)}, f32[4,1,1,4,40]{4,3,0,2,1:T(4,128)S(1)}, u32[]{:S(2)}, u32[]{:S(2)}) collective-permute-start(f32[4,1,1,4,40]{4,3,0,2,1:T(4,128)S(1)} %dynamic-slice_bitcast_fusion), channel_id=1, source_target_pairs={{0,2},{2,0},{1,3},{3,1},{4,6},{6,4},{5,7},{7,5},{8,10},{10,8},{9,1... | collective-permute-start | bytes 7688 | tf_op jit(solution)/shard_map/ppermute | solution.py:201
  46.0 4.6 %collective-permute-start.5 = (f32[4,2,1,2,40]{4,3,1,0,2:T(2,128)S(1)}, f32[4,2,1,2,40]{4,3,1,0,2:T(2,128)S(1)}, u32[]{:S(2)}, u32[]{:S(2)}) collective-permute-start(f32[4,2,1,2,40]{4,3,1,0,2:T(2,128)S(1)} %bitcast.53), channel_id=1, source_target_pairs={{0,8},{4,12},{8,0},{12,4},{1,9},{5,13},{9,1},{13,5},{2,10},{6,14},... | collective-permute-start | bytes 7688 | tf_op jit(solution)/shard_map/ppermute | solution.py:201
  50.7 3.7 %collective-permute-start.6 = (f32[4,2,2,1,40]{4,2,1,0,3:T(2,128)S(1)}, f32[4,2,2,1,40]{4,2,1,0,3:T(2,128)S(1)}, u32[]{:S(2)}, u32[]{:S(2)}) collective-permute-start(f32[4,2,2,1,40]{4,2,1,0,3:T(2,128)S(1)} %bitcast.54), channel_id=1, source_target_pairs={{0,4},{4,0},{8,12},{12,8},{1,5},{5,1},{9,13},{13,9},{2,6},{6,2},{1... | collective-permute-start | bytes 7688 | tf_op jit(solution)/shard_map/ppermute | solution.py:201

commit v2 on v1

--- a/solution.py
+++ b/solution.py
@@ -22,13 +22,9 @@
     return lax.broadcasted_iota(jnp.int32, shape, axis)
 
 
-def call(body, outs, scratch, name, n_smem=0, n_any=0):
+def call(body, outs, scratch, name, mib, n_smem=0):
     def run(*args):
-        spaces = (
-            [pltpu.SMEM] * n_smem
-            + [pltpu.VMEM] * (len(args) - n_smem - n_any)
-            + [pl.ANY] * n_any
-        )
+        spaces = [pltpu.SMEM] * n_smem + [pltpu.VMEM] * (len(args) - n_smem)
         return pl.pallas_call(
             body,
             out_shape=outs,
@@ -36,7 +32,7 @@
             out_specs=jax.tree.map(lambda _: pl.BlockSpec(memory_space=pltpu.VMEM), outs),
             scratch_shapes=scratch,
             name=name,
-            compiler_params=pltpu.CompilerParams(vmem_limit_bytes=48 << 20),
+            compiler_params=pltpu.CompilerParams(vmem_limit_bytes=mib << 20),
         )(*args)
 
     return run
@@ -53,7 +49,7 @@
             up_ref[x - (span_x - HALO)] = layer
 
 
-def edges_body(own_ref, before_ref, after_ref, right_ref, left_ref):
+def edges_body(own_ref, before_ref, after_ref, _, right_ref, left_ref):
     span_x, span_y = own_ref.shape[:2]
     for ref, base, span in (
         (before_ref, 0, HALO),
@@ -65,7 +61,10 @@
 
 
 def make_points_body(span_x, span_y, bricks, sects, capacity):
-    def body(flags_ref, place_ref, dest_ref, attr_ref, first_ref, pick_ref, wz_ref, wxy_ref, pre_ref):
+    def body(
+        flags_ref, place_ref, dest_ref, attr_ref, first_ref, conv_ref,
+        pick_ref, wz_ref, wxy_ref, pre_ref, kernel_ref,
+    ):
         count = place_ref.shape[1]
         span_z = wz_ref.shape[0]
         slots = pick_ref.shape[0]
@@ -92,9 +91,10 @@
             for y in range(span_y + 2):
                 row = x * (span_y + 2) + y
                 wxy_ref[row : row + 1, :] = w * weight_y[y]
-        along = jnp.broadcast_to(dest_ref[...].astype(F32), (count, count))
+        row = dest_ref[...].astype(F32)
         earlier, later = iota((count, count), 0), iota((count, count), 1)
-        row = jnp.sum(jnp.where(earlier == later, along, 0.0), axis=0, keepdims=True)
+        diagonal = jnp.where(earlier == later, jnp.broadcast_to(row, (count, count)), 0.0)
+        along = jnp.sum(diagonal, axis=1, keepdims=True)
         same = jnp.where((along == row) & (earlier < later), 1.0, 0.0)
         arrival = jnp.sum(same, axis=0, keepdims=True).astype(jnp.int32)
         target = row.astype(jnp.int32)
@@ -102,26 +102,32 @@
         slot = (sect * bricks + brick) * capacity + arrival
         pick = jnp.where(iota((slots, count), 0) == slot, 1.0, 0.0).astype(BF16)
         pick_ref[...] = pick
-        attr = jnp.dot(pick, attr_ref[...], preferred_element_type=F32).astype(BF16)
+        attr = lax.dot_general(
+            pick, attr_ref[...], (((1,), (1,)), ((), ())), preferred_element_type=F32
+        ).astype(BF16)
         channels = first_ref.shape[1] - attr.shape[1]
         for s in range(2):
             pre_ref[s * half : (s + 1) * half] = jnp.dot(
                 attr[s * half : (s + 1) * half], first_ref[s, channels:], preferred_element_type=F32
             )
+        for a in range(3):
+            for b in range(3):
+                for e in range(3):
+                    tile = conv_ref[a, b, e].astype(F32).T.astype(BF16)
+                    lanes = (a * 3 + e) * channels
+                    kernel_ref[b * channels : (b + 1) * channels, lanes : lanes + channels] = tile
 
     return body
 
 
 def main_body(
     own_ref, before_ref, after_ref, right_ref, left_ref, kernel_ref,
-    pick_ref, wz_ref, wxy_ref, pre_ref, first_ref, last_ref, middle_hbm,
-    value_ref, shifted, latent, middle_ref, sem,
+    pick_ref, wz_ref, wxy_ref, pre_ref, first_ref, last_ref, middle_ref,
+    value_ref, shifted, latent,
 ):
     span_x, span_y, channels, span_z = own_ref.shape
     wide_x, wide_y = span_x + 2 * HALO, span_y + 2 * HALO
     out_x, out_y = span_x + 2, span_y + 2
-    fetch = pltpu.make_async_copy(middle_hbm, middle_ref, sem)
-    fetch.start()
     lane = iota((channels, span_z), 1)
 
     def column(x, y):
@@ -166,7 +172,6 @@
     feature = lax.dot_general(
         pick_ref[...], total.astype(BF16), (((1,), (1,)), ((), ())), preferred_element_type=F32
     ).astype(BF16)
-    fetch.wait()
     half = feature.shape[0] // 2
     for s in range(2):
         span = slice(s * half, (s + 1) * half)
@@ -229,7 +234,6 @@
     flags = jnp.stack(
         [brick > 0, brick < bricks - 1, line > 0, line < lax.axis_size(lines) - 1]
     ).astype(jnp.int32)
-    kernel = conv_kernels[0].transpose(1, 4, 0, 2, 3).reshape(3 * channels, 9 * channels)
 
     def block(*shape):
         return jax.ShapeDtypeStruct(shape, BF16)
@@ -243,26 +247,29 @@
         ],
         [],
         "columns",
+        8,
     )(geometry)
     before = shift(up, "brick", 1)
     after = shift(down, "brick", -1)
-    to_right, to_left = call(
-        edges_body, [block(span_x + 2 * HALO, HALO, channels, span_z)] * 2, [], "edges"
-    )(own, before, after)
-    left = shift(to_right, lines, 1)
-    right = shift(to_left, lines, -1)
-    pick, wz, wxy, pre = call(
+    pick, wz, wxy, pre, kernel = call(
         make_points_body(span_x, span_y, bricks, sects, capacity),
         [
             block(slots, count),
             block(span_z, count),
             jax.ShapeDtypeStruct(((span_x + 2) * (span_y + 2), count), F32),
             jax.ShapeDtypeStruct((slots, hidden), F32),
+            block(3 * channels, 9 * channels),
         ],
         [],
         "points",
+        12,
         n_smem=1,
-    )(flags, point_place, destination, point_attr, dense_first)
+    )(flags, point_place, destination.reshape(1, count), point_attr.T, dense_first, conv_kernels[0])
+    to_right, to_left = call(
+        edges_body, [block(span_x + 2 * HALO, HALO, channels, span_z)] * 2, [], "edges", 8
+    )(own, before, after, wxy)
+    left = shift(to_right, lines, 1)
+    right = shift(to_left, lines, -1)
     wide = (span_x + 2 * HALO) * 3 * channels
     value = call(
         main_body,
@@ -270,11 +277,9 @@
         [
             pltpu.VMEM((wide, (span_y + 2 * HALO) * span_z), BF16),
             pltpu.VMEM(((span_y + 2) * channels, span_z), BF16),
-            pltpu.VMEM(dense_middle.shape, BF16),
-            pltpu.SemaphoreType.DMA,
         ],
         "main",
-        n_any=1,
+        28,
     )(own, before, after, right, left, kernel, pick, wz, wxy, pre, dense_first, dense_last, dense_middle)
     value = value.transpose(1, 0, 2).reshape(outputs, sects, bricks, capacity)
     value = swap_blocks(value, "sect", 1)

time: 55.7 us -> 48.3 us (0.87)
  waiting for transfers between devices: 14.5 us -> 9.88 us
  local copies, waits for them, and re-layouts: 13.2 us -> 9.47 us
  starting transfers between devices: 17.3 us -> 20.5 us
  Pallas kernels: 9.85 us -> 7.58 us
    ppermute x4, waiting for transfers between devices: 8.36 us -> 4.18 us  [shift(): return lax.ppermute(array, axes, pairs)]
    ppermute x3, starting transfers between devices: 5.83 us -> 9.94 us  [swap_blocks(): got = lax.ppermute(sent, axis, [(i, i ^ step) for i in range(size)])]
    pallas_call x4, Pallas kernels: 9.85 us -> 7.58 us  [run(): pl.pallas_call(body, out_shape=outs, in_specs=[pl.BlockSpec(memory_space=...]
    reshape x1 -> x0, local copies, waits for them, and re-layouts: 2.08 us -> none  [on_device(): conv_kernels[0].transpose(1, 4, 0, 2, 3).reshape(3 * channels, 9 * channels)]
    transpose x1 -> x0, local copies, waits for them, and re-layouts: 2.04 us -> none  [on_device(): conv_kernels[0].transpose(1, 4, 0, 2, 3).reshape(3 * channels, 9 * channels)]
    ppermute x4, starting transfers between devices: 11.4 us -> 10.6 us  [shift(): return lax.ppermute(array, axes, pairs)]
    unnamed x30 -> x18, local copies, waits for them, and re-layouts: 8.26 us -> 8.66 us
  transfers between devices with their start and end apart: 7 -> 7, of which waited for: 5 -> 5; matrix products, arithmetic and copies ran while one was open for 11% -> 0% of each run, Pallas kernels for 2% -> 2%
where the time goes in v2:
time: 48.3 us; the launch traced here: 47.8 us
  starting transfers between devices  20.5 us (42%)
  waiting for transfers between devices  9.88 us (20%)
  local copies, waits for them, and re-layouts  9.47 us (20%)
  Pallas kernels  7.58 us (16%)
    ppermute x4, starting transfers between devices, shift(): return lax.ppermute(array, axes, pairs)  10.6 us
    ppermute x3, starting transfers between devices, swap_blocks(): got = lax.ppermute(sent, axis, [(i, i ^ step) for i in range(size)])  9.94 us
    unnamed x18, local copies, waits for them, and re-layouts  8.66 us
    pallas_call x4, Pallas kernels, run(): pl.pallas_call(body, out_shape=outs, in_specs=[pl.BlockSpec(memory_space=...  7.58 us
    ppermute x3, waiting for transfers between devices, swap_blocks(): got = lax.ppermute(sent, axis, [(i, i ^ step) for i in range(size)])  5.7 us
    ppermute x4, waiting for transfers between devices, shift(): return lax.ppermute(array, axes, pairs)  4.18 us
  transfers between devices with their start and end apart: 7, of which 5 were waited for; matrix products, arithmetic and copies ran while one was open for 0% of the time, Pallas kernels for 2%

profile of v2, /device:TPU:0, one launch (start us, length us, event | category | flops | bytes accessed | tf_op | source)
XLA Modules:
  0.0 47.8 jit_solution(3461066456383765035)
XLA Ops:
  0.0 1.0 %copy-done.3 = bf16[64,4,8,128]{3,2,1,0:T(8,128)(2,1)S(1)} copy-done((bf16[64,4,8,128]{3,2,1,0:T(8,128)(2,1)S(1)}, bf16[64,4,8,128]{3,2,1,0:T(8,128)(2,1)}, u32[]{:S(2)}) %copy-start.3) | copy-done | bytes 524312
  1.3 5.0 %collective-permute-start = (bf16[2,8,64,128]{3,2,1,0:T(8,128)(2,1)S(1)}, bf16[2,8,64,128]{3,2,1,0:T(8,128)(2,1)S(1)}, u32[]{:S(2)}, u32[]{:S(2)}) collective-permute-start(bf16[2,8,64,128]{3,2,1,0:T(8,128)(2,1)S(1)} %get-tuple-element.16), channel_id=1, source_target_pairs={{0,4},{4,8},{8,12},{1,5},{5,9},{9,13},{2,6},{6,10},{10,14},{3,7},{... | collective-permute-start | bytes 786440 | tf_op jit(solution)/shard_map/ppermute | solution.py:192
  6.3 1.3 %collective-permute-start.1 = (bf16[2,8,64,128]{3,2,1,0:T(8,128)(2,1)S(1)}, bf16[2,8,64,128]{3,2,1,0:T(8,128)(2,1)S(1)}, u32[]{:S(2)}, u32[]{:S(2)}) collective-permute-start(bf16[2,8,64,128]{3,2,1,0:T(8,128)(2,1)S(1)} %get-tuple-element.17), channel_id=1, source_target_pairs={{4,0},{8,4},{12,8},{5,1},{9,5},{13,9},{6,2},{10,6},{14,10},{7,3},{... | collective-permute-start | bytes 786440 | tf_op jit(solution)/shard_map/ppermute | solution.py:192
  7.7 0.9 %copy-done.1 = bf16[2,128,512]{2,1,0:T(8,128)(2,1)S(1)} copy-done((bf16[2,128,512]{2,1,0:T(8,128)(2,1)S(1)}, bf16[2,128,512]{2,1,0:T(8,128)(2,1)}, u32[]{:S(2)}) %copy-start.1) | copy-done | bytes 262168
  8.6 1.0 %copy-done.4 = bf16[1,3,3,3,64,64]{5,4,3,2,1,0:T(8,128)(2,1)S(1)} copy-done((bf16[1,3,3,3,64,64]{5,4,3,2,1,0:T(8,128)(2,1)S(1)}, bf16[1,3,3,3,64,64]{5,4,3,2,1,0:T(8,128)(2,1)}, u32[]{:S(2)}) %copy-start.4) | copy-done | bytes 221208
  9.7 0.8 %copy-done.5 = bf16[256,64]{0,1:T(8,128)(2,1)S(1)} copy-done((bf16[256,64]{0,1:T(8,128)(2,1)S(1)}, bf16[256,64]{0,1:T(8,128)(2,1)}, u32[]{:S(2)}) %copy-start.5) | copy-done | bytes 32792
  10.4 0.7 %copy-done.7 = f32[3,256]{1,0:T(4,128)S(1)} copy-done((f32[3,256]{1,0:T(4,128)S(1)}, f32[3,256]{1,0:T(4,128)}, u32[]{:S(2)}) %copy-start.7) | copy-done | bytes 3096
  11.1 0.7 %copy-done.8 = s32[256,1]{0,1:T(1,128)S(1)} copy-done((s32[256,1]{0,1:T(1,128)S(1)}, s32[256,1]{0,1:T(1,128)}, u32[]{:S(2)}) %copy-start.8) | copy-done | bytes 1048
  11.8 1.1 %points.1 = (bf16[320,256]{1,0:T(8,128)(2,1)S(1)}, bf16[128,256]{1,0:T(8,128)(2,1)S(1)}, f32[60,256]{1,0:T(8,128)S(1)}, f32[320,512]{1,0:T(8,128)S(1)}, bf16[192,576]{1,0:T(8,128)(2,1)S(1)}) custom-call(s32[4]{0:T(128)S(1)} %add_convert_fusion.flags_ref, f32[3,256]{1,0:T(4,128)S(1)} %copy-done.7, s32[1,256]{1,0:T(1,128)S(1)} %bitcast.51, ...), custom_call_target="tpu_custom_call" | custom-call | tf_op jit(solution)/shard_map/points/pallas_call | solution.py:28
  12.9 3.1 %collective-permute-done.1.after_ref = bf16[2,8,64,128]{3,2,1,0:T(8,128)(2,1)S(1)} collective-permute-done((bf16[2,8,64,128]{3,2,1,0:T(8,128)(2,1)S(1)}, bf16[2,8,64,128]{3,2,1,0:T(8,128)(2,1)S(1)}, u32[]{:S(2)}, u32[]{:S(2)}) %collective-permute-start.1) | collective-permute-done | bytes 262176 | tf_op jit(solution)/shard_map/ppermute | solution.py:192
  16.0 1.3 %collective-permute-start.2 = (bf16[8,2,64,128]{3,2,1,0:T(8,128)(2,1)S(1)}, bf16[8,2,64,128]{3,2,1,0:T(8,128)(2,1)S(1)}, u32[]{:S(2)}, u32[]{:S(2)}) collective-permute-start(bf16[8,2,64,128]{3,2,1,0:T(8,128)(2,1)S(1)} %get-tuple-element.19), channel_id=1, source_target_pairs={{1,0},{2,1},{3,2},{5,4},{6,5},{7,6},{9,8},{10,9},{11,10},{13,12},{... | collective-permute-start | bytes 786440 | tf_op jit(solution)/shard_map/ppermute | solution.py:192
  17.3 3.0 %collective-permute-start.3 = (bf16[8,2,64,128]{3,2,1,0:T(8,128)(2,1)S(1)}, bf16[8,2,64,128]{3,2,1,0:T(8,128)(2,1)S(1)}, u32[]{:S(2)}, u32[]{:S(2)}) collective-permute-start(bf16[8,2,64,128]{3,2,1,0:T(8,128)(2,1)S(1)} %get-tuple-element.20), channel_id=1, source_target_pairs={{0,1},{1,2},{2,3},{4,5},{5,6},{6,7},{8,9},{9,10},{10,11},{12,13},{... | collective-permute-start | bytes 786440 | tf_op jit(solution)/shard_map/ppermute | solution.py:192
  20.4 1.1 %collective-permute-done.3.left_ref = bf16[8,2,64,128]{3,2,1,0:T(8,128)(2,1)S(1)} collective-permute-done((bf16[8,2,64,128]{3,2,1,0:T(8,128)(2,1)S(1)}, bf16[8,2,64,128]{3,2,1,0:T(8,128)(2,1)S(1)}, u32[]{:S(2)}, u32[]{:S(2)}) %collective-permute-start.3) | collective-permute-done | bytes 262176 | tf_op jit(solution)/shard_map/ppermute | solution.py:192
  21.5 1.9 %copy-done = bf16[2,3,512,512]{3,2,1,0:T(8,128)(2,1)S(1)} copy-done((bf16[2,3,512,512]{3,2,1,0:T(8,128)(2,1)S(1)}, bf16[2,3,512,512]{3,2,1,0:T(8,128)(2,1)}, u32[]{:S(2)}) %copy-start) | copy-done | bytes 3145752
  23.4 0.9 %copy-done.2 = bf16[2,128,512]{2,1,0:T(8,128)(2,1)S(1)} copy-done((bf16[2,128,512]{2,1,0:T(8,128)(2,1)S(1)}, bf16[2,128,512]{2,1,0:T(8,128)(2,1)}, u32[]{:S(2)}) %copy-start.2) | copy-done | bytes 262168
  24.3 0.7 %copy-done.6 = bf16[2,4,512]{2,1,0:T(4,128)(2,1)S(1)} copy-done((bf16[2,4,512]{2,1,0:T(4,128)(2,1)S(1)}, bf16[2,4,512]{2,1,0:T(4,128)(2,1)}, u32[]{:S(2)}) %copy-start.6) | copy-done | bytes 8216
  25.0 6.2 %main.1 = f32[2,4,160]{2,1,0:T(4,128)S(1)} custom-call(bf16[4,8,64,128]{3,2,1,0:T(8,128)(2,1)S(1)} %get-tuple-element.15.own_ref, bf16[2,8,64,128]{3,2,1,0:T(8,128)(2,1)S(1)} %collective-permute-done.before_ref, bf16[2,8,64,128]{3,2,1,0:T(8,128)(2,1)S(1)} %collective-permute-done.1.after_ref, bf16[8,2,64,128]{3,2,1,0:T(8,128)(2,1)S(1)} %collective-permute-done.2.right_ref, ...), custom_call_target="tpu_custom_call" | custom-call | tf_op jit(solution)/shard_map/main/pallas_call | solution.py:28
  31.3 5.7 %collective-permute-start.4 = (f32[4,1,1,4,40]{4,3,0,2,1:T(4,128)S(1)}, f32[4,1,1,4,40]{4,3,0,2,1:T(4,128)S(1)}, u32[]{:S(2)}, u32[]{:S(2)}) collective-permute-start(f32[4,1,1,4,40]{4,3,0,2,1:T(4,128)S(1)} %dynamic-slice_bitcast_fusion), channel_id=1, source_target_pairs={{0,2},{2,0},{1,3},{3,1},{4,6},{6,4},{5,7},{7,5},{8,10},{10,8},{9,1... | collective-permute-start | bytes 7688 | tf_op jit(solution)/shard_map/ppermute | solution.py:206
  37.0 1.6 %collective-permute-done.4 = f32[4,1,1,4,40]{4,3,0,2,1:T(4,128)S(1)} collective-permute-done((f32[4,1,1,4,40]{4,3,0,2,1:T(4,128)S(1)}, f32[4,1,1,4,40]{4,3,0,2,1:T(4,128)S(1)}, u32[]{:S(2)}, u32[]{:S(2)}) %collective-permute-start.4) | collective-permute-done | bytes 2592 | tf_op jit(solution)/shard_map/ppermute | solution.py:206
  38.6 2.6 %collective-permute-start.5 = (f32[4,2,1,2,40]{4,3,1,0,2:T(2,128)S(1)}, f32[4,2,1,2,40]{4,3,1,0,2:T(2,128)S(1)}, u32[]{:S(2)}, u32[]{:S(2)}) collective-permute-start(f32[4,2,1,2,40]{4,3,1,0,2:T(2,128)S(1)} %bitcast.55), channel_id=1, source_target_pairs={{0,8},{4,12},{8,0},{12,4},{1,9},{5,13},{9,1},{13,5},{2,10},{6,14},... | collective-permute-start | bytes 7688 | tf_op jit(solution)/shard_map/ppermute | solution.py:206
  41.3 2.0 %collective-permute-done.5 = f32[4,2,1,2,40]{4,3,1,0,2:T(2,128)S(1)} collective-permute-done((f32[4,2,1,2,40]{4,3,1,0,2:T(2,128)S(1)}, f32[4,2,1,2,40]{4,3,1,0,2:T(2,128)S(1)}, u32[]{:S(2)}, u32[]{:S(2)}) %collective-permute-start.5) | collective-permute-done | bytes 2592 | tf_op jit(solution)/shard_map/ppermute | solution.py:206
  43.3 1.6 %collective-permute-start.6 = (f32[4,2,2,1,40]{4,2,1,0,3:T(2,128)S(1)}, f32[4,2,2,1,40]{4,2,1,0,3:T(2,128)S(1)}, u32[]{:S(2)}, u32[]{:S(2)}) collective-permute-start(f32[4,2,2,1,40]{4,2,1,0,3:T(2,128)S(1)} %bitcast.56), channel_id=1, source_target_pairs={{0,4},{4,0},{8,12},{12,8},{1,5},{5,1},{9,13},{13,9},{2,6},{6,2},{1... | collective-permute-start | bytes 7688 | tf_op jit(solution)/shard_map/ppermute | solution.py:206
  45.0 2.1 %collective-permute-done.6 = f32[4,2,2,1,40]{4,2,1,0,3:T(2,128)S(1)} collective-permute-done((f32[4,2,2,1,40]{4,2,1,0,3:T(2,128)S(1)}, f32[4,2,2,1,40]{4,2,1,0,3:T(2,128)S(1)}, u32[]{:S(2)}, u32[]{:S(2)}) %collective-permute-start.6) | collective-permute-done | bytes 2592 | tf_op jit(solution)/shard_map/ppermute | solution.py:206
  47.1 0.7 %reshape.19 = f32[4,320]{1,0:T(4,128)} reshape(f32[4,4,2,40]{3,2,1,0:T(2,128)S(1)} %copy.19) | data formatting | bytes 10240 | tf_op jit(solution)/shard_map/reshape | solution.py:287
  (26 shorter events, 0.6 us)
Async XLA Ops:
  0.0 1.0 %copy-start.3 = (bf16[64,4,8,128]{3,2,1,0:T(8,128)(2,1)S(1)}, bf16[64,4,8,128]{3,2,1,0:T(8,128)(2,1)}, u32[]{:S(2)}) copy-start(bf16[64,4,8,128]{3,2,1,0:T(8,128)(2,1)} %g_ref.1) | copy-start | bytes 1572868
  1.3 11.6 %collective-permute-start = (bf16[2,8,64,128]{3,2,1,0:T(8,128)(2,1)S(1)}, bf16[2,8,64,128]{3,2,1,0:T(8,128)(2,1)S(1)}, u32[]{:S(2)}, u32[]{:S(2)}) collective-permute-start(bf16[2,8,64,128]{3,2,1,0:T(8,128)(2,1)S(1)} %get-tuple-element.16), channel_id=1, source_target_pairs={{0,4},{4,8},{8,12},{1,5},{5,9},{9,13},{2,6},{6,10},{10,14},{3,7},{... | collective-permute-start | bytes 786440 | tf_op jit(solution)/shard_map/ppermute | solution.py:192
  6.3 9.7 %collective-permute-start.1 = (bf16[2,8,64,128]{3,2,1,0:T(8,128)(2,1)S(1)}, bf16[2,8,64,128]{3,2,1,0:T(8,128)(2,1)S(1)}, u32[]{:S(2)}, u32[]{:S(2)}) collective-permute-start(bf16[2,8,64,128]{3,2,1,0:T(8,128)(2,1)S(1)} %get-tuple-element.17), channel_id=1, source_target_pairs={{4,0},{8,4},{12,8},{5,1},{9,5},{13,9},{6,2},{10,6},{14,10},{7,3},{... | collective-permute-start | bytes 786440 | tf_op jit(solution)/shard_map/ppermute | solution.py:192
  7.7 1.0 %copy-start.1 = (bf16[2,128,512]{2,1,0:T(8,128)(2,1)S(1)}, bf16[2,128,512]{2,1,0:T(8,128)(2,1)}, u32[]{:S(2)}) copy-start(bf16[2,128,512]{2,1,0:T(8,128)(2,1)} %first_ref.3) | copy-start | bytes 786436
  8.6 1.0 %copy-start.4 = (bf16[1,3,3,3,64,64]{5,4,3,2,1,0:T(8,128)(2,1)S(1)}, bf16[1,3,3,3,64,64]{5,4,3,2,1,0:T(8,128)(2,1)}, u32[]{:S(2)}) copy-start(bf16[1,3,3,3,64,64]{5,4,3,2,1,0:T(8,128)(2,1)} %param.9) | copy-start | bytes 663556
  9.6 0.8 %copy-start.5 = (bf16[256,64]{0,1:T(8,128)(2,1)S(1)}, bf16[256,64]{0,1:T(8,128)(2,1)}, u32[]{:S(2)}) copy-start(bf16[256,64]{0,1:T(8,128)(2,1)} %param.11) | copy-start | bytes 98308
  10.4 0.7 %copy-start.7 = (f32[3,256]{1,0:T(4,128)S(1)}, f32[3,256]{1,0:T(4,128)}, u32[]{:S(2)}) copy-start(f32[3,256]{1,0:T(4,128)} %place_ref.1) | copy-start | bytes 9220
  11.1 0.7 %copy-start.8 = (s32[256,1]{0,1:T(1,128)S(1)}, s32[256,1]{0,1:T(1,128)}, u32[]{:S(2)}) copy-start(s32[256,1]{0,1:T(1,128)} %param.12) | copy-start | bytes 3076
  16.0 4.4 %collective-permute-start.2 = (bf16[8,2,64,128]{3,2,1,0:T(8,128)(2,1)S(1)}, bf16[8,2,64,128]{3,2,1,0:T(8,128)(2,1)S(1)}, u32[]{:S(2)}, u32[]{:S(2)}) collective-permute-start(bf16[8,2,64,128]{3,2,1,0:T(8,128)(2,1)S(1)} %get-tuple-element.19), channel_id=1, source_target_pairs={{1,0},{2,1},{3,2},{5,4},{6,5},{7,6},{9,8},{10,9},{11,10},{13,12},{... | collective-permute-start | bytes 786440 | tf_op jit(solution)/shard_map/ppermute | solution.py:192
  17.3 4.2 %collective-permute-start.3 = (bf16[8,2,64,128]{3,2,1,0:T(8,128)(2,1)S(1)}, bf16[8,2,64,128]{3,2,1,0:T(8,128)(2,1)S(1)}, u32[]{:S(2)}, u32[]{:S(2)}) collective-permute-start(bf16[8,2,64,128]{3,2,1,0:T(8,128)(2,1)S(1)} %get-tuple-element.20), channel_id=1, source_target_pairs={{0,1},{1,2},{2,3},{4,5},{5,6},{6,7},{8,9},{9,10},{10,11},{12,13},{... | collective-permute-start | bytes 786440 | tf_op jit(solution)/shard_map/ppermute | solution.py:192
  21.5 1.9 %copy-start = (bf16[2,3,512,512]{3,2,1,0:T(8,128)(2,1)S(1)}, bf16[2,3,512,512]{3,2,1,0:T(8,128)(2,1)}, u32[]{:S(2)}) copy-start(bf16[2,3,512,512]{3,2,1,0:T(8,128)(2,1)} %middle_ref.1) | copy-start | bytes 9437188
  23.4 0.9 %copy-start.2 = (bf16[2,128,512]{2,1,0:T(8,128)(2,1)S(1)}, bf16[2,128,512]{2,1,0:T(8,128)(2,1)}, u32[]{:S(2)}) copy-start(bf16[2,128,512]{2,1,0:T(8,128)(2,1)} %first_ref.3) | copy-start | bytes 786436
  24.3 0.7 %copy-start.6 = (bf16[2,4,512]{2,1,0:T(4,128)(2,1)S(1)}, bf16[2,4,512]{2,1,0:T(4,128)(2,1)}, u32[]{:S(2)}) copy-start(bf16[2,4,512]{2,1,0:T(4,128)(2,1)} %last_ref.1) | copy-start | bytes 24580
  31.3 7.3 %collective-permute-start.4 = (f32[4,1,1,4,40]{4,3,0,2,1:T(4,128)S(1)}, f32[4,1,1,4,40]{4,3,0,2,1:T(4,128)S(1)}, u32[]{:S(2)}, u32[]{:S(2)}) collective-permute-start(f32[4,1,1,4,40]{4,3,0,2,1:T(4,128)S(1)} %dynamic-slice_bitcast_fusion), channel_id=1, source_target_pairs={{0,2},{2,0},{1,3},{3,1},{4,6},{6,4},{5,7},{7,5},{8,10},{10,8},{9,1... | collective-permute-start | bytes 7688 | tf_op jit(solution)/shard_map/ppermute | solution.py:206
  38.6 4.6 %collective-permute-start.5 = (f32[4,2,1,2,40]{4,3,1,0,2:T(2,128)S(1)}, f32[4,2,1,2,40]{4,3,1,0,2:T(2,128)S(1)}, u32[]{:S(2)}, u32[]{:S(2)}) collective-permute-start(f32[4,2,1,2,40]{4,3,1,0,2:T(2,128)S(1)} %bitcast.55), channel_id=1, source_target_pairs={{0,8},{4,12},{8,0},{12,4},{1,9},{5,13},{9,1},{13,5},{2,10},{6,14},... | collective-permute-start | bytes 7688 | tf_op jit(solution)/shard_map/ppermute | solution.py:206
  43.3 3.7 %collective-permute-start.6 = (f32[4,2,2,1,40]{4,2,1,0,3:T(2,128)S(1)}, f32[4,2,2,1,40]{4,2,1,0,3:T(2,128)S(1)}, u32[]{:S(2)}, u32[]{:S(2)}) collective-permute-start(f32[4,2,2,1,40]{4,2,1,0,3:T(2,128)S(1)} %bitcast.56), channel_id=1, source_target_pairs={{0,4},{4,0},{8,12},{12,8},{1,5},{5,1},{9,13},{13,9},{2,6},{6,2},{1... | collective-permute-start | bytes 7688 | tf_op jit(solution)/shard_map/ppermute | solution.py:206

commit v3 on v2

--- a/solution.py
+++ b/solution.py
@@ -22,9 +22,10 @@
     return lax.broadcasted_iota(jnp.int32, shape, axis)
 
 
-def call(body, outs, scratch, name, mib, n_smem=0):
+def call(body, outs, scratch, name, mib, n_hbm=0):
     def run(*args):
-        spaces = [pltpu.SMEM] * n_smem + [pltpu.VMEM] * (len(args) - n_smem)
+        spaces = [pltpu.VMEM] * (len(args) - n_hbm) + [pltpu.HBM] * n_hbm
+        args = [pltpu.with_memory_space_constraint(a, s) if s == pltpu.HBM else a for a, s in zip(args, spaces)]
         return pl.pallas_call(
             body,
             out_shape=outs,
@@ -49,25 +50,32 @@
             up_ref[x - (span_x - HALO)] = layer
 
 
-def edges_body(own_ref, before_ref, after_ref, _, right_ref, left_ref):
+def edges_body(own_ref, before_ref, after_ref, _, partner_ref, cross_ref):
     span_x, span_y = own_ref.shape[:2]
-    for ref, base, span in (
-        (before_ref, 0, HALO),
-        (own_ref, HALO, span_x),
-        (after_ref, HALO + span_x, HALO),
-    ):
-        right_ref[base : base + span] = ref[:, span_y - HALO :]
-        left_ref[base : base + span] = ref[:, :HALO]
+    facing = ((partner_ref, cross_ref), (cross_ref, partner_ref))
+    for slab, (right_ref, left_ref) in enumerate(facing):
+
+        @pl.when(lax.axis_index("slab") == slab)
+        def _(right_ref=right_ref, left_ref=left_ref):
+            for ref, base, span in (
+                (before_ref, 0, HALO),
+                (own_ref, HALO, span_x),
+                (after_ref, HALO + span_x, HALO),
+            ):
+                right_ref[base : base + span] = ref[:, span_y - HALO :]
+                left_ref[base : base + span] = ref[:, :HALO]
 
 
 def make_points_body(span_x, span_y, bricks, sects, capacity):
     def body(
-        flags_ref, place_ref, dest_ref, attr_ref, first_ref, conv_ref,
+        place_ref, dest_ref, attr_ref, first_ref, conv_ref,
         pick_ref, wz_ref, wxy_ref, pre_ref, kernel_ref,
     ):
         count = place_ref.shape[1]
         span_z = wz_ref.shape[0]
         slots = pick_ref.shape[0]
+        brick, line = lax.axis_index("brick"), lax.axis_index(("sect", "slab"))
+        last_brick, last_line = lax.axis_size("brick") - 1, lax.axis_size(("sect", "slab")) - 1
         half = slots // 2
         local_x = place_ref[0:1, :] * span_x
         local_y = place_ref[1:2, :] * span_y
@@ -78,16 +86,16 @@
         for y in range(span_y + 2):
             w = hat(local_y - (y - 0.5))
             if y == 0:
-                w = w * flags_ref[2].astype(F32)
+                w = jnp.where(line > 0, w, 0.0)
             if y == span_y + 1:
-                w = w * flags_ref[3].astype(F32)
+                w = jnp.where(line < last_line, w, 0.0)
             weight_y.append(w)
         for x in range(span_x + 2):
             w = hat(local_x - (x - 0.5))
             if x == 0:
-                w = w * flags_ref[0].astype(F32)
+                w = jnp.where(brick > 0, w, 0.0)
             if x == span_x + 1:
-                w = w * flags_ref[1].astype(F32)
+                w = jnp.where(brick < last_brick, w, 0.0)
             for y in range(span_y + 2):
                 row = x * (span_y + 2) + y
                 wxy_ref[row : row + 1, :] = w * weight_y[y]
@@ -98,8 +106,7 @@
         same = jnp.where((along == row) & (earlier < later), 1.0, 0.0)
         arrival = jnp.sum(same, axis=0, keepdims=True).astype(jnp.int32)
         target = row.astype(jnp.int32)
-        brick, sect = target // sects, target % sects
-        slot = (sect * bricks + brick) * capacity + arrival
+        slot = ((target % sects) * bricks + target // sects) * capacity + arrival
         pick = jnp.where(iota((slots, count), 0) == slot, 1.0, 0.0).astype(BF16)
         pick_ref[...] = pick
         attr = lax.dot_general(
@@ -120,58 +127,117 @@
     return body
 
 
-def main_body(
-    own_ref, before_ref, after_ref, right_ref, left_ref, kernel_ref,
-    pick_ref, wz_ref, wxy_ref, pre_ref, first_ref, last_ref, middle_ref,
-    value_ref, shifted, latent,
+def shifted_tiles(tile):
+    span_z = tile.shape[1]
+    lane = iota(tile.shape, 1)
+    wide = tile.astype(F32)
+    lower = jnp.where(lane == 0, 0.0, pltpu.roll(wide, 1, 1)).astype(BF16)
+    upper = jnp.where(lane == span_z - 1, 0.0, pltpu.roll(wide, span_z - 1, 1)).astype(BF16)
+    return lower, tile, upper
+
+
+def latent_tile(part, centre, y):
+    channels, span_z = centre.shape
+    response = sum(
+        part[b * channels : (b + 1) * channels, (y + b) * span_z : (y + b + 1) * span_z]
+        for b in range(3)
+    )
+    return (centre.astype(F32) + gelu(response)).astype(BF16)
+
+
+def layer_of(own_ref, before_ref, after_ref, x):
+    span_x = own_ref.shape[0]
+    if x < HALO:
+        return before_ref, x
+    if x >= HALO + span_x:
+        return after_ref, x - HALO - span_x
+    return own_ref, x - HALO
+
+
+def inner_body(
+    own_ref, before_ref, after_ref, kernel_ref, wz_ref, wxy_ref, total_ref, shifted, latent
 ):
     span_x, span_y, channels, span_z = own_ref.shape
-    wide_x, wide_y = span_x + 2 * HALO, span_y + 2 * HALO
-    out_x, out_y = span_x + 2, span_y + 2
-    lane = iota((channels, span_z), 1)
-
-    def column(x, y):
-        if y < HALO:
-            return left_ref[x, y]
-        if y >= HALO + span_y:
-            return right_ref[x, y - HALO - span_y]
-        if x < HALO:
-            return before_ref[x, y - HALO]
-        if x >= HALO + span_x:
-            return after_ref[x - HALO - span_x, y - HALO]
-        return own_ref[x - HALO, y - HALO]
 
     def put(x):
-        for y in range(wide_y):
-            tile = column(x, y)
-            wide = tile.astype(F32)
-            lower = jnp.where(lane == 0, 0.0, pltpu.roll(wide, 1, 1)).astype(BF16)
-            upper = jnp.where(lane == span_z - 1, 0.0, pltpu.roll(wide, span_z - 1, 1)).astype(BF16)
-            for e, piece in enumerate((lower, tile, upper)):
+        ref, at = layer_of(own_ref, before_ref, after_ref, x)
+        for y in range(span_y):
+            for e, piece in enumerate(shifted_tiles(ref[at, y])):
                 base = (x * 3 + e) * channels
                 shifted[base : base + channels, y * span_z : (y + 1) * span_z] = piece
 
     put(0)
     put(1)
-    total = jnp.zeros((channels, wz_ref.shape[1]), F32)
-    for x in range(out_x):
+    total = jnp.zeros(total_ref.shape, F32)
+    for x in range(span_x + 2):
         put(x + 2)
         rows = shifted[x * 3 * channels : (x + 3) * 3 * channels, :]
         part = jnp.dot(kernel_ref[...], rows, preferred_element_type=F32)
-        for y in range(out_y):
-            response = sum(
-                part[b * channels : (b + 1) * channels, (y + b) * span_z : (y + b + 1) * span_z]
-                for b in range(3)
-            )
-            centre = column(x + 1, y + 1).astype(F32)
-            latent[y * channels : (y + 1) * channels, :] = (centre + gelu(response)).astype(BF16)
+        ref, at = layer_of(own_ref, before_ref, after_ref, x + 1)
+        for y in range(span_y - 2):
+            latent[y * channels : (y + 1) * channels, :] = latent_tile(part, ref[at, y + 1], y)
         sampled = jnp.dot(latent[...], wz_ref[...], preferred_element_type=F32)
-        for y in range(out_y):
-            row = x * out_y + y
+        for y in range(span_y - 2):
+            row = x * (span_y + 2) + y + 2
             total += sampled[y * channels : (y + 1) * channels] * wxy_ref[row : row + 1, :]
+    total_ref[...] = total
+
+
+def outer_body(
+    own_ref, before_ref, after_ref, partner_ref, cross_ref, kernel_ref, total_ref,
+    pick_ref, wz_ref, wxy_ref, pre_ref, last_ref, first_hbm, middle_hbm,
+    value_ref, shifted, latent, first_ref, middle_ref, sems,
+):
+    span_x, span_y, channels, span_z = own_ref.shape
+    copies = [
+        pltpu.make_async_copy(first_hbm, first_ref, sems.at[0]),
+        pltpu.make_async_copy(middle_hbm, middle_ref, sems.at[1]),
+    ]
+    for copy in copies:
+        copy.start()
+    slab = lax.axis_index("slab")
+    group = 3 * channels
+
+    def put(x):
+        base = x * group
+        ref, at = layer_of(own_ref, before_ref, after_ref, x)
+        for side in range(2):
+            for j in range(2):
+                tile = ref[at, j if side == 0 else span_y - HALO + j]
+                for e, piece in enumerate(shifted_tiles(tile)):
+                    rows = slice(base + e * channels, base + (e + 1) * channels)
+                    shifted[side, j + (HALO if side == 0 else 0), rows, :] = piece
+        for ref, side in ((cross_ref, slab), (partner_ref, 1 - slab)):
+            for j in range(2):
+                for e, piece in enumerate(shifted_tiles(ref[x, j])):
+                    rows = slice(base + e * channels, base + (e + 1) * channels)
+                    shifted[side, j + HALO * side, rows, :] = piece
+
+    put(0)
+    put(1)
+    total = total_ref[...]
+    for x in range(span_x + 2):
+        put(x + 2)
+        rows = slice(x * group, (x + 3) * group)
+        middle = slice((x + 1) * group + channels, (x + 1) * group + 2 * channels)
+        for side in range(2):
+            wide = jnp.concatenate([shifted[side, c, rows, :] for c in range(4)], axis=1)
+            part = jnp.dot(kernel_ref[...], wide, preferred_element_type=F32)
+            for y in range(2):
+                at = (side * 2 + y) * channels
+                centre = shifted[side, y + 1, middle, :]
+                latent[at : at + channels, :] = latent_tile(part, centre, y)
+        sampled = jnp.dot(latent[...], wz_ref[...], preferred_element_type=F32)
+        for side in range(2):
+            for y in range(2):
+                at = (side * 2 + y) * channels
+                row = x * (span_y + 2) + side * span_y + y
+                total += sampled[at : at + channels] * wxy_ref[row : row + 1, :]
     feature = lax.dot_general(
         pick_ref[...], total.astype(BF16), (((1,), (1,)), ((), ())), preferred_element_type=F32
     ).astype(BF16)
+    for copy in copies:
+        copy.wait()
     half = feature.shape[0] // 2
     for s in range(2):
         span = slice(s * half, (s + 1) * half)
@@ -230,10 +296,7 @@
     slots = bricks * sects * capacity
     outputs = dense_last.shape[1]
     lines = ("sect", "slab")
-    brick, line = lax.axis_index("brick"), lax.axis_index(lines)
-    flags = jnp.stack(
-        [brick > 0, brick < bricks - 1, line > 0, line < lax.axis_size(lines) - 1]
-    ).astype(jnp.int32)
+    width = lax.axis_size(lines)
 
     def block(*shape):
         return jax.ShapeDtypeStruct(shape, BF16)
@@ -263,24 +326,40 @@
         [],
         "points",
         12,
-        n_smem=1,
-    )(flags, point_place, destination.reshape(1, count), point_attr.T, dense_first, conv_kernels[0])
-    to_right, to_left = call(
-        edges_body, [block(span_x + 2 * HALO, HALO, channels, span_z)] * 2, [], "edges", 8
-    )(own, before, after, wxy)
-    left = shift(to_right, lines, 1)
-    right = shift(to_left, lines, -1)
-    wide = (span_x + 2 * HALO) * 3 * channels
+    )(point_place, destination.reshape(1, count), point_attr.T, dense_first, conv_kernels[0])
+    edge = block(span_x + 2 * HALO, HALO, channels, span_z)
+    to_partner, to_cross = call(edges_body, [edge] * 2, [], "edges", 4)(
+        own, before, after, wxy
+    )
+    partner = lax.ppermute(to_partner, lines, [(i, i ^ 1) for i in range(width)])
+    inward = [(i, i + 1) for i in range(1, width - 1, 2)]
+    cross = lax.ppermute(to_cross, lines, inward + [(j, i) for i, j in inward])
+    rows = (span_x + 2 * HALO) * 3 * channels
+    total = call(
+        inner_body,
+        jax.ShapeDtypeStruct((channels, count), F32),
+        [
+            pltpu.VMEM((rows, span_y * span_z), BF16),
+            pltpu.VMEM(((span_y - 2) * channels, span_z), BF16),
+        ],
+        "inner",
+        10,
+    )(own, before, after, kernel, wz, wxy)
     value = call(
-        main_body,
+        outer_body,
         jax.ShapeDtypeStruct((2, outputs, slots // 2), F32),
         [
-            pltpu.VMEM((wide, (span_y + 2 * HALO) * span_z), BF16),
-            pltpu.VMEM(((span_y + 2) * channels, span_z), BF16),
+            pltpu.VMEM((2, 4, rows, span_z), BF16),
+            pltpu.VMEM((4 * channels, span_z), BF16),
+            pltpu.VMEM(dense_first.shape, BF16),
+            pltpu.VMEM(dense_middle.shape, BF16),
+            pltpu.SemaphoreType.DMA((2,)),
         ],
-        "main",
-        28,
-    )(own, before, after, right, left, kernel, pick, wz, wxy, pre, dense_first, dense_last, dense_middle)
+        "outer",
+        16,
+        n_hbm=2,
+    )(own, before, after, partner, cross, kernel, total, pick, wz, wxy, pre, dense_last,
+      dense_first, dense_middle)
     value = value.transpose(1, 0, 2).reshape(outputs, sects, bricks, capacity)
     value = swap_blocks(value, "sect", 1)
     value = swap_blocks(value, "brick", 2)

time: 48.3 us -> 43.9 us (0.909)
  starting transfers between devices: 20.5 us -> 16.5 us
  Pallas kernels: 7.58 us -> 11.5 us
  local copies, waits for them, and re-layouts: 9.47 us -> 5.93 us
  waiting for transfers between devices: 9.88 us -> 9.39 us
    ppermute x4 -> x2, starting transfers between devices: 10.6 us -> 6.26 us  [shift(): return lax.ppermute(array, axes, pairs)]
    pallas_call x4 -> x5, Pallas kernels: 7.58 us -> 11.5 us  [run(): pl.pallas_call(body, out_shape=outs, in_specs=[pl.BlockSpec(memory_space=...]
    unnamed x18 -> x14, local copies, waits for them, and re-layouts: 8.66 us -> 5.12 us
    ppermute x0 -> x2, starting transfers between devices: none -> 0.75 us  [the longest x1 0.68 us: on_device(): cross = lax.ppermute(to_cross, lines, inward + [(j, i) for i, j in inward])]
    ppermute x3, starting transfers between devices: 9.94 us -> 9.45 us  [swap_blocks(): got = lax.ppermute(sent, axis, [(i, i ^ step) for i in range(size)])]
    ppermute x4 -> x2, waiting for transfers between devices: 4.18 us -> 3.72 us  [shift(): return lax.ppermute(array, axes, pairs)]
  transfers between devices with their start and end apart: 7 -> 7, of which waited for: 5 -> 4; matrix products, arithmetic and copies ran while one was open for 0% -> 0% of each run, Pallas kernels for 2% -> 9%
where the time goes in v3:
time: 43.9 us; the launch traced here: 43.5 us
  starting transfers between devices  16.5 us (38%)
  Pallas kernels  11.5 us (26%)
  waiting for transfers between devices  9.39 us (21%)
  local copies, waits for them, and re-layouts  5.93 us (14%)
    pallas_call x5, Pallas kernels, run(): pl.pallas_call(body, out_shape=outs, in_specs=[pl.BlockSpec(memory_space=...  11.5 us
    ppermute x3, starting transfers between devices, swap_blocks(): got = lax.ppermute(sent, axis, [(i, i ^ step) for i in range(size)])  9.45 us
    ppermute x2, starting transfers between devices, shift(): return lax.ppermute(array, axes, pairs)  6.26 us
    ppermute x3, waiting for transfers between devices, swap_blocks(): got = lax.ppermute(sent, axis, [(i, i ^ step) for i in range(size)])  5.67 us
    unnamed x14, local copies, waits for them, and re-layouts  5.12 us
    ppermute x2, waiting for transfers between devices, shift(): return lax.ppermute(array, axes, pairs)  3.72 us
  transfers between devices with their start and end apart: 7, of which 4 were waited for; matrix products, arithmetic and copies ran while one was open for 0% of the time, Pallas kernels for 9%

profile of v3, /device:TPU:0, one launch (start us, length us, event | category | flops | bytes accessed | tf_op | source)
XLA Modules:
  0.0 43.5 jit_solution(14842995550797633909)
XLA Ops:
  0.0 1.0 %copy-done.1 = bf16[64,4,8,128]{3,2,1,0:T(8,128)(2,1)S(1)} copy-done((bf16[64,4,8,128]{3,2,1,0:T(8,128)(2,1)S(1)}, bf16[64,4,8,128]{3,2,1,0:T(8,128)(2,1)}, u32[]{:S(2)}) %copy-start.1) | copy-done | bytes 524312
  1.0 0.3 columns.1
  1.3 5.0 %collective-permute-start = (bf16[2,8,64,128]{3,2,1,0:T(8,128)(2,1)S(1)}, bf16[2,8,64,128]{3,2,1,0:T(8,128)(2,1)S(1)}, u32[]{:S(2)}, u32[]{:S(2)}) collective-permute-start(bf16[2,8,64,128]{3,2,1,0:T(8,128)(2,1)S(1)} %get-tuple-element.16), channel_id=1, source_target_pairs={{0,4},{4,8},{8,12},{1,5},{5,9},{9,13},{2,6},{6,10},{10,14},{3,7},{... | collective-permute-start | bytes 786440 | tf_op jit(solution)/shard_map/ppermute | solution.py:258
  6.3 1.3 %collective-permute-start.1 = (bf16[2,8,64,128]{3,2,1,0:T(8,128)(2,1)S(1)}, bf16[2,8,64,128]{3,2,1,0:T(8,128)(2,1)S(1)}, u32[]{:S(2)}, u32[]{:S(2)}) collective-permute-start(bf16[2,8,64,128]{3,2,1,0:T(8,128)(2,1)S(1)} %get-tuple-element.17), channel_id=1, source_target_pairs={{4,0},{8,4},{12,8},{5,1},{9,5},{13,9},{6,2},{10,6},{14,10},{7,3},{... | collective-permute-start | bytes 786440 | tf_op jit(solution)/shard_map/ppermute | solution.py:258
  7.6 0.0 copy-start
  7.6 0.9 %copy-done = bf16[2,128,512]{2,1,0:T(8,128)(2,1)S(1)} copy-done((bf16[2,128,512]{2,1,0:T(8,128)(2,1)S(1)}, bf16[2,128,512]{2,1,0:T(8,128)(2,1)}, u32[]{:S(2)}) %copy-start) | copy-done | bytes 262168
  8.5 1.0 %copy-done.2 = bf16[1,3,3,3,64,64]{5,4,3,2,1,0:T(8,128)(2,1)S(1)} copy-done((bf16[1,3,3,3,64,64]{5,4,3,2,1,0:T(8,128)(2,1)S(1)}, bf16[1,3,3,3,64,64]{5,4,3,2,1,0:T(8,128)(2,1)}, u32[]{:S(2)}) %copy-start.2) | copy-done | bytes 221208
  9.6 0.8 %copy-done.3 = bf16[256,64]{0,1:T(8,128)(2,1)S(1)} copy-done((bf16[256,64]{0,1:T(8,128)(2,1)S(1)}, bf16[256,64]{0,1:T(8,128)(2,1)}, u32[]{:S(2)}) %copy-start.3) | copy-done | bytes 32792
  10.3 0.7 %copy-done.5 = f32[3,256]{1,0:T(4,128)S(1)} copy-done((f32[3,256]{1,0:T(4,128)S(1)}, f32[3,256]{1,0:T(4,128)}, u32[]{:S(2)}) %copy-start.5) | copy-done | bytes 3096
  11.0 0.7 %copy-done.6 = s32[256,1]{0,1:T(1,128)S(1)} copy-done((s32[256,1]{0,1:T(1,128)S(1)}, s32[256,1]{0,1:T(1,128)}, u32[]{:S(2)}) %copy-start.6) | copy-done | bytes 1048
  11.7 0.5 %points.1 = (bf16[320,256]{1,0:T(8,128)(2,1)S(1)}, bf16[128,256]{1,0:T(8,128)(2,1)S(1)}, f32[60,256]{1,0:T(8,128)S(1)}, f32[320,512]{1,0:T(8,128)S(1)}, bf16[192,576]{1,0:T(8,128)(2,1)S(1)}) custom-call(f32[3,256]{1,0:T(4,128)S(1)} %copy-done.5, s32[1,256]{1,0:T(1,128)S(1)} %bitcast.47, bf16[64,256]{1,0:T(8,128)(2,1)S(1)} %bitcast.46, ...), custom_call_target="tpu_custom_call" | custom-call | tf_op jit(solution)/shard_map/points/pallas_call | solution.py:29
  12.2 3.7 %collective-permute-done.1.after_ref = bf16[2,8,64,128]{3,2,1,0:T(8,128)(2,1)S(1)} collective-permute-done((bf16[2,8,64,128]{3,2,1,0:T(8,128)(2,1)S(1)}, bf16[2,8,64,128]{3,2,1,0:T(8,128)(2,1)S(1)}, u32[]{:S(2)}, u32[]{:S(2)}) %collective-permute-start.1) | collective-permute-done | bytes 262176 | tf_op jit(solution)/shard_map/ppermute | solution.py:258
  16.0 0.1 collective-permute-start.2
  16.1 0.7 %collective-permute-start.3 = (bf16[8,2,64,128]{3,2,1,0:T(8,128)(2,1)S(1)}, bf16[8,2,64,128]{3,2,1,0:T(8,128)(2,1)S(1)}, u32[]{:S(2)}, u32[]{:S(2)}) collective-permute-start(bf16[8,2,64,128]{3,2,1,0:T(8,128)(2,1)S(1)} %get-tuple-element.20), channel_id=1, source_target_pairs={{1,2},{2,1},{5,6},{6,5},{9,10},{10,9},{13,14},{14,13},{17,18},{18,... | collective-permute-start | bytes 786440 | tf_op jit(solution)/shard_map/ppermute | solution.py:336
  16.8 3.3 %inner.1.total_ref = f32[64,256]{1,0:T(8,128)S(1)} custom-call(bf16[4,8,64,128]{3,2,1,0:T(8,128)(2,1)S(1)} %get-tuple-element.15.own_ref, bf16[2,8,64,128]{3,2,1,0:T(8,128)(2,1)S(1)} %collective-permute-done.before_ref, bf16[2,8,64,128]{3,2,1,0:T(8,128)(2,1)S(1)} %collective-permute-done.1.after_ref, bf16[192,576]{1,0:T(8,128)(2,1)S(1)} %get-tuple-element.21.kernel_ref, ...), custom_call_target="tpu_custom_call" | custom-call | tf_op jit(solution)/shard_map/inner/pallas_call | solution.py:29
  20.1 7.3 %outer.1 = f32[2,4,160]{2,1,0:T(4,128)S(1)} custom-call(bf16[4,8,64,128]{3,2,1,0:T(8,128)(2,1)S(1)} %get-tuple-element.15.own_ref, bf16[2,8,64,128]{3,2,1,0:T(8,128)(2,1)S(1)} %collective-permute-done.before_ref, bf16[2,8,64,128]{3,2,1,0:T(8,128)(2,1)S(1)} %collective-permute-done.1.after_ref, ...), custom_call_target="tpu_custom_call" | custom-call | tf_op jit(solution)/shard_map/outer/pallas_call | solution.py:29
  27.4 0.1 reshape_reshape.2
  27.5 5.1 %collective-permute-start.4 = (f32[4,1,1,4,40]{4,3,0,2,1:T(4,128)S(1)}, f32[4,1,1,4,40]{4,3,0,2,1:T(4,128)S(1)}, u32[]{:S(2)}, u32[]{:S(2)}) collective-permute-start(f32[4,1,1,4,40]{4,3,0,2,1:T(4,128)S(1)} %dynamic-slice_bitcast_fusion), channel_id=1, source_target_pairs={{0,2},{2,0},{1,3},{3,1},{4,6},{6,4},{5,7},{7,5},{8,10},{10,8},{9,1... | collective-permute-start | bytes 7688 | tf_op jit(solution)/shard_map/ppermute | solution.py:272
  32.7 1.7 %collective-permute-done.4 = f32[4,1,1,4,40]{4,3,0,2,1:T(4,128)S(1)} collective-permute-done((f32[4,1,1,4,40]{4,3,0,2,1:T(4,128)S(1)}, f32[4,1,1,4,40]{4,3,0,2,1:T(4,128)S(1)}, u32[]{:S(2)}, u32[]{:S(2)}) %collective-permute-start.4) | collective-permute-done | bytes 2592 | tf_op jit(solution)/shard_map/ppermute | solution.py:272
  34.4 2.7 %collective-permute-start.5 = (f32[4,2,1,2,40]{4,3,1,0,2:T(2,128)S(1)}, f32[4,2,1,2,40]{4,3,1,0,2:T(2,128)S(1)}, u32[]{:S(2)}, u32[]{:S(2)}) collective-permute-start(f32[4,2,1,2,40]{4,3,1,0,2:T(2,128)S(1)} %bitcast.51), channel_id=1, source_target_pairs={{0,8},{4,12},{8,0},{12,4},{1,9},{5,13},{9,1},{13,5},{2,10},{6,14},... | collective-permute-start | bytes 7688 | tf_op jit(solution)/shard_map/ppermute | solution.py:272
  37.0 2.0 %collective-permute-done.5 = f32[4,2,1,2,40]{4,3,1,0,2:T(2,128)S(1)} collective-permute-done((f32[4,2,1,2,40]{4,3,1,0,2:T(2,128)S(1)}, f32[4,2,1,2,40]{4,3,1,0,2:T(2,128)S(1)}, u32[]{:S(2)}, u32[]{:S(2)}) %collective-permute-start.5) | collective-permute-done | bytes 2592 | tf_op jit(solution)/shard_map/ppermute | solution.py:272
  39.0 1.6 %collective-permute-start.6 = (f32[4,2,2,1,40]{4,2,1,0,3:T(2,128)S(1)}, f32[4,2,2,1,40]{4,2,1,0,3:T(2,128)S(1)}, u32[]{:S(2)}, u32[]{:S(2)}) collective-permute-start(f32[4,2,2,1,40]{4,2,1,0,3:T(2,128)S(1)} %bitcast.52), channel_id=1, source_target_pairs={{0,4},{4,0},{8,12},{12,8},{1,5},{5,1},{9,13},{13,9},{2,6},{6,2},{1... | collective-permute-start | bytes 7688 | tf_op jit(solution)/shard_map/ppermute | solution.py:272
  40.7 2.1 %collective-permute-done.6 = f32[4,2,2,1,40]{4,2,1,0,3:T(2,128)S(1)} collective-permute-done((f32[4,2,2,1,40]{4,2,1,0,3:T(2,128)S(1)}, f32[4,2,2,1,40]{4,2,1,0,3:T(2,128)S(1)}, u32[]{:S(2)}, u32[]{:S(2)}) %collective-permute-start.6) | collective-permute-done | bytes 2592 | tf_op jit(solution)/shard_map/ppermute | solution.py:272
  42.8 0.7 %reshape.19 = f32[4,320]{1,0:T(4,128)} reshape(f32[4,4,2,40]{3,2,1,0:T(2,128)S(1)} %copy.19) | data formatting | bytes 10240 | tf_op jit(solution)/shard_map/reshape | solution.py:366
  (22 shorter events, 0.2 us)
Async XLA Ops:
  0.0 1.0 %copy-start.1 = (bf16[64,4,8,128]{3,2,1,0:T(8,128)(2,1)S(1)}, bf16[64,4,8,128]{3,2,1,0:T(8,128)(2,1)}, u32[]{:S(2)}) copy-start(bf16[64,4,8,128]{3,2,1,0:T(8,128)(2,1)} %g_ref.1) | copy-start | bytes 1572868
  1.0 19.1 %copy-start.4 = (bf16[2,4,512]{2,1,0:T(4,128)(2,1)S(1)}, bf16[2,4,512]{2,1,0:T(4,128)(2,1)}, u32[]{:S(2)}) copy-start(bf16[2,4,512]{2,1,0:T(4,128)(2,1)} %last_ref.1) | copy-start | bytes 24580
  1.3 10.9 %collective-permute-start = (bf16[2,8,64,128]{3,2,1,0:T(8,128)(2,1)S(1)}, bf16[2,8,64,128]{3,2,1,0:T(8,128)(2,1)S(1)}, u32[]{:S(2)}, u32[]{:S(2)}) collective-permute-start(bf16[2,8,64,128]{3,2,1,0:T(8,128)(2,1)S(1)} %get-tuple-element.16), channel_id=1, source_target_pairs={{0,4},{4,8},{8,12},{1,5},{5,9},{9,13},{2,6},{6,10},{10,14},{3,7},{... | collective-permute-start | bytes 786440 | tf_op jit(solution)/shard_map/ppermute | solution.py:258
  6.3 9.7 %collective-permute-start.1 = (bf16[2,8,64,128]{3,2,1,0:T(8,128)(2,1)S(1)}, bf16[2,8,64,128]{3,2,1,0:T(8,128)(2,1)S(1)}, u32[]{:S(2)}, u32[]{:S(2)}) collective-permute-start(bf16[2,8,64,128]{3,2,1,0:T(8,128)(2,1)S(1)} %get-tuple-element.17), channel_id=1, source_target_pairs={{4,0},{8,4},{12,8},{5,1},{9,5},{13,9},{6,2},{10,6},{14,10},{7,3},{... | collective-permute-start | bytes 786440 | tf_op jit(solution)/shard_map/ppermute | solution.py:258
  7.6 1.0 %copy-start = (bf16[2,128,512]{2,1,0:T(8,128)(2,1)S(1)}, bf16[2,128,512]{2,1,0:T(8,128)(2,1)}, u32[]{:S(2)}) copy-start(bf16[2,128,512]{2,1,0:T(8,128)(2,1)} %first_hbm.1) | copy-start | bytes 786436
  8.5 1.0 %copy-start.2 = (bf16[1,3,3,3,64,64]{5,4,3,2,1,0:T(8,128)(2,1)S(1)}, bf16[1,3,3,3,64,64]{5,4,3,2,1,0:T(8,128)(2,1)}, u32[]{:S(2)}) copy-start(bf16[1,3,3,3,64,64]{5,4,3,2,1,0:T(8,128)(2,1)} %param.9) | copy-start | bytes 663556
  9.6 0.8 %copy-start.3 = (bf16[256,64]{0,1:T(8,128)(2,1)S(1)}, bf16[256,64]{0,1:T(8,128)(2,1)}, u32[]{:S(2)}) copy-start(bf16[256,64]{0,1:T(8,128)(2,1)} %param.11) | copy-start | bytes 98308
  10.3 0.7 %copy-start.5 = (f32[3,256]{1,0:T(4,128)S(1)}, f32[3,256]{1,0:T(4,128)}, u32[]{:S(2)}) copy-start(f32[3,256]{1,0:T(4,128)} %place_ref.1) | copy-start | bytes 9220
  11.0 0.7 %copy-start.6 = (s32[256,1]{0,1:T(1,128)S(1)}, s32[256,1]{0,1:T(1,128)}, u32[]{:S(2)}) copy-start(s32[256,1]{0,1:T(1,128)} %param.12) | copy-start | bytes 3076
  16.0 4.1 %collective-permute-start.2 = (bf16[8,2,64,128]{3,2,1,0:T(8,128)(2,1)S(1)}, bf16[8,2,64,128]{3,2,1,0:T(8,128)(2,1)S(1)}, u32[]{:S(2)}, u32[]{:S(2)}) collective-permute-start(bf16[8,2,64,128]{3,2,1,0:T(8,128)(2,1)S(1)} %get-tuple-element.19), channel_id=1, source_target_pairs={{0,1},{1,0},{2,3},{3,2},{4,5},{5,4},{6,7},{7,6},{8,9},{9,8},{10,11... | collective-permute-start | bytes 786440 | tf_op jit(solution)/shard_map/ppermute | solution.py:334
  16.1 4.1 %collective-permute-start.3 = (bf16[8,2,64,128]{3,2,1,0:T(8,128)(2,1)S(1)}, bf16[8,2,64,128]{3,2,1,0:T(8,128)(2,1)S(1)}, u32[]{:S(2)}, u32[]{:S(2)}) collective-permute-start(bf16[8,2,64,128]{3,2,1,0:T(8,128)(2,1)S(1)} %get-tuple-element.20), channel_id=1, source_target_pairs={{1,2},{2,1},{5,6},{6,5},{9,10},{10,9},{13,14},{14,13},{17,18},{18,... | collective-permute-start | bytes 786440 | tf_op jit(solution)/shard_map/ppermute | solution.py:336
  27.5 6.8 %collective-permute-start.4 = (f32[4,1,1,4,40]{4,3,0,2,1:T(4,128)S(1)}, f32[4,1,1,4,40]{4,3,0,2,1:T(4,128)S(1)}, u32[]{:S(2)}, u32[]{:S(2)}) collective-permute-start(f32[4,1,1,4,40]{4,3,0,2,1:T(4,128)S(1)} %dynamic-slice_bitcast_fusion), channel_id=1, source_target_pairs={{0,2},{2,0},{1,3},{3,1},{4,6},{6,4},{5,7},{7,5},{8,10},{10,8},{9,1... | collective-permute-start | bytes 7688 | tf_op jit(solution)/shard_map/ppermute | solution.py:272
  34.4 4.6 %collective-permute-start.5 = (f32[4,2,1,2,40]{4,3,1,0,2:T(2,128)S(1)}, f32[4,2,1,2,40]{4,3,1,0,2:T(2,128)S(1)}, u32[]{:S(2)}, u32[]{:S(2)}) collective-permute-start(f32[4,2,1,2,40]{4,3,1,0,2:T(2,128)S(1)} %bitcast.51), channel_id=1, source_target_pairs={{0,8},{4,12},{8,0},{12,4},{1,9},{5,13},{9,1},{13,5},{2,10},{6,14},... | collective-permute-start | bytes 7688 | tf_op jit(solution)/shard_map/ppermute | solution.py:272
  39.0 3.7 %collective-permute-start.6 = (f32[4,2,2,1,40]{4,2,1,0,3:T(2,128)S(1)}, f32[4,2,2,1,40]{4,2,1,0,3:T(2,128)S(1)}, u32[]{:S(2)}, u32[]{:S(2)}) collective-permute-start(f32[4,2,2,1,40]{4,2,1,0,3:T(2,128)S(1)} %bitcast.52), channel_id=1, source_target_pairs={{0,4},{4,0},{8,12},{12,8},{1,5},{5,1},{9,13},{13,9},{2,6},{6,2},{1... | collective-permute-start | bytes 7688 | tf_op jit(solution)/shard_map/ppermute | solution.py:272

commit v4 on v3

v4 whole, which is shorter than its diff:
```python
import jax
import jax.numpy as jnp
from jax import lax
from jax.experimental import pallas as pl
from jax.experimental.pallas import tpu as pltpu
from jax.sharding import PartitionSpec as P


F32 = jnp.float32
BF16 = jnp.bfloat16
HALO = 2


def hat(offset):
    return jnp.maximum(0.0, 1.0 - jnp.abs(offset))


def gelu(value):
    half = 0.5 * value
    slope = 0.7978845608028654
    return half + half * jnp.tanh(value * (slope + (slope * 0.044715) * (value * value)))


def iota(shape, axis):
    return lax.broadcasted_iota(jnp.int32, shape, axis)


def call(body, outs, scratch, mib, n_hbm=0):
    def run(*args):
        spaces = [pltpu.VMEM] * (len(args) - n_hbm) + [pltpu.HBM] * n_hbm
        args = [pltpu.with_memory_space_constraint(a, s) if s == pltpu.HBM else a for a, s in zip(args, spaces)]
        return pl.pallas_call(
            body,
            out_shape=outs,
            in_specs=[pl.BlockSpec(memory_space=s) for s in spaces],
            out_specs=jax.tree.map(lambda _: pl.BlockSpec(memory_space=pltpu.VMEM), outs),
            scratch_shapes=scratch,
            compiler_params=pltpu.CompilerParams(vmem_limit_bytes=mib << 20),
        )(*args)

    return run


def columns_body(g_ref, own_ref, up_ref, down_ref, cross_ref):
    span_x, span_y = g_ref.shape[1:3]
    slab = lax.axis_index("slab")
    for x in range(span_x):
        layer = jnp.swapaxes(g_ref[:, x].astype(F32), 0, 1).astype(BF16)
        own_ref[x] = layer
        if x < HALO:
            down_ref[x] = layer
        if x >= span_x - HALO:
            up_ref[x - (span_x - HALO)] = layer
    for side in range(2):

        @pl.when(slab == side)
        def _(side=side):
            cross_ref[...] = own_ref[:, span_y - HALO :] if side else own_ref[:, :HALO]


def edges_body(own_ref, before_ref, after_ref, _, partner_ref, cross_ref):
    span_x, span_y = own_ref.shape[:2]
    for slab in range(2):

        @pl.when(lax.axis_index("slab") == slab)
        def _(slab=slab):
            near, far = slice(0, HALO), slice(span_y - HALO, span_y)
            facing, outward = (near, far) if slab else (far, near)
            partner_ref[:HALO] = before_ref[:, facing]
            partner_ref[HALO : HALO + span_x] = own_ref[:, facing]
            partner_ref[HALO + span_x :] = after_ref[:, facing]
            cross_ref[:HALO] = before_ref[:, outward]
            cross_ref[HALO:] = after_ref[:, outward]


def make_points_body(span_x, span_y, bricks, sects, capacity):
    def body(
        place_ref, dest_ref, attr_ref, first_ref, conv_ref, middle_hbm,
        pick_ref, wz_ref, wxy_ref, pre_ref, kernel_ref, middle_ref, sem,
    ):
        fetch = pltpu.make_async_copy(middle_hbm, middle_ref, sem)
        fetch.start()
        count = place_ref.shape[1]
        span_z = wz_ref.shape[0]
        slots = pick_ref.shape[0]
        brick, line = lax.axis_index("brick"), lax.axis_index(("sect", "slab"))
        last_brick, last_line = lax.axis_size("brick") - 1, lax.axis_size(("sect", "slab")) - 1
        half = slots // 2
        local_x = place_ref[0:1, :] * span_x
        local_y = place_ref[1:2, :] * span_y
        local_z = place_ref[2:3, :] * span_z
        cell_z = iota((span_z, count), 0).astype(F32) + 0.5
        wz_ref[...] = hat(local_z - cell_z).astype(BF16)
        weight_y = []
        for y in range(span_y + 2):
            w = hat(local_y - (y - 0.5))
            if y == 0:
                w = jnp.where(line > 0, w, 0.0)
            if y == span_y + 1:
                w = jnp.where(line < last_line, w, 0.0)
            weight_y.append(w)
        for x in range(span_x + 2):
            w = hat(local_x - (x - 0.5))
            if x == 0:
                w = jnp.where(brick > 0, w, 0.0)
            if x == span_x + 1:
                w = jnp.where(brick < last_brick, w, 0.0)
            for y in range(span_y + 2):
                row = x * (span_y + 2) + y
                wxy_ref[row : row + 1, :] = w * weight_y[y]
        row = dest_ref[...].astype(F32)
        earlier, later = iota((count, count), 0), iota((count, count), 1)
        diagonal = jnp.where(earlier == later, jnp.broadcast_to(row, (count, count)), 0.0)
        along = jnp.sum(diagonal, axis=1, keepdims=True)
        same = jnp.where((along == row) & (earlier < later), 1.0, 0.0)
        arrival = jnp.sum(same, axis=0, keepdims=True).astype(jnp.int32)
        target = row.astype(jnp.int32)
        slot = ((target % sects) * bricks + target // sects) * capacity + arrival
        pick = jnp.where(iota((slots, count), 0) == slot, 1.0, 0.0).astype(BF16)
        pick_ref[...] = pick
        attr = lax.dot_general(
            pick, attr_ref[...], (((1,), (1,)), ((), ())), preferred_element_type=F32
        ).astype(BF16)
        channels = first_ref.shape[1] - attr.shape[1]
        for s in range(2):
            pre_ref[s] = jnp.dot(
                attr[s * half : (s + 1) * half], first_ref[s, channels:], preferred_element_type=F32
            )
        group = 9 * channels
        kernel_ref[:channels, 3 * group :] = jnp.zeros((channels, group), BF16)
        kernel_ref[channels:, :group] = jnp.zeros((channels, group), BF16)
        for a in range(3):
            for b in range(3):
                for e in range(3):
                    tile = conv_ref[a, b, e].astype(F32).T.astype(BF16)
                    for j in range(2):
                        lanes = (j + b) * group + (a * 3 + e) * channels
                        kernel_ref[j * channels : (j + 1) * channels, lanes : lanes + channels] = tile
        fetch.wait()

    return body


def shifted_tiles(tile):
    span_z = tile.shape[1]
    lane = iota(tile.shape, 1)
    wide = tile.astype(F32)
    lower = jnp.where(lane == 0, 0.0, pltpu.roll(wide, 1, 1)).astype(BF16)
    upper = jnp.where(lane == span_z - 1, 0.0, pltpu.roll(wide, span_z - 1, 1)).astype(BF16)
    return lower, tile, upper


def layer_of(own_ref, before_ref, after_ref, x):
    span_x = own_ref.shape[0]
    if x < HALO:
        return before_ref, x
    if x >= HALO + span_x:
        return after_ref, x - HALO - span_x
    return own_ref, x - HALO


def inner_body(
    own_ref, before_ref, after_ref, kernel_ref, wz_ref, wxy_ref, total_ref, shifted, latent
):
    span_x, span_y, channels, span_z = own_ref.shape
    group, pairs, step = 3 * channels, (span_y - 2) // 2, 2

    def put(x):
        ref, at = layer_of(own_ref, before_ref, after_ref, x)
        for y in range(span_y):
            for e, piece in enumerate(shifted_tiles(ref[at, y])):
                base = x * group + e * channels
                shifted[base : base + channels, y * span_z : (y + 1) * span_z] = piece

    def lanes(y):
        return slice(y * span_z, (y + 1) * span_z)

    put(0)
    put(1)
    total = jnp.zeros(total_ref.shape, F32)
    for x in range(0, span_x + 2, step):
        layers = range(x, x + step)
        for k in layers:
            put(k + 2)
        wide = jnp.concatenate(
            [
                jnp.concatenate(
                    [shifted[k * group : (k + 3) * group, lanes(2 * p + c)] for k in layers for p in range(pairs)],
                    axis=1,
                )
                for c in range(4)
            ],
            axis=0,
        )
        part = jnp.dot(kernel_ref[...], wide, preferred_element_type=F32)
        for k in layers:
            ref, at = layer_of(own_ref, before_ref, after_ref, k + 1)
            for y in range(2 * pairs):
                response = part[
                    (y % 2) * channels : (y % 2 + 1) * channels, lanes((k - x) * pairs + y // 2)
                ]
                base = ((k - x) * 2 * pairs + y) * channels
                latent[base : base + channels, :] = (
                    ref[at, y + 1].astype(F32) + gelu(response)
                ).astype(BF16)
        sampled = jnp.dot(latent[...], wz_ref[...], preferred_element_type=F32)
        for k in layers:
            for y in range(2 * pairs):
                row = k * (span_y + 2) + y + 2
                base = ((k - x) * 2 * pairs + y) * channels
                total += sampled[base : base + channels] * wxy_ref[row : row + 1, :]
    total_ref[...] = total


def outer_body(
    own_ref, before_ref, after_ref, partner_ref, cross_ref, corner_ref, kernel_ref, total_ref,
    pick_ref, wz_ref, wxy_ref, pre_ref, last_ref, first_ref, middle_ref,
    value_ref, feature_ref, shifted, latent,
):
    span_x, span_y, channels, span_z = own_ref.shape
    group = 3 * channels
    left_chip = lax.axis_index("slab") == 0

    def put(x):
        ref, at = layer_of(own_ref, before_ref, after_ref, x)
        far, near = layer_of(cross_ref, corner_ref, corner_ref.at[HALO:], x)
        for j in range(2):
            cross, partner = far[near, j].astype(F32), partner_ref[x, j].astype(F32)
            left = jnp.where(left_chip, cross, partner).astype(BF16)
            right = jnp.where(left_chip, partner, cross).astype(BF16)
            for side, column, tile in (
                (0, j, left),
                (0, j + HALO, ref[at, j]),
                (1, j, ref[at, span_y - HALO + j]),
                (1, j + HALO, right),
            ):
                for e, piece in enumerate(shifted_tiles(tile)):
                    rows = slice(x * group + e * channels, x * group + (e + 1) * channels)
                    shifted[column, rows, side * span_z : (side + 1) * span_z] = piece

    put(0)
    put(1)
    total = total_ref[...]
    for x in range(span_x + 2):
        put(x + 2)
        wide = jnp.concatenate([shifted[c, x * group : (x + 3) * group, :] for c in range(4)], axis=0)
        part = jnp.dot(kernel_ref[...], wide, preferred_element_type=F32)
        middle = slice((x + 1) * group + channels, (x + 1) * group + 2 * channels)
        for y in range(2):
            response = part[y * channels : (y + 1) * channels]
            tiles = (shifted[y + 1, middle, :].astype(F32) + gelu(response)).astype(BF16)
            for side in range(2):
                base = (side * 2 + y) * channels
                latent[base : base + channels, :] = tiles[:, side * span_z : (side + 1) * span_z]
        sampled = jnp.dot(latent[...], wz_ref[...], preferred_element_type=F32)
        for side in range(2):
            for y in range(2):
                base = (side * 2 + y) * channels
                row = x * (span_y + 2) + side * span_y + y
                total += sampled[base : base + channels] * wxy_ref[row : row + 1, :]
    feature = lax.dot_general(
        pick_ref[...], total.astype(BF16), (((1,), (1,)), ((), ())), preferred_element_type=F32
    ).astype(BF16)
    half = feature.shape[0] // 2
    for s in range(2):
        feature_ref[s] = feature[s * half : (s + 1) * half]
    network(1 - own_section(), feature_ref, pre_ref, first_ref, middle_ref, last_ref, value_ref)


def own_section():
    return lax.axis_index("sect") // (lax.axis_size("sect") // 2)


def network(s, feature_ref, pre_ref, first_ref, middle_ref, last_ref, value_ref):
    channels = feature_ref.shape[2]
    act = gelu(
        jnp.dot(feature_ref[s], first_ref[s, :channels], preferred_element_type=F32) + pre_ref[s]
    ).astype(BF16)
    for i in range(middle_ref.shape[1]):
        act = gelu(jnp.dot(act, middle_ref[s, i], preferred_element_type=F32)).astype(BF16)
    value_ref[...] = lax.dot_general(
        last_ref[s], act, (((1,), (1,)), ((), ())), preferred_element_type=F32
    )


def own_body(*refs):
    network(own_section(), *refs)


def shift(array, axes, step):
    size = lax.axis_size(axes)
    pairs = [(i, i + step) for i in range(size) if 0 <= i + step < size]
    return lax.ppermute(array, axes, pairs)


def by_source(kept, got, bit, dim):
    first = jnp.where(bit == 0, kept, got)
    return jnp.stack([first, jnp.where(bit == 0, got, kept)], axis=dim)


def trade(blocks, axis, step, dim):
    bit = (lax.axis_index(axis) // step) % 2
    sent = lax.dynamic_index_in_dim(blocks, 1 - bit, dim, False)
    kept = lax.dynamic_index_in_dim(blocks, bit, dim, False)
    return by_source(kept, swap(sent, axis, step), bit, dim)


def swap(array, axis, step):
    return lax.ppermute(array, axis, [(i, i ^ step) for i in range(lax.axis_size(axis))])


def on_device(
    geometry,
    conv_kernels,
    point_place,
    point_attr,
    destination,
    dense_first,
    dense_middle,
    dense_last,
):
    channels, span_x, span_y, span_z = geometry.shape
    count = point_place.shape[1]
    hidden = dense_first.shape[2]
    bricks, sects = lax.axis_size("brick"), lax.axis_size("sect")
    capacity = 5 * count // (4 * bricks * sects)
    slots = bricks * sects * capacity
    outputs = dense_last.shape[1]
    lines = ("sect", "slab")
    width = lax.axis_size(lines)

    def block(*shape):
        return jax.ShapeDtypeStruct(shape, BF16)

    own, up, down, facing = call(
        columns_body,
        [
            block(span_x, span_y, channels, span_z),
            block(HALO, span_y, channels, span_z),
            block(HALO, span_y, channels, span_z),
            block(span_x, HALO, channels, span_z),
        ],
        [],
        8,
    )(geometry)
    inward = [(i, i + 1) for i in range(1, width - 1, 2)]
    inward = inward + [(j, i) for i, j in inward]
    before = shift(up, "brick", 1)
    after = shift(down, "brick", -1)
    cross = lax.ppermute(facing, lines, inward)
    pick, wz, wxy, pre, kernel, middle = call(
        make_points_body(span_x, span_y, bricks, sects, capacity),
        [
            block(slots, count),
            block(span_z, count),
            jax.ShapeDtypeStruct(((span_x + 2) * (span_y + 2), count), F32),
            jax.ShapeDtypeStruct((2, slots // 2, hidden), F32),
            block(2 * channels, 36 * channels),
            block(*dense_middle.shape),
        ],
        [pltpu.SemaphoreType.DMA],
        16,
        n_hbm=1,
    )(point_place, destination.reshape(1, count), point_attr.T, dense_first, conv_kernels[0], dense_middle)
    to_partner, to_cross = call(
        edges_body,
        [
            block(span_x + 2 * HALO, HALO, channels, span_z),
            block(2 * HALO, HALO, channels, span_z),
        ],
        [],
        4,
    )(own, before, after, wxy)
    partner = lax.ppermute(to_partner, lines, [(i, i ^ 1) for i in range(width)])
    corner = lax.ppermute(to_cross, lines, inward)
    rows = (span_x + 2 * HALO) * 3 * channels
    total = call(
        inner_body,
        jax.ShapeDtypeStruct((channels, count), F32),
        [
            pltpu.VMEM((rows, span_y * span_z), BF16),
            pltpu.VMEM((2 * (span_y - 2) * channels, span_z), BF16),
        ],
        10,
    )(own, before, after, kernel, wz, wxy)
    value = jax.ShapeDtypeStruct((outputs, slots // 2), F32)
    sent, feature = call(
        outer_body,
        [value, block(2, slots // 2, channels)],
        [
            pltpu.VMEM((4, rows, 2 * span_z), BF16),
            pltpu.VMEM((4 * channels, span_z), BF16),
        ],
        12,
    )(own, before, after, partner, cross, corner, kernel, total, pick, wz, wxy, pre, dense_last,
      dense_first, middle)
    got = swap(sent, "sect", sects // 2)
    kept = call(own_body, value, [], 8)(feature, pre, dense_first, middle, dense_last)
    value = by_source(kept, got, own_section(), 1)
    bits = [("sect", 1 << i) for i in reversed(range(sects.bit_length() - 2))]
    bits += [("brick", 1 << i) for i in reversed(range(bricks.bit_length() - 1))]
    value = value.reshape((outputs, 2) + (2,) * len(bits) + (capacity,))
    for i, (axis, step) in enumerate(bits):
        value = trade(value, axis, step, i + 2)
    value = value.reshape(outputs, sects, bricks, capacity)
    return value.transpose(0, 2, 1, 3).reshape(outputs, slots)


def solution(mesh):
    in_specs = (
        P(None, ("case", "brick"), ("sect", "slab"), None),
        P(),
        P(None, ("case", "brick", "sect", "slab")),
        P(("case", "brick", "sect", "slab"), None),
        P(("case", "brick", "sect", "slab"), None),
        P(),
        P(),
        P(),
    )
    out_specs = P(None, ("case", "brick", "sect", "slab"))
    return jax.shard_map(on_device, mesh=mesh, in_specs=in_specs, out_specs=out_specs, check_vma=False)
```

time: 43.9 us -> 42.6 us (0.970)
  waiting for transfers between devices: 9.39 us -> 6.4 us
  starting transfers between devices: 16.5 us -> 18 us
  local copies, waits for them, and re-layouts: 5.93 us -> 7.13 us
  Pallas kernels: 11.5 us -> 10.4 us
    ppermute x4 -> x5, waiting for transfers between devices: 5.67 us -> 4.07 us  [the longest x3 4.06 us: swap(): lax.ppermute(array, axis, [(i, i ^ step) for i in range(lax.axis_size(axi...]
    ppermute x4 -> x5, starting transfers between devices: 10.1 us -> 11.6 us  [the longest x3 10.3 us: swap(): lax.ppermute(array, axis, [(i, i ^ step) for i in range(lax.axis_size(axi...]
    ppermute x2, waiting for transfers between devices: 3.72 us -> 2.33 us  [shift(): return lax.ppermute(array, axes, pairs)]
    unnamed x14 -> x21, local copies, waits for them, and re-layouts: 5.12 us -> 6.23 us
    pallas_call x5 -> x6, Pallas kernels: 11.5 us -> 10.4 us  [run(): pl.pallas_call(body, out_shape=outs, in_specs=[pl.BlockSpec(memory_space=...]
  transfers between devices with their start and end apart: 7 -> 8, of which waited for: 4 -> 3; matrix products, arithmetic and copies ran while one was open for 0% -> 0% of each run, Pallas kernels for 9% -> 14%
where the time goes in v4:
time: 42.6 us; the launch traced here: 42.1 us
  starting transfers between devices  18 us (42%)
  Pallas kernels  10.4 us (24%)
  local copies, waits for them, and re-layouts  7.13 us (17%)
  waiting for transfers between devices  6.4 us (15%)
    pallas_call x6, Pallas kernels, run(): pl.pallas_call(body, out_shape=outs, in_specs=[pl.BlockSpec(memory_space=...  10.4 us
    ppermute x3, starting transfers between devices, swap(): lax.ppermute(array, axis, [(i, i ^ step) for i in range(lax.axis_size(axi...  10.3 us
    ppermute x2, starting transfers between devices, shift(): return lax.ppermute(array, axes, pairs)  6.26 us
    unnamed x21, local copies, waits for them, and re-layouts  6.23 us
    ppermute x3, waiting for transfers between devices, swap(): lax.ppermute(array, axis, [(i, i ^ step) for i in range(lax.axis_size(axi...  4.06 us
    ppermute x2, waiting for transfers between devices, shift(): return lax.ppermute(array, axes, pairs)  2.33 us
  transfers between devices with their start and end apart: 8, of which 3 were waited for; matrix products, arithmetic and copies ran while one was open for 0% of the time, Pallas kernels for 14%

profile of v4, /device:TPU:0, one launch (start us, length us, event | category | flops | bytes accessed | tf_op | source)
XLA Modules:
  0.0 42.1 jit_solution(471832638948189847)
XLA Ops:
  0.0 1.0 %copy-done.4 = bf16[64,4,8,128]{3,2,1,0:T(8,128)(2,1)S(1)} copy-done((bf16[64,4,8,128]{3,2,1,0:T(8,128)(2,1)S(1)}, bf16[64,4,8,128]{3,2,1,0:T(8,128)(2,1)}, u32[]{:S(2)}) %copy-start.4) | copy-done | bytes 524312
  1.0 0.3 shard_map.82
  1.3 5.0 %collective-permute-start = (bf16[2,8,64,128]{3,2,1,0:T(8,128)(2,1)S(1)}, bf16[2,8,64,128]{3,2,1,0:T(8,128)(2,1)S(1)}, u32[]{:S(2)}, u32[]{:S(2)}) collective-permute-start(bf16[2,8,64,128]{3,2,1,0:T(8,128)(2,1)S(1)} %get-tuple-element.20), channel_id=1, source_target_pairs={{0,4},{4,8},{8,12},{1,5},{5,9},{9,13},{2,6},{6,10},{10,14},{3,7},{... | collective-permute-start | bytes 786440 | tf_op jit(solution)/shard_map/ppermute | solution.py:293
  6.3 1.3 %collective-permute-start.1 = (bf16[2,8,64,128]{3,2,1,0:T(8,128)(2,1)S(1)}, bf16[2,8,64,128]{3,2,1,0:T(8,128)(2,1)S(1)}, u32[]{:S(2)}, u32[]{:S(2)}) collective-permute-start(bf16[2,8,64,128]{3,2,1,0:T(8,128)(2,1)S(1)} %get-tuple-element.21), channel_id=1, source_target_pairs={{4,0},{8,4},{12,8},{5,1},{9,5},{13,9},{6,2},{10,6},{14,10},{7,3},{... | collective-permute-start | bytes 786440 | tf_op jit(solution)/shard_map/ppermute | solution.py:293
  7.6 0.9 %copy-done.2 = bf16[2,128,512]{2,1,0:T(8,128)(2,1)S(1)} copy-done((bf16[2,128,512]{2,1,0:T(8,128)(2,1)S(1)}, bf16[2,128,512]{2,1,0:T(8,128)(2,1)}, u32[]{:S(2)}) %copy-start.2) | copy-done | bytes 262168
  8.6 1.0 %copy-done.5 = bf16[1,3,3,3,64,64]{5,4,3,2,1,0:T(8,128)(2,1)S(1)} copy-done((bf16[1,3,3,3,64,64]{5,4,3,2,1,0:T(8,128)(2,1)S(1)}, bf16[1,3,3,3,64,64]{5,4,3,2,1,0:T(8,128)(2,1)}, u32[]{:S(2)}) %copy-start.5) | copy-done | bytes 221208
  9.6 0.8 %copy-done.6 = bf16[256,64]{0,1:T(8,128)(2,1)S(1)} copy-done((bf16[256,64]{0,1:T(8,128)(2,1)S(1)}, bf16[256,64]{0,1:T(8,128)(2,1)}, u32[]{:S(2)}) %copy-start.6) | copy-done | bytes 32792
  10.3 0.7 %copy-done.8 = f32[3,256]{1,0:T(4,128)S(1)} copy-done((f32[3,256]{1,0:T(4,128)S(1)}, f32[3,256]{1,0:T(4,128)}, u32[]{:S(2)}) %copy-start.8) | copy-done | bytes 3096
  11.0 0.7 %copy-done.9 = s32[256,1]{0,1:T(1,128)S(1)} copy-done((s32[256,1]{0,1:T(1,128)S(1)}, s32[256,1]{0,1:T(1,128)}, u32[]{:S(2)}) %copy-start.9) | copy-done | bytes 1048
  11.7 1.9 %shard_map.83 = (bf16[320,256]{1,0:T(8,128)(2,1)S(1)}, bf16[128,256]{1,0:T(8,128)(2,1)S(1)}, f32[60,256]{1,0:T(8,128)S(1)}, f32[2,160,512]{2,1,0:T(8,128)S(1)}, ...) custom-call(f32[3,256]{1,0:T(4,128)S(1)} %copy-done.8, s32[1,256]{1,0:T(1,128)S(1)} %bitcast.30, ...), custom_call_target="tpu_custom_call" | custom-call | tf_op jit(solution)/shard_map/pallas_call | solution.py:32
  13.6 2.3 %collective-permute-done.1.after_ref = bf16[2,8,64,128]{3,2,1,0:T(8,128)(2,1)S(1)} collective-permute-done((bf16[2,8,64,128]{3,2,1,0:T(8,128)(2,1)S(1)}, bf16[2,8,64,128]{3,2,1,0:T(8,128)(2,1)S(1)}, u32[]{:S(2)}, u32[]{:S(2)}) %collective-permute-start.1) | collective-permute-done | bytes 262176 | tf_op jit(solution)/shard_map/ppermute | solution.py:293
  16.1 0.7 %collective-permute-start.3 = (bf16[4,2,64,128]{3,2,1,0:T(8,128)(2,1)S(1)}, bf16[4,2,64,128]{3,2,1,0:T(8,128)(2,1)S(1)}, u32[]{:S(2)}, u32[]{:S(2)}) collective-permute-start(bf16[4,2,64,128]{3,2,1,0:T(8,128)(2,1)S(1)} %get-tuple-element.24), channel_id=1, source_target_pairs={{1,2},{2,1},{5,6},{6,5},{9,10},{10,9},{13,14},{14,13},{17,18},{18,... | collective-permute-start | bytes 393224 | tf_op jit(solution)/shard_map/ppermute | solution.py:350
  16.7 0.7 %collective-permute-start.4 = (bf16[4,2,64,128]{3,2,1,0:T(8,128)(2,1)S(1)}, bf16[4,2,64,128]{3,2,1,0:T(8,128)(2,1)S(1)}, u32[]{:S(2)}, u32[]{:S(2)}) collective-permute-start(bf16[4,2,64,128]{3,2,1,0:T(8,128)(2,1)S(1)} %get-tuple-element.25), channel_id=1, source_target_pairs={{1,2},{2,1},{5,6},{6,5},{9,10},{10,9},{13,14},{14,13},{17,18},{18,... | collective-permute-start | bytes 393224 | tf_op jit(solution)/shard_map/ppermute | solution.py:375
  17.4 2.9 %shard_map.85.total_ref = f32[64,256]{1,0:T(8,128)S(1)} custom-call(bf16[4,8,64,128]{3,2,1,0:T(8,128)(2,1)S(1)} %get-tuple-element.19.own_ref, bf16[2,8,64,128]{3,2,1,0:T(8,128)(2,1)S(1)} %collective-permute-done.before_ref, bf16[2,8,64,128]{3,2,1,0:T(8,128)(2,1)S(1)} %collective-permute-done.1.after_ref, ...), custom_call_target="tpu_custom_call" | custom-call | tf_op jit(solution)/shard_map/pallas_call | solution.py:32
  20.4 4.3 %shard_map.86 = (f32[4,160]{1,0:T(4,128)S(1)}, bf16[2,160,64]{2,1,0:T(8,128)(2,1)S(1)}) custom-call(bf16[4,8,64,128]{3,2,1,0:T(8,128)(2,1)S(1)} %get-tuple-element.19.own_ref, bf16[2,8,64,128]{3,2,1,0:T(8,128)(2,1)S(1)} %collective-permute-done.before_ref, bf16[2,8,64,128]{3,2,1,0:T(8,128)(2,1)S(1)} %collective-permute-done.1.after_ref, ...), custom_call_target="tpu_custom_call" | custom-call | tf_op jit(solution)/shard_map/pallas_call | solution.py:32
  24.6 6.0 %collective-permute-start.5 = (f32[4,160]{1,0:T(4,128)S(1)}, f32[4,160]{1,0:T(4,128)S(1)}, u32[]{:S(2)}, u32[]{:S(2)}) collective-permute-start(f32[4,160]{1,0:T(4,128)S(1)} %get-tuple-element.32), channel_id=1, source_target_pairs={{0,2},{2,0},{1,3},{3,1},{4,6},{6,4},{5,7},{7,5},{8,10},{10,8},{9,1... | collective-permute-start | bytes 7688 | tf_op jit(solution)/shard_map/ppermute | solution.py:309
  30.7 1.1 %copy-done.1 = f32[2,160,512]{2,1,0:T(8,128)S(1)} copy-done((f32[2,160,512]{2,1,0:T(8,128)S(1)}, f32[2,160,512]{2,1,0:T(8,128)}, u32[]{:S(2)}) %copy-start.1) | copy-done | bytes 655384
  31.8 1.0 %shard_map.87 = f32[4,160]{1,0:T(4,128)S(1)} custom-call(bf16[2,160,64]{2,1,0:T(8,128)(2,1)S(1)} %get-tuple-element.31.refs_0_, f32[2,160,512]{2,1,0:T(8,128)S(1)} %copy-done.1, bf16[2,128,512]{2,1,0:T(8,128)(2,1)S(1)} %copy-done.3, bf16[2,3,512,512]{3,2,1,0:T(8,128)(2,1)S(1)} %get-tuple-element.30.middle_ref.refs_3_, bf16[2,4,512]{2,1,0:T(4,128)(2,1)S(1)} %copy-done.7), custom_call_target="tpu_custom_call" | custom-call | tf_op jit(solution)/shard_map/pallas_call | solution.py:32
  32.8 0.1 stack.27
  33.0 2.6 %collective-permute-start.6 = (f32[4,2,2,40]{3,1,0,2:T(2,128)S(1)}, f32[4,2,2,40]{3,1,0,2:T(2,128)S(1)}, u32[]{:S(2)}, u32[]{:S(2)}) collective-permute-start(f32[4,2,2,40]{3,1,0,2:T(2,128)S(1)} %bitcast.36), channel_id=1, source_target_pairs={{0,8},{4,12},{8,0},{12,4},{1,9},{5,13},{9,1},{13,5},{2,10},{6,14},... | collective-permute-start | bytes 7688 | tf_op jit(solution)/shard_map/ppermute | solution.py:309
  35.7 2.0 %collective-permute-done.6 = f32[4,2,2,40]{3,1,0,2:T(2,128)S(1)} collective-permute-done((f32[4,2,2,40]{3,1,0,2:T(2,128)S(1)}, f32[4,2,2,40]{3,1,0,2:T(2,128)S(1)}, u32[]{:S(2)}, u32[]{:S(2)}) %collective-permute-start.6) | collective-permute-done | bytes 2592 | tf_op jit(solution)/shard_map/ppermute | solution.py:309
  37.7 1.6 %collective-permute-start.7 = (f32[4,2,2,40]{3,2,1,0:T(2,128)S(1)}, f32[4,2,2,40]{3,2,1,0:T(2,128)S(1)}, u32[]{:S(2)}, u32[]{:S(2)}) collective-permute-start(f32[4,2,2,40]{3,2,1,0:T(2,128)S(1)} %fusion.1), channel_id=1, source_target_pairs={{0,4},{4,0},{8,12},{12,8},{1,5},{5,1},{9,13},{13,9},{2,6},{6,2},{1... | collective-permute-start | bytes 7688 | tf_op jit(solution)/shard_map/ppermute | solution.py:309
  39.3 2.1 %collective-permute-done.7 = f32[4,2,2,40]{3,2,1,0:T(2,128)S(1)} collective-permute-done((f32[4,2,2,40]{3,2,1,0:T(2,128)S(1)}, f32[4,2,2,40]{3,2,1,0:T(2,128)S(1)}, u32[]{:S(2)}, u32[]{:S(2)}) %collective-permute-start.7) | collective-permute-done | bytes 2592 | tf_op jit(solution)/shard_map/ppermute | solution.py:309
  41.5 0.7 %reshape.16 = f32[4,320]{1,0:T(4,128)} reshape(f32[4,4,2,40]{3,2,1,0:T(2,128)S(1)} %copy.21) | data formatting | bytes 10240 | tf_op jit(solution)/shard_map/reshape | solution.py:406
  (32 shorter events, 0.3 us)
Async XLA Ops:
  0.0 1.0 %copy-start.4 = (bf16[64,4,8,128]{3,2,1,0:T(8,128)(2,1)S(1)}, bf16[64,4,8,128]{3,2,1,0:T(8,128)(2,1)}, u32[]{:S(2)}) copy-start(bf16[64,4,8,128]{3,2,1,0:T(8,128)(2,1)} %g_ref.1) | copy-start | bytes 1572868
  1.3 12.3 %collective-permute-start = (bf16[2,8,64,128]{3,2,1,0:T(8,128)(2,1)S(1)}, bf16[2,8,64,128]{3,2,1,0:T(8,128)(2,1)S(1)}, u32[]{:S(2)}, u32[]{:S(2)}) collective-permute-start(bf16[2,8,64,128]{3,2,1,0:T(8,128)(2,1)S(1)} %get-tuple-element.20), channel_id=1, source_target_pairs={{0,4},{4,8},{8,12},{1,5},{5,9},{9,13},{2,6},{6,10},{10,14},{3,7},{... | collective-permute-start | bytes 786440 | tf_op jit(solution)/shard_map/ppermute | solution.py:293
  6.3 9.7 %collective-permute-start.1 = (bf16[2,8,64,128]{3,2,1,0:T(8,128)(2,1)S(1)}, bf16[2,8,64,128]{3,2,1,0:T(8,128)(2,1)S(1)}, u32[]{:S(2)}, u32[]{:S(2)}) collective-permute-start(bf16[2,8,64,128]{3,2,1,0:T(8,128)(2,1)S(1)} %get-tuple-element.21), channel_id=1, source_target_pairs={{4,0},{8,4},{12,8},{5,1},{9,5},{13,9},{6,2},{10,6},{14,10},{7,3},{... | collective-permute-start | bytes 786440 | tf_op jit(solution)/shard_map/ppermute | solution.py:293
  7.6 1.0 %copy-start.2 = (bf16[2,128,512]{2,1,0:T(8,128)(2,1)S(1)}, bf16[2,128,512]{2,1,0:T(8,128)(2,1)}, u32[]{:S(2)}) copy-start(bf16[2,128,512]{2,1,0:T(8,128)(2,1)} %refs_2_.1) | copy-start | bytes 786436
  8.6 1.0 %copy-start.5 = (bf16[1,3,3,3,64,64]{5,4,3,2,1,0:T(8,128)(2,1)S(1)}, bf16[1,3,3,3,64,64]{5,4,3,2,1,0:T(8,128)(2,1)}, u32[]{:S(2)}) copy-start(bf16[1,3,3,3,64,64]{5,4,3,2,1,0:T(8,128)(2,1)} %param.9) | copy-start | bytes 663556
  9.6 0.8 %copy-start.6 = (bf16[256,64]{0,1:T(8,128)(2,1)S(1)}, bf16[256,64]{0,1:T(8,128)(2,1)}, u32[]{:S(2)}) copy-start(bf16[256,64]{0,1:T(8,128)(2,1)} %param.11) | copy-start | bytes 98308
  10.3 0.7 %copy-start.8 = (f32[3,256]{1,0:T(4,128)S(1)}, f32[3,256]{1,0:T(4,128)}, u32[]{:S(2)}) copy-start(f32[3,256]{1,0:T(4,128)} %place_ref.1) | copy-start | bytes 9220
  11.0 0.7 %copy-start.9 = (s32[256,1]{0,1:T(1,128)S(1)}, s32[256,1]{0,1:T(1,128)}, u32[]{:S(2)}) copy-start(s32[256,1]{0,1:T(1,128)} %param.12) | copy-start | bytes 3076
  11.7 8.7 %copy-start.7 = (bf16[2,4,512]{2,1,0:T(4,128)(2,1)S(1)}, bf16[2,4,512]{2,1,0:T(4,128)(2,1)}, u32[]{:S(2)}) copy-start(bf16[2,4,512]{2,1,0:T(4,128)(2,1)} %refs_4_.1) | copy-start | bytes 24580
  13.6 11.0 %copy-start = (f32[2,160,512]{2,1,0:T(8,128)}, f32[2,160,512]{2,1,0:T(8,128)S(1)}, u32[]{:S(2)}) copy-start(f32[2,160,512]{2,1,0:T(8,128)S(1)} %get-tuple-element.29.pre_ref.refs_1_) | copy-start | bytes 1966084
  16.0 4.3 %collective-permute-start.2 = (bf16[8,2,64,128]{3,2,1,0:T(8,128)(2,1)S(1)}, bf16[8,2,64,128]{3,2,1,0:T(8,128)(2,1)S(1)}, u32[]{:S(2)}, u32[]{:S(2)}) collective-permute-start(bf16[8,2,64,128]{3,2,1,0:T(8,128)(2,1)S(1)} %get-tuple-element.23), channel_id=1, source_target_pairs={{0,1},{1,0},{2,3},{3,2},{4,5},{5,4},{6,7},{7,6},{8,9},{9,8},{10,11... | collective-permute-start | bytes 786440 | tf_op jit(solution)/shard_map/ppermute | solution.py:374
  16.1 4.2 %collective-permute-start.3 = (bf16[4,2,64,128]{3,2,1,0:T(8,128)(2,1)S(1)}, bf16[4,2,64,128]{3,2,1,0:T(8,128)(2,1)S(1)}, u32[]{:S(2)}, u32[]{:S(2)}) collective-permute-start(bf16[4,2,64,128]{3,2,1,0:T(8,128)(2,1)S(1)} %get-tuple-element.24), channel_id=1, source_target_pairs={{1,2},{2,1},{5,6},{6,5},{9,10},{10,9},{13,14},{14,13},{17,18},{18,... | collective-permute-start | bytes 393224 | tf_op jit(solution)/shard_map/ppermute | solution.py:350
  16.7 3.6 %collective-permute-start.4 = (bf16[4,2,64,128]{3,2,1,0:T(8,128)(2,1)S(1)}, bf16[4,2,64,128]{3,2,1,0:T(8,128)(2,1)S(1)}, u32[]{:S(2)}, u32[]{:S(2)}) collective-permute-start(bf16[4,2,64,128]{3,2,1,0:T(8,128)(2,1)S(1)} %get-tuple-element.25), channel_id=1, source_target_pairs={{1,2},{2,1},{5,6},{6,5},{9,10},{10,9},{13,14},{14,13},{17,18},{18,... | collective-permute-start | bytes 393224 | tf_op jit(solution)/shard_map/ppermute | solution.py:375
  20.4 10.3 %copy-start.3 = (bf16[2,128,512]{2,1,0:T(8,128)(2,1)S(1)}, bf16[2,128,512]{2,1,0:T(8,128)(2,1)}, u32[]{:S(2)}) copy-start(bf16[2,128,512]{2,1,0:T(8,128)(2,1)} %refs_2_.1) | copy-start | bytes 786436
  24.6 8.1 %collective-permute-start.5 = (f32[4,160]{1,0:T(4,128)S(1)}, f32[4,160]{1,0:T(4,128)S(1)}, u32[]{:S(2)}, u32[]{:S(2)}) collective-permute-start(f32[4,160]{1,0:T(4,128)S(1)} %get-tuple-element.32), channel_id=1, source_target_pairs={{0,2},{2,0},{1,3},{3,1},{4,6},{6,4},{5,7},{7,5},{8,10},{10,8},{9,1... | collective-permute-start | bytes 7688 | tf_op jit(solution)/shard_map/ppermute | solution.py:309
  30.7 1.1 %copy-start.1 = (f32[2,160,512]{2,1,0:T(8,128)S(1)}, f32[2,160,512]{2,1,0:T(8,128)}, u32[]{:S(2)}) copy-start(f32[2,160,512]{2,1,0:T(8,128)} %copy-done) | copy-start | bytes 1966084
  33.0 4.6 %collective-permute-start.6 = (f32[4,2,2,40]{3,1,0,2:T(2,128)S(1)}, f32[4,2,2,40]{3,1,0,2:T(2,128)S(1)}, u32[]{:S(2)}, u32[]{:S(2)}) collective-permute-start(f32[4,2,2,40]{3,1,0,2:T(2,128)S(1)} %bitcast.36), channel_id=1, source_target_pairs={{0,8},{4,12},{8,0},{12,4},{1,9},{5,13},{9,1},{13,5},{2,10},{6,14},... | collective-permute-start | bytes 7688 | tf_op jit(solution)/shard_map/ppermute | solution.py:309
  37.7 3.7 %collective-permute-start.7 = (f32[4,2,2,40]{3,2,1,0:T(2,128)S(1)}, f32[4,2,2,40]{3,2,1,0:T(2,128)S(1)}, u32[]{:S(2)}, u32[]{:S(2)}) collective-permute-start(f32[4,2,2,40]{3,2,1,0:T(2,128)S(1)} %fusion.1), channel_id=1, source_target_pairs={{0,4},{4,0},{8,12},{12,8},{1,5},{5,1},{9,13},{13,9},{2,6},{6,2},{1... | collective-permute-start | bytes 7688 | tf_op jit(solution)/shard_map/ppermute | solution.py:309

commit v5 on v4

--- a/solution.py
+++ b/solution.py
@@ -41,25 +41,32 @@
     return run
 
 
-def columns_body(g_ref, own_ref, up_ref, down_ref, cross_ref):
+def columns_body(g_ref, own_ref, even_ref, odd_ref, cross_ref):
     span_x, span_y = g_ref.shape[1:3]
-    slab = lax.axis_index("slab")
+    parity, slab = lax.axis_index("brick") % 2, lax.axis_index("slab")
     for x in range(span_x):
-        layer = jnp.swapaxes(g_ref[:, x].astype(F32), 0, 1).astype(BF16)
-        own_ref[x] = layer
-        if x < HALO:
-            down_ref[x] = layer
-        if x >= span_x - HALO:
-            up_ref[x - (span_x - HALO)] = layer
+        own_ref[x] = jnp.swapaxes(g_ref[:, x].astype(F32), 0, 1).astype(BF16)
     for side in range(2):
+
+        @pl.when(parity == side)
+        def _(up=(even_ref, odd_ref)[side], down=(odd_ref, even_ref)[side]):
+            up[...] = own_ref[span_x - HALO :]
+            down[...] = own_ref[:HALO]
 
         @pl.when(slab == side)
         def _(side=side):
             cross_ref[...] = own_ref[:, span_y - HALO :] if side else own_ref[:, :HALO]
 
 
-def edges_body(own_ref, before_ref, after_ref, _, partner_ref, cross_ref):
+def edges_body(own_ref, even_ref, odd_ref, _, before_ref, after_ref, partner_ref, cross_ref):
     span_x, span_y = own_ref.shape[:2]
+    for side in range(2):
+
+        @pl.when(lax.axis_index("brick") % 2 == side)
+        def _(before=(odd_ref, even_ref)[side], after=(even_ref, odd_ref)[side]):
+            before_ref[...] = before[...]
+            after_ref[...] = after[...]
+
     for slab in range(2):
 
         @pl.when(lax.axis_index("slab") == slab)
@@ -75,17 +82,24 @@
 
 def make_points_body(span_x, span_y, bricks, sects, capacity):
     def body(
-        place_ref, dest_ref, attr_ref, first_ref, conv_ref, middle_hbm,
-        pick_ref, wz_ref, wxy_ref, pre_ref, kernel_ref, middle_ref, sem,
+        place_hbm, dest_hbm, conv_hbm, attr_hbm, first_hbm, middle_hbm, last_hbm,
+        pick_ref, wz_ref, wxy_ref, kernel_ref, attr_ref, first_ref, middle_ref, last_ref,
+        place_ref, dest_ref, conv_ref, sems,
     ):
-        fetch = pltpu.make_async_copy(middle_hbm, middle_ref, sem)
-        fetch.start()
+        sources = (place_hbm, dest_hbm, conv_hbm, attr_hbm, first_hbm, middle_hbm, last_hbm)
+        targets = (place_ref, dest_ref, conv_ref, attr_ref, first_ref, middle_ref, last_ref)
+        copies = [
+            pltpu.make_async_copy(source, target, sems.at[i])
+            for i, (source, target) in enumerate(zip(sources, targets))
+        ]
+        for copy in copies:
+            copy.start()
+        copies[0].wait()
         count = place_ref.shape[1]
         span_z = wz_ref.shape[0]
         slots = pick_ref.shape[0]
         brick, line = lax.axis_index("brick"), lax.axis_index(("sect", "slab"))
         last_brick, last_line = lax.axis_size("brick") - 1, lax.axis_size(("sect", "slab")) - 1
-        half = slots // 2
         local_x = place_ref[0:1, :] * span_x
         local_y = place_ref[1:2, :] * span_y
         local_z = place_ref[2:3, :] * span_z
@@ -108,6 +122,7 @@
             for y in range(span_y + 2):
                 row = x * (span_y + 2) + y
                 wxy_ref[row : row + 1, :] = w * weight_y[y]
+        copies[1].wait()
         row = dest_ref[...].astype(F32)
         earlier, later = iota((count, count), 0), iota((count, count), 1)
         diagonal = jnp.where(earlier == later, jnp.broadcast_to(row, (count, count)), 0.0)
@@ -118,14 +133,8 @@
         slot = ((target % sects) * bricks + target // sects) * capacity + arrival
         pick = jnp.where(iota((slots, count), 0) == slot, 1.0, 0.0).astype(BF16)
         pick_ref[...] = pick
-        attr = lax.dot_general(
-            pick, attr_ref[...], (((1,), (1,)), ((), ())), preferred_element_type=F32
-        ).astype(BF16)
-        channels = first_ref.shape[1] - attr.shape[1]
-        for s in range(2):
-            pre_ref[s] = jnp.dot(
-                attr[s * half : (s + 1) * half], first_ref[s, channels:], preferred_element_type=F32
-            )
+        copies[2].wait()
+        channels = conv_ref.shape[-1]
         group = 9 * channels
         kernel_ref[:channels, 3 * group :] = jnp.zeros((channels, group), BF16)
         kernel_ref[channels:, :group] = jnp.zeros((channels, group), BF16)
@@ -136,7 +145,8 @@
                     for j in range(2):
                         lanes = (j + b) * group + (a * 3 + e) * channels
                         kernel_ref[j * channels : (j + 1) * channels, lanes : lanes + channels] = tile
-        fetch.wait()
+        for copy in copies[3:]:
+            copy.wait()
 
     return body
 
@@ -214,8 +224,8 @@
 
 def outer_body(
     own_ref, before_ref, after_ref, partner_ref, cross_ref, corner_ref, kernel_ref, total_ref,
-    pick_ref, wz_ref, wxy_ref, pre_ref, last_ref, first_ref, middle_ref,
-    value_ref, feature_ref, shifted, latent,
+    pick_ref, wz_ref, wxy_ref, attr_ref, first_ref, middle_ref, last_ref,
+    value_ref, row_ref, shifted, latent,
 ):
     span_x, span_y, channels, span_z = own_ref.shape
     group = 3 * channels
@@ -258,55 +268,74 @@
                 base = (side * 2 + y) * channels
                 row = x * (span_y + 2) + side * span_y + y
                 total += sampled[base : base + channels] * wxy_ref[row : row + 1, :]
-    feature = lax.dot_general(
-        pick_ref[...], total.astype(BF16), (((1,), (1,)), ((), ())), preferred_element_type=F32
+    table = jnp.concatenate([total.astype(BF16), attr_ref[...]], axis=0)
+    row = lax.dot_general(
+        pick_ref[...], table, (((1,), (1,)), ((), ())), preferred_element_type=F32
     ).astype(BF16)
-    half = feature.shape[0] // 2
+    half = row.shape[0] // 2
     for s in range(2):
-        feature_ref[s] = feature[s * half : (s + 1) * half]
-    network(1 - own_section(), feature_ref, pre_ref, first_ref, middle_ref, last_ref, value_ref)
+        row_ref[s] = row[s * half : (s + 1) * half]
+    network(1 - own_section(), row_ref, first_ref, middle_ref, last_ref, value_ref)
 
 
 def own_section():
     return lax.axis_index("sect") // (lax.axis_size("sect") // 2)
 
 
-def network(s, feature_ref, pre_ref, first_ref, middle_ref, last_ref, value_ref):
-    channels = feature_ref.shape[2]
-    act = gelu(
-        jnp.dot(feature_ref[s], first_ref[s, :channels], preferred_element_type=F32) + pre_ref[s]
-    ).astype(BF16)
+def own_place():
+    return (
+        lax.axis_index("sect") % (lax.axis_size("sect") // 2) * lax.axis_size("brick")
+        + lax.axis_index("brick")
+    )
+
+
+def network(s, row_ref, first_ref, middle_ref, last_ref, value_ref):
+    act = gelu(jnp.dot(row_ref[s], first_ref[s], preferred_element_type=F32)).astype(BF16)
     for i in range(middle_ref.shape[1]):
         act = gelu(jnp.dot(act, middle_ref[s, i], preferred_element_type=F32)).astype(BF16)
-    value_ref[...] = lax.dot_general(
+    value = lax.dot_general(
         last_ref[s], act, (((1,), (1,)), ((), ())), preferred_element_type=F32
     )
+    blocks, _, capacity = value_ref.shape
+    place = own_place()
+    for q in range(blocks):
+        value_ref[q ^ place] = value[:, q * capacity : (q + 1) * capacity]
 
 
 def own_body(*refs):
     network(own_section(), *refs)
 
 
-def shift(array, axes, step):
-    size = lax.axis_size(axes)
-    pairs = [(i, i + step) for i in range(size) if 0 <= i + step < size]
-    return lax.ppermute(array, axes, pairs)
-
-
-def by_source(kept, got, bit, dim):
-    first = jnp.where(bit == 0, kept, got)
-    return jnp.stack([first, jnp.where(bit == 0, got, kept)], axis=dim)
-
-
-def trade(blocks, axis, step, dim):
-    bit = (lax.axis_index(axis) // step) % 2
-    sent = lax.dynamic_index_in_dim(blocks, 1 - bit, dim, False)
-    kept = lax.dynamic_index_in_dim(blocks, bit, dim, False)
-    return by_source(kept, swap(sent, axis, step), bit, dim)
+def make_deal_body(sent, kept):
+    def body(kept_ref, got_ref, sent_out, kept_out):
+        for out, blocks in ((sent_out, sent), (kept_out, kept)):
+            for i, (which, at) in enumerate(blocks):
+                out[i] = (kept_ref, got_ref)[which][at]
+
+    return body
+
+
+def make_collect_body(order, bricks, sects):
+    def body(kept_ref, got_ref, out_ref, blocks):
+        for r, (which, at) in enumerate(order):
+            blocks[r] = (kept_ref, got_ref)[which][at]
+        capacity = kept_ref.shape[2]
+        me = own_section() * (bricks * sects // 2) + own_place()
+        for brick in range(bricks):
+            for sect in range(sects):
+                lane = (brick * sects + sect) * capacity
+                out_ref[:, lane : lane + capacity] = blocks[(sect * bricks + brick) ^ me]
+
+    return body
 
 
 def swap(array, axis, step):
     return lax.ppermute(array, axis, [(i, i ^ step) for i in range(lax.axis_size(axis))])
+
+
+def swap_pairs(array, axis, start):
+    pairs = [(i, i + 1) for i in range(start, lax.axis_size(axis) - 1, 2)]
+    return lax.ppermute(array, axis, pairs + [(j, i) for i, j in pairs])
 
 
 def on_device(
@@ -321,18 +350,16 @@
 ):
     channels, span_x, span_y, span_z = geometry.shape
     count = point_place.shape[1]
-    hidden = dense_first.shape[2]
     bricks, sects = lax.axis_size("brick"), lax.axis_size("sect")
     capacity = 5 * count // (4 * bricks * sects)
     slots = bricks * sects * capacity
     outputs = dense_last.shape[1]
     lines = ("sect", "slab")
-    width = lax.axis_size(lines)
 
     def block(*shape):
         return jax.ShapeDtypeStruct(shape, BF16)
 
-    own, up, down, facing = call(
+    own, even, odd, facing = call(
         columns_body,
         [
             block(span_x, span_y, channels, span_z),
@@ -343,36 +370,44 @@
         [],
         8,
     )(geometry)
-    inward = [(i, i + 1) for i in range(1, width - 1, 2)]
-    inward = inward + [(j, i) for i, j in inward]
-    before = shift(up, "brick", 1)
-    after = shift(down, "brick", -1)
-    cross = lax.ppermute(facing, lines, inward)
-    pick, wz, wxy, pre, kernel, middle = call(
+    even = swap_pairs(even, "brick", 0)
+    odd = swap_pairs(odd, "brick", 1)
+    cross = swap_pairs(facing, lines, 1)
+    pick, wz, wxy, kernel, attr, first, middle, last = call(
         make_points_body(span_x, span_y, bricks, sects, capacity),
         [
             block(slots, count),
             block(span_z, count),
             jax.ShapeDtypeStruct(((span_x + 2) * (span_y + 2), count), F32),
-            jax.ShapeDtypeStruct((2, slots // 2, hidden), F32),
             block(2 * channels, 36 * channels),
+            block(point_attr.shape[1], count),
+            block(*dense_first.shape),
             block(*dense_middle.shape),
-        ],
-        [pltpu.SemaphoreType.DMA],
-        16,
-        n_hbm=1,
-    )(point_place, destination.reshape(1, count), point_attr.T, dense_first, conv_kernels[0], dense_middle)
-    to_partner, to_cross = call(
+            block(*dense_last.shape),
+        ],
+        [
+            pltpu.VMEM(point_place.shape, F32),
+            pltpu.VMEM((1, count), jnp.int32),
+            pltpu.VMEM(conv_kernels.shape[1:], BF16),
+            pltpu.SemaphoreType.DMA((7,)),
+        ],
+        12,
+        n_hbm=7,
+    )(point_place, destination.reshape(1, count), conv_kernels[0], point_attr.T, dense_first,
+      dense_middle, dense_last)
+    before, after, to_partner, to_cross = call(
         edges_body,
         [
+            block(HALO, span_y, channels, span_z),
+            block(HALO, span_y, channels, span_z),
             block(span_x + 2 * HALO, HALO, channels, span_z),
             block(2 * HALO, HALO, channels, span_z),
         ],
         [],
         4,
-    )(own, before, after, wxy)
-    partner = lax.ppermute(to_partner, lines, [(i, i ^ 1) for i in range(width)])
-    corner = lax.ppermute(to_cross, lines, inward)
+    )(own, even, odd, wxy)
+    partner = swap(to_partner, "slab", 1)
+    corner = swap_pairs(to_cross, lines, 1)
     rows = (span_x + 2 * HALO) * 3 * channels
     total = call(
         inner_body,
@@ -383,27 +418,43 @@
         ],
         10,
     )(own, before, after, kernel, wz, wxy)
-    value = jax.ShapeDtypeStruct((outputs, slots // 2), F32)
-    sent, feature = call(
+    blocks = bricks * sects // 2
+
+    def values(number):
+        return jax.ShapeDtypeStruct((number, outputs, capacity), F32)
+
+    sent, table = call(
         outer_body,
-        [value, block(2, slots // 2, channels)],
+        [values(blocks), block(2, slots // 2, point_attr.shape[1] + channels)],
         [
             pltpu.VMEM((4, rows, 2 * span_z), BF16),
             pltpu.VMEM((4 * channels, span_z), BF16),
         ],
         12,
-    )(own, before, after, partner, cross, corner, kernel, total, pick, wz, wxy, pre, dense_last,
-      dense_first, middle)
+    )(own, before, after, partner, cross, corner, kernel, total, pick, wz, wxy, attr, first, middle,
+      last)
     got = swap(sent, "sect", sects // 2)
-    kept = call(own_body, value, [], 8)(feature, pre, dense_first, middle, dense_last)
-    value = by_source(kept, got, own_section(), 1)
-    bits = [("sect", 1 << i) for i in reversed(range(sects.bit_length() - 2))]
-    bits += [("brick", 1 << i) for i in reversed(range(bricks.bit_length() - 1))]
-    value = value.reshape((outputs, 2) + (2,) * len(bits) + (capacity,))
-    for i, (axis, step) in enumerate(bits):
-        value = trade(value, axis, step, i + 2)
-    value = value.reshape(outputs, sects, bricks, capacity)
-    return value.transpose(0, 2, 1, 3).reshape(outputs, slots)
+    kept = call(own_body, values(blocks), [], 8)(table, first, middle, last)
+    labels = [list(range(blocks)), [blocks + q for q in range(blocks)]]
+    step = blocks // 2
+    while step:
+        found = [(label, w, i) for w in range(2) for i, label in enumerate(labels[w])]
+        leaving = [f for f in found if f[0] & step]
+        staying = [f for f in found if not f[0] & step]
+        sent, kept = call(
+            make_deal_body([f[1:] for f in leaving], [f[1:] for f in staying]), [values(blocks)] * 2, [], 2
+        )(kept, got)
+        axis, distance = ("brick", step) if step < bricks else ("sect", step // bricks)
+        got = swap(sent, axis, distance)
+        labels = [[f[0] for f in staying], [f[0] for f in leaving]]
+        step //= 2
+    order = {label: (w, i) for w in range(2) for i, label in enumerate(labels[w])}
+    return call(
+        make_collect_body([order[r] for r in range(2 * blocks)], bricks, sects),
+        jax.ShapeDtypeStruct((outputs, slots), F32),
+        [pltpu.VMEM((2 * blocks, outputs, capacity), F32)],
+        2,
+    )(kept, got)
 
 
 def solution(mesh):

time: 42.6 us -> 39.2 us (0.920)
  local copies, waits for them, and re-layouts: 7.13 us -> 1.04 us
  waiting for transfers between devices: 6.4 us -> 7.48 us
  Pallas kernels: 10.4 us -> 11.4 us
  starting transfers between devices: 18 us -> 19 us
    unnamed x21 -> x2, local copies, waits for them, and re-layouts: 6.23 us -> 1.04 us
    ppermute x3 -> x4, starting transfers between devices: 10.3 us -> 13.9 us  [swap(): lax.ppermute(array, axis, [(i, i ^ step) for i in range(lax.axis_size(axi...]
    ppermute x5 -> x4, starting transfers between devices: 7.67 us -> 5.12 us  [swap_pairs(): return lax.ppermute(array, axis, pairs + [(j, i) for i, j in pairs])]
    ppermute x5 -> x4, waiting for transfers between devices: 2.33 us -> 3.4 us  [swap_pairs(): return lax.ppermute(array, axis, pairs + [(j, i) for i, j in pairs])]
    pallas_call x6 -> x9, Pallas kernels: 10.4 us -> 11.4 us  [run(): pl.pallas_call(body, out_shape=outs, in_specs=[pl.BlockSpec(memory_space=...]
    reshape x1 -> x0, local copies, waits for them, and re-layouts: 0.68 us -> none  [on_device(): return value.transpose(0, 2, 1, 3).reshape(outputs, slots)]
    ppermute x3 -> x4, waiting for transfers between devices: 4.06 us -> 4.08 us  [swap(): lax.ppermute(array, axis, [(i, i ^ step) for i in range(lax.axis_size(axi...]
  transfers between devices with their start and end apart: 8 -> 8, of which waited for: 3 -> 4; matrix products, arithmetic and copies ran while one was open for 0% -> 0% of each run, Pallas kernels for 14% -> 16%
where the time goes in v5:
time: 39.2 us; the launch traced here: 39 us
  starting transfers between devices  19 us (48%)
  Pallas kernels  11.4 us (29%)
  waiting for transfers between devices  7.48 us (19%)
  local copies, waits for them, and re-layouts  1.04 us (3%)
    ppermute x4, starting transfers between devices, swap(): lax.ppermute(array, axis, [(i, i ^ step) for i in range(lax.axis_size(axi...  13.9 us
    pallas_call x9, Pallas kernels, run(): pl.pallas_call(body, out_shape=outs, in_specs=[pl.BlockSpec(memory_space=...  11.4 us
    ppermute x4, starting transfers between devices, swap_pairs(): return lax.ppermute(array, axis, pairs + [(j, i) for i, j in pairs])  5.12 us
    ppermute x4, waiting for transfers between devices, swap(): lax.ppermute(array, axis, [(i, i ^ step) for i in range(lax.axis_size(axi...  4.08 us
    ppermute x4, waiting for transfers between devices, swap_pairs(): return lax.ppermute(array, axis, pairs + [(j, i) for i, j in pairs])  3.4 us
    unnamed x2, local copies, waits for them, and re-layouts  1.04 us
  transfers between devices with their start and end apart: 8, of which 4 were waited for; matrix products, arithmetic and copies ran while one was open for 0% of the time, Pallas kernels for 16%

profile of v5, /device:TPU:0, one launch (start us, length us, event | category | flops | bytes accessed | tf_op | source)
XLA Modules:
  0.0 39.0 jit_solution(12799510652293738301)
XLA Ops:
  0.0 1.0 %copy-done = bf16[64,4,8,128]{3,2,1,0:T(8,128)(2,1)S(1)} copy-done((bf16[64,4,8,128]{3,2,1,0:T(8,128)(2,1)S(1)}, bf16[64,4,8,128]{3,2,1,0:T(8,128)(2,1)}, u32[]{:S(2)}) %copy-start) | copy-done | bytes 524312
  1.0 0.3 shard_map.82
  1.4 3.1 %collective-permute-start = (bf16[2,8,64,128]{3,2,1,0:T(8,128)(2,1)S(1)}, bf16[2,8,64,128]{3,2,1,0:T(8,128)(2,1)S(1)}, u32[]{:S(2)}, u32[]{:S(2)}) collective-permute-start(bf16[2,8,64,128]{3,2,1,0:T(8,128)(2,1)S(1)} %get-tuple-element.28), channel_id=1, source_target_pairs={{0,4},{8,12},{4,0},{12,8},{1,5},{9,13},{5,1},{13,9},{2,6},{10,14},... | collective-permute-start | bytes 786440 | tf_op jit(solution)/shard_map/ppermute | solution.py:338
  4.5 0.7 %collective-permute-start.1 = (bf16[2,8,64,128]{3,2,1,0:T(8,128)(2,1)S(1)}, bf16[2,8,64,128]{3,2,1,0:T(8,128)(2,1)S(1)}, u32[]{:S(2)}, u32[]{:S(2)}) collective-permute-start(bf16[2,8,64,128]{3,2,1,0:T(8,128)(2,1)S(1)} %get-tuple-element.29), channel_id=1, source_target_pairs={{4,8},{8,4},{5,9},{9,5},{6,10},{10,6},{7,11},{11,7},{20,24},{24,20... | collective-permute-start | bytes 786440 | tf_op jit(solution)/shard_map/ppermute | solution.py:338
  5.1 2.2 %shard_map.83 = (bf16[320,256]{1,0:T(8,128)(2,1)S(1)}, bf16[128,256]{1,0:T(8,128)(2,1)S(1)}, f32[60,256]{1,0:T(8,128)S(1)}, bf16[128,2304]{1,0:T(8,128)(2,1)S(1)...) custom-call(f32[3,256]{1,0:T(4,128)} %place_hbm.1, ...), custom_call_target="tpu_custom_call" | custom-call | tf_op jit(solution)/shard_map/pallas_call | solution.py:32
  7.4 3.4 %collective-permute-done.even_ref = bf16[2,8,64,128]{3,2,1,0:T(8,128)(2,1)S(1)} collective-permute-done((bf16[2,8,64,128]{3,2,1,0:T(8,128)(2,1)S(1)}, bf16[2,8,64,128]{3,2,1,0:T(8,128)(2,1)S(1)}, u32[]{:S(2)}, u32[]{:S(2)}) %collective-permute-start) | collective-permute-done | bytes 262176 | tf_op jit(solution)/shard_map/ppermute | solution.py:338
  10.8 0.0 collective-permute-done.1.odd_ref
  10.8 0.1 shard_map.84
  10.9 0.1 collective-permute-start.2
  10.9 0.7 %collective-permute-start.3 = (bf16[4,2,64,128]{3,2,1,0:T(8,128)(2,1)S(1)}, bf16[4,2,64,128]{3,2,1,0:T(8,128)(2,1)S(1)}, u32[]{:S(2)}, u32[]{:S(2)}) collective-permute-start(bf16[4,2,64,128]{3,2,1,0:T(8,128)(2,1)S(1)} %get-tuple-element.34), channel_id=1, source_target_pairs={{1,2},{2,1},{5,6},{6,5},{9,10},{10,9},{13,14},{14,13},{17,18},{18,... | collective-permute-start | bytes 393224 | tf_op jit(solution)/shard_map/ppermute | solution.py:338
  11.6 0.7 %collective-permute-start.4 = (bf16[4,2,64,128]{3,2,1,0:T(8,128)(2,1)S(1)}, bf16[4,2,64,128]{3,2,1,0:T(8,128)(2,1)S(1)}, u32[]{:S(2)}, u32[]{:S(2)}) collective-permute-start(bf16[4,2,64,128]{3,2,1,0:T(8,128)(2,1)S(1)} %get-tuple-element.35), channel_id=1, source_target_pairs={{1,2},{2,1},{5,6},{6,5},{9,10},{10,9},{13,14},{14,13},{17,18},{18,... | collective-permute-start | bytes 393224 | tf_op jit(solution)/shard_map/ppermute | solution.py:338
  12.3 2.8 %shard_map.85.total_ref = f32[64,256]{1,0:T(8,128)S(1)} custom-call(bf16[4,8,64,128]{3,2,1,0:T(8,128)(2,1)S(1)} %get-tuple-element.27.own_ref, bf16[2,8,64,128]{3,2,1,0:T(8,128)(2,1)S(1)} %get-tuple-element.31.before_ref, bf16[2,8,64,128]{3,2,1,0:T(8,128)(2,1)S(1)} %get-tuple-element.32.after_ref, bf16[128,2304]{1,0:T(8,128)(2,1)S(1)} %get-tuple-element.36.kernel_ref, ...), custom_call_target="tpu_custom_call" | custom-call | tf_op jit(solution)/shard_map/pallas_call | solution.py:32
  15.1 0.0 collective-permute-done.3.cross_ref
  15.1 0.0 collective-permute-done.4.corner_ref
  15.1 0.0 collective-permute-done.2.partner_ref
  15.1 4.3 %shard_map.86 = (f32[4,4,40]{2,1,0:T(4,128)S(1)}, bf16[2,160,128]{2,1,0:T(8,128)(2,1)S(1)}) custom-call(bf16[4,8,64,128]{3,2,1,0:T(8,128)(2,1)S(1)} %get-tuple-element.27.own_ref, bf16[2,8,64,128]{3,2,1,0:T(8,128)(2,1)S(1)} %get-tuple-element.31.before_ref, bf16[2,8,64,128]{3,2,1,0:T(8,128)(2,1)S(1)} %get-tuple-element.32.after_ref, ...), custom_call_target="tpu_custom_call" | custom-call | tf_op jit(solution)/shard_map/pallas_call | solution.py:32
  19.4 6.2 %collective-permute-start.5 = (f32[4,4,40]{2,1,0:T(4,128)S(1)}, f32[4,4,40]{2,1,0:T(4,128)S(1)}, u32[]{:S(2)}, u32[]{:S(2)}) collective-permute-start(f32[4,4,40]{2,1,0:T(4,128)S(1)} %get-tuple-element.44), channel_id=1, source_target_pairs={{0,2},{2,0},{1,3},{3,1},{4,6},{6,4},{5,7},{7,5},{8,10},{10,8},{9,1... | collective-permute-start | bytes 7688 | tf_op jit(solution)/shard_map/ppermute | solution.py:333
  25.5 1.1 %shard_map.87.kept_ref = f32[4,4,40]{2,1,0:T(4,128)S(1)} custom-call(bf16[2,160,128]{2,1,0:T(8,128)(2,1)S(1)} %get-tuple-element.43.refs_0_, bf16[2,128,512]{2,1,0:T(8,128)(2,1)S(1)} %get-tuple-element.40.first_ref.refs_1_, bf16[2,3,512,512]{3,2,1,0:T(8,128)(2,1)S(1)} %get-tuple-element.41.middle_ref.refs_2_, ...), custom_call_target="tpu_custom_call" | custom-call | tf_op jit(solution)/shard_map/pallas_call | solution.py:32
  26.6 0.5 %collective-permute-done.5.got_ref = f32[4,4,40]{2,1,0:T(4,128)S(1)} collective-permute-done((f32[4,4,40]{2,1,0:T(4,128)S(1)}, f32[4,4,40]{2,1,0:T(4,128)S(1)}, u32[]{:S(2)}, u32[]{:S(2)}) %collective-permute-start.5) | collective-permute-done | bytes 2592 | tf_op jit(solution)/shard_map/ppermute | solution.py:333
  27.2 5.9 %collective-permute-start.6 = (f32[4,4,40]{2,1,0:T(4,128)S(1)}, f32[4,4,40]{2,1,0:T(4,128)S(1)}, u32[]{:S(2)}, u32[]{:S(2)}) collective-permute-start(f32[4,4,40]{2,1,0:T(4,128)S(1)} %get-tuple-element.46), channel_id=1, source_target_pairs={{0,8},{4,12},{8,0},{12,4},{1,9},{5,13},{9,1},{13,5},{2,10},{6,14},... | collective-permute-start | bytes 7688 | tf_op jit(solution)/shard_map/ppermute | solution.py:333
  33.1 1.6 %collective-permute-done.6.got_ref = f32[4,4,40]{2,1,0:T(4,128)S(1)} collective-permute-done((f32[4,4,40]{2,1,0:T(4,128)S(1)}, f32[4,4,40]{2,1,0:T(4,128)S(1)}, u32[]{:S(2)}, u32[]{:S(2)}) %collective-permute-start.6) | collective-permute-done | bytes 2592 | tf_op jit(solution)/shard_map/ppermute | solution.py:333
  34.7 1.7 %collective-permute-start.7 = (f32[4,4,40]{2,1,0:T(4,128)S(1)}, f32[4,4,40]{2,1,0:T(4,128)S(1)}, u32[]{:S(2)}, u32[]{:S(2)}) collective-permute-start(f32[4,4,40]{2,1,0:T(4,128)S(1)} %get-tuple-element.48), channel_id=1, source_target_pairs={{0,4},{4,0},{8,12},{12,8},{1,5},{5,1},{9,13},{13,9},{2,6},{6,2},{1... | collective-permute-start | bytes 7688 | tf_op jit(solution)/shard_map/ppermute | solution.py:333
  36.5 1.9 %collective-permute-done.7.got_ref = f32[4,4,40]{2,1,0:T(4,128)S(1)} collective-permute-done((f32[4,4,40]{2,1,0:T(4,128)S(1)}, f32[4,4,40]{2,1,0:T(4,128)S(1)}, u32[]{:S(2)}, u32[]{:S(2)}) %collective-permute-start.7) | collective-permute-done | bytes 2592 | tf_op jit(solution)/shard_map/ppermute | solution.py:333
  38.4 0.7 %shard_map.90 = f32[4,320]{1,0:T(4,128)} custom-call(f32[4,4,40]{2,1,0:T(4,128)S(1)} %get-tuple-element.47.kept_ref, f32[4,4,40]{2,1,0:T(4,128)S(1)} %collective-permute-done.7.got_ref), custom_call_target="tpu_custom_call" | custom-call | tf_op jit(solution)/shard_map/pallas_call | solution.py:32
  (3 shorter events, 0.0 us)
Async XLA Ops:
  0.0 1.0 %copy-start = (bf16[64,4,8,128]{3,2,1,0:T(8,128)(2,1)S(1)}, bf16[64,4,8,128]{3,2,1,0:T(8,128)(2,1)}, u32[]{:S(2)}) copy-start(bf16[64,4,8,128]{3,2,1,0:T(8,128)(2,1)} %g_ref.1) | copy-start | bytes 1572868
  1.4 9.4 %collective-permute-start = (bf16[2,8,64,128]{3,2,1,0:T(8,128)(2,1)S(1)}, bf16[2,8,64,128]{3,2,1,0:T(8,128)(2,1)S(1)}, u32[]{:S(2)}, u32[]{:S(2)}) collective-permute-start(bf16[2,8,64,128]{3,2,1,0:T(8,128)(2,1)S(1)} %get-tuple-element.28), channel_id=1, source_target_pairs={{0,4},{8,12},{4,0},{12,8},{1,5},{9,13},{5,1},{13,9},{2,6},{10,14},... | collective-permute-start | bytes 786440 | tf_op jit(solution)/shard_map/ppermute | solution.py:338
  4.5 6.3 %collective-permute-start.1 = (bf16[2,8,64,128]{3,2,1,0:T(8,128)(2,1)S(1)}, bf16[2,8,64,128]{3,2,1,0:T(8,128)(2,1)S(1)}, u32[]{:S(2)}, u32[]{:S(2)}) collective-permute-start(bf16[2,8,64,128]{3,2,1,0:T(8,128)(2,1)S(1)} %get-tuple-element.29), channel_id=1, source_target_pairs={{4,8},{8,4},{5,9},{9,5},{6,10},{10,6},{7,11},{11,7},{20,24},{24,20... | collective-permute-start | bytes 786440 | tf_op jit(solution)/shard_map/ppermute | solution.py:338
  10.9 4.2 %collective-permute-start.2 = (bf16[8,2,64,128]{3,2,1,0:T(8,128)(2,1)S(1)}, bf16[8,2,64,128]{3,2,1,0:T(8,128)(2,1)S(1)}, u32[]{:S(2)}, u32[]{:S(2)}) collective-permute-start(bf16[8,2,64,128]{3,2,1,0:T(8,128)(2,1)S(1)} %get-tuple-element.33), channel_id=1, source_target_pairs={{0,1},{1,0},{2,3},{3,2},{4,5},{5,4},{6,7},{7,6},{8,9},{9,8},{10,11... | collective-permute-start | bytes 786440 | tf_op jit(solution)/shard_map/ppermute | solution.py:333
  10.9 4.1 %collective-permute-start.3 = (bf16[4,2,64,128]{3,2,1,0:T(8,128)(2,1)S(1)}, bf16[4,2,64,128]{3,2,1,0:T(8,128)(2,1)S(1)}, u32[]{:S(2)}, u32[]{:S(2)}) collective-permute-start(bf16[4,2,64,128]{3,2,1,0:T(8,128)(2,1)S(1)} %get-tuple-element.34), channel_id=1, source_target_pairs={{1,2},{2,1},{5,6},{6,5},{9,10},{10,9},{13,14},{14,13},{17,18},{18,... | collective-permute-start | bytes 393224 | tf_op jit(solution)/shard_map/ppermute | solution.py:338
  11.6 3.5 %collective-permute-start.4 = (bf16[4,2,64,128]{3,2,1,0:T(8,128)(2,1)S(1)}, bf16[4,2,64,128]{3,2,1,0:T(8,128)(2,1)S(1)}, u32[]{:S(2)}, u32[]{:S(2)}) collective-permute-start(bf16[4,2,64,128]{3,2,1,0:T(8,128)(2,1)S(1)} %get-tuple-element.35), channel_id=1, source_target_pairs={{1,2},{2,1},{5,6},{6,5},{9,10},{10,9},{13,14},{14,13},{17,18},{18,... | collective-permute-start | bytes 393224 | tf_op jit(solution)/shard_map/ppermute | solution.py:338
  19.4 7.8 %collective-permute-start.5 = (f32[4,4,40]{2,1,0:T(4,128)S(1)}, f32[4,4,40]{2,1,0:T(4,128)S(1)}, u32[]{:S(2)}, u32[]{:S(2)}) collective-permute-start(f32[4,4,40]{2,1,0:T(4,128)S(1)} %get-tuple-element.44), channel_id=1, source_target_pairs={{0,2},{2,0},{1,3},{3,1},{4,6},{6,4},{5,7},{7,5},{8,10},{10,8},{9,1... | collective-permute-start | bytes 7688 | tf_op jit(solution)/shard_map/ppermute | solution.py:333
  27.2 7.6 %collective-permute-start.6 = (f32[4,4,40]{2,1,0:T(4,128)S(1)}, f32[4,4,40]{2,1,0:T(4,128)S(1)}, u32[]{:S(2)}, u32[]{:S(2)}) collective-permute-start(f32[4,4,40]{2,1,0:T(4,128)S(1)} %get-tuple-element.46), channel_id=1, source_target_pairs={{0,8},{4,12},{8,0},{12,4},{1,9},{5,13},{9,1},{13,5},{2,10},{6,14},... | collective-permute-start | bytes 7688 | tf_op jit(solution)/shard_map/ppermute | solution.py:333
  34.7 3.7 %collective-permute-start.7 = (f32[4,4,40]{2,1,0:T(4,128)S(1)}, f32[4,4,40]{2,1,0:T(4,128)S(1)}, u32[]{:S(2)}, u32[]{:S(2)}) collective-permute-start(f32[4,4,40]{2,1,0:T(4,128)S(1)} %get-tuple-element.48), channel_id=1, source_target_pairs={{0,4},{4,0},{8,12},{12,8},{1,5},{5,1},{9,13},{13,9},{2,6},{6,2},{1... | collective-permute-start | bytes 7688 | tf_op jit(solution)/shard_map/ppermute | solution.py:333

commit v6 on v5

--- a/solution.py
+++ b/solution.py
@@ -1,5 +1,6 @@
 import jax
 import jax.numpy as jnp
+import numpy as np
 from jax import lax
 from jax.experimental import pallas as pl
 from jax.experimental.pallas import tpu as pltpu
@@ -64,8 +65,12 @@
 
         @pl.when(lax.axis_index("brick") % 2 == side)
         def _(before=(odd_ref, even_ref)[side], after=(even_ref, odd_ref)[side]):
-            before_ref[...] = before[...]
-            after_ref[...] = after[...]
+            brick = lax.axis_index("brick")
+            outside = jnp.zeros(before_ref.shape, F32)
+            inside = before[...].astype(F32)
+            before_ref[...] = jnp.where(brick > 0, inside, outside).astype(BF16)
+            inside = after[...].astype(F32)
+            after_ref[...] = jnp.where(brick < lax.axis_size("brick") - 1, inside, outside).astype(BF16)
 
     for slab in range(2):
 
@@ -230,12 +235,15 @@
     span_x, span_y, channels, span_z = own_ref.shape
     group = 3 * channels
     left_chip = lax.axis_index("slab") == 0
+    line = lax.axis_index(("sect", "slab"))
+    inside = (line > 0) & (line < lax.axis_size(("sect", "slab")) - 1)
 
     def put(x):
         ref, at = layer_of(own_ref, before_ref, after_ref, x)
         far, near = layer_of(cross_ref, corner_ref, corner_ref.at[HALO:], x)
         for j in range(2):
             cross, partner = far[near, j].astype(F32), partner_ref[x, j].astype(F32)
+            cross = jnp.where(inside, cross, 0.0)
             left = jnp.where(left_chip, cross, partner).astype(BF16)
             right = jnp.where(left_chip, partner, cross).astype(BF16)
             for side, column, tile in (
@@ -333,9 +341,23 @@
     return lax.ppermute(array, axis, [(i, i ^ step) for i in range(lax.axis_size(axis))])
 
 
-def swap_pairs(array, axis, start):
-    pairs = [(i, i + 1) for i in range(start, lax.axis_size(axis) - 1, 2)]
-    return lax.ppermute(array, axis, pairs + [(j, i) for i, j in pairs])
+def swap_pairs(array, axes, start, fill):
+    everything = ("case", "brick", "sect", "slab")
+    sizes = [lax.axis_size(a) for a in everything]
+    pairs = []
+    for i, at in enumerate(np.ndindex(*sizes)):
+        at = dict(zip(everything, at))
+        place, size = 0, 1
+        for a in axes:
+            place, size = place * lax.axis_size(a) + at[a], size * lax.axis_size(a)
+        other = place + 1 if (place - start) % 2 == 0 else place - 1
+        if 0 <= other < size:
+            for a in reversed(axes):
+                other, at[a] = divmod(other, lax.axis_size(a))
+        else:
+            at[fill] ^= 1
+        pairs.append((i, int(np.ravel_multi_index([at[a] for a in everything], sizes))))
+    return lax.ppermute(array, everything, pairs)
 
 
 def on_device(
@@ -370,9 +392,9 @@
         [],
         8,
     )(geometry)
-    even = swap_pairs(even, "brick", 0)
-    odd = swap_pairs(odd, "brick", 1)
-    cross = swap_pairs(facing, lines, 1)
+    even = swap_pairs(even, ("brick",), 0, "slab")
+    odd = swap_pairs(odd, ("brick",), 1, "slab")
+    cross = swap_pairs(facing, lines, 1, "case")
     pick, wz, wxy, kernel, attr, first, middle, last = call(
         make_points_body(span_x, span_y, bricks, sects, capacity),
         [
@@ -407,7 +429,7 @@
         4,
     )(own, even, odd, wxy)
     partner = swap(to_partner, "slab", 1)
-    corner = swap_pairs(to_cross, lines, 1)
+    corner = swap_pairs(to_cross, lines, 1, "case")
     rows = (span_x + 2 * HALO) * 3 * channels
     total = call(
         inner_body,

time: 39.2 us -> 35.6 us (0.908)
  starting transfers between devices: 19 us -> 11.7 us
  waiting for transfers between devices: 7.48 us -> 11.2 us
    ppermute x4, starting transfers between devices: 13.9 us -> 6.49 us  [swap(): lax.ppermute(array, axis, [(i, i ^ step) for i in range(lax.axis_size(axi...]
    ppermute x4, waiting for transfers between devices: 3.4 us -> 5.92 us  [swap_pairs(): return lax.ppermute(array, everything, pairs)]
    ppermute x4, waiting for transfers between devices: 4.08 us -> 5.31 us  [swap(): lax.ppermute(array, axis, [(i, i ^ step) for i in range(lax.axis_size(axi...]
  transfers between devices with their start and end apart: 8 -> 8, of which waited for: 4 -> 6; matrix products, arithmetic and copies ran while one was open for 0% -> 0% of each run, Pallas kernels for 16% -> 17%
where the time goes in v6:
time: 35.6 us; the launch traced here: 35.5 us
  starting transfers between devices  11.7 us (33%)
  Pallas kernels  11.5 us (32%)
  waiting for transfers between devices  11.2 us (31%)
  local copies, waits for them, and re-layouts  1.04 us (3%)
    pallas_call x9, Pallas kernels, run(): pl.pallas_call(body, out_shape=outs, in_specs=[pl.BlockSpec(memory_space=...  11.5 us
    ppermute x4, starting transfers between devices, swap(): lax.ppermute(array, axis, [(i, i ^ step) for i in range(lax.axis_size(axi...  6.49 us
    ppermute x4, waiting for transfers between devices, swap_pairs(): return lax.ppermute(array, everything, pairs)  5.92 us
    ppermute x4, waiting for transfers between devices, swap(): lax.ppermute(array, axis, [(i, i ^ step) for i in range(lax.axis_size(axi...  5.31 us
    ppermute x4, starting transfers between devices, swap_pairs(): return lax.ppermute(array, everything, pairs)  5.21 us
    unnamed x2, local copies, waits for them, and re-layouts  1.04 us
  transfers between devices with their start and end apart: 8, of which 6 were waited for; matrix products, arithmetic and copies ran while one was open for 0% of the time, Pallas kernels for 17%

profile of v6, /device:TPU:0, one launch (start us, length us, event | category | flops | bytes accessed | tf_op | source)
XLA Modules:
  0.0 35.5 jit_solution(10195650275713653311)
XLA Ops:
  0.0 1.0 %copy-done = bf16[64,4,8,128]{3,2,1,0:T(8,128)(2,1)S(1)} copy-done((bf16[64,4,8,128]{3,2,1,0:T(8,128)(2,1)S(1)}, bf16[64,4,8,128]{3,2,1,0:T(8,128)(2,1)}, u32[]{:S(2)}) %copy-start) | copy-done | bytes 524312
  1.0 0.3 shard_map.82
  1.4 3.1 %collective-permute-start = (bf16[2,8,64,128]{3,2,1,0:T(8,128)(2,1)S(1)}, bf16[2,8,64,128]{3,2,1,0:T(8,128)(2,1)S(1)}, u32[]{:S(2)}, u32[]{:S(2)}) collective-permute-start(bf16[2,8,64,128]{3,2,1,0:T(8,128)(2,1)S(1)} %get-tuple-element.28), channel_id=1, source_target_pairs={{0,4},{1,5},{2,6},{3,7},{4,0},{5,1},{6,2},{7,3},{8,12},{9,13},{10,... | collective-permute-start | bytes 786440 | tf_op jit(solution)/shard_map/ppermute | solution.py:360
  4.5 0.0 collective-permute-start.1
  4.5 2.2 %shard_map.83 = (bf16[320,256]{1,0:T(8,128)(2,1)S(1)}, bf16[128,256]{1,0:T(8,128)(2,1)S(1)}, f32[60,256]{1,0:T(8,128)S(1)}, bf16[128,2304]{1,0:T(8,128)(2,1)S(1)...) custom-call(f32[3,256]{1,0:T(4,128)} %place_hbm.1, ...), custom_call_target="tpu_custom_call" | custom-call | tf_op jit(solution)/shard_map/pallas_call | solution.py:33
  6.7 4.1 %collective-permute-done.even_ref = bf16[2,8,64,128]{3,2,1,0:T(8,128)(2,1)S(1)} collective-permute-done((bf16[2,8,64,128]{3,2,1,0:T(8,128)(2,1)S(1)}, bf16[2,8,64,128]{3,2,1,0:T(8,128)(2,1)S(1)}, u32[]{:S(2)}, u32[]{:S(2)}) %collective-permute-start) | collective-permute-done | bytes 262176 | tf_op jit(solution)/shard_map/ppermute | solution.py:360
  10.8 0.0 collective-permute-done.1.odd_ref
  10.8 0.1 shard_map.84
  10.9 0.1 collective-permute-start.2
  11.0 1.7 %collective-permute-start.3 = (bf16[4,2,64,128]{3,2,1,0:T(8,128)(2,1)S(1)}, bf16[4,2,64,128]{3,2,1,0:T(8,128)(2,1)S(1)}, u32[]{:S(2)}, u32[]{:S(2)}) collective-permute-start(bf16[4,2,64,128]{3,2,1,0:T(8,128)(2,1)S(1)} %get-tuple-element.34), channel_id=1, source_target_pairs={{0,16},{1,2},{2,1},{3,19},{4,20},{5,6},{6,5},{7,23},{8,24},{9,10},... | collective-permute-start | bytes 393224 | tf_op jit(solution)/shard_map/ppermute | solution.py:360
  12.7 0.3 collective-permute-start.4
  13.1 2.8 %shard_map.85.total_ref = f32[64,256]{1,0:T(8,128)S(1)} custom-call(bf16[4,8,64,128]{3,2,1,0:T(8,128)(2,1)S(1)} %get-tuple-element.27.own_ref, bf16[2,8,64,128]{3,2,1,0:T(8,128)(2,1)S(1)} %get-tuple-element.31.before_ref, bf16[2,8,64,128]{3,2,1,0:T(8,128)(2,1)S(1)} %get-tuple-element.32.after_ref, bf16[128,2304]{1,0:T(8,128)(2,1)S(1)} %get-tuple-element.36.kernel_ref, ...), custom_call_target="tpu_custom_call" | custom-call | tf_op jit(solution)/shard_map/pallas_call | solution.py:33
  15.9 0.2 collective-permute-done.3.cross_ref
  16.0 1.7 %collective-permute-done.4.corner_ref = bf16[4,2,64,128]{3,2,1,0:T(8,128)(2,1)S(1)} collective-permute-done((bf16[4,2,64,128]{3,2,1,0:T(8,128)(2,1)S(1)}, bf16[4,2,64,128]{3,2,1,0:T(8,128)(2,1)S(1)}, u32[]{:S(2)}, u32[]{:S(2)}) %collective-permute-start.4) | collective-permute-done | bytes 131104 | tf_op jit(solution)/shard_map/ppermute | solution.py:360
  17.7 0.0 collective-permute-done.2.partner_ref
  17.7 4.3 %shard_map.86 = (f32[4,4,40]{2,1,0:T(4,128)S(1)}, bf16[2,160,128]{2,1,0:T(8,128)(2,1)S(1)}) custom-call(bf16[4,8,64,128]{3,2,1,0:T(8,128)(2,1)S(1)} %get-tuple-element.27.own_ref, bf16[2,8,64,128]{3,2,1,0:T(8,128)(2,1)S(1)} %get-tuple-element.31.before_ref, bf16[2,8,64,128]{3,2,1,0:T(8,128)(2,1)S(1)} %get-tuple-element.32.after_ref, ...), custom_call_target="tpu_custom_call" | custom-call | tf_op jit(solution)/shard_map/pallas_call | solution.py:33
  22.0 0.8 %collective-permute-start.5 = (f32[4,4,40]{2,1,0:T(4,128)S(1)}, f32[4,4,40]{2,1,0:T(4,128)S(1)}, u32[]{:S(2)}, u32[]{:S(2)}) collective-permute-start(f32[4,4,40]{2,1,0:T(4,128)S(1)} %get-tuple-element.44), channel_id=1, source_target_pairs={{0,2},{2,0},{1,3},{3,1},{4,6},{6,4},{5,7},{7,5},{8,10},{10,8},{9,1... | collective-permute-start | bytes 7688 | tf_op jit(solution)/shard_map/ppermute | solution.py:341
  22.8 1.1 %shard_map.87.kept_ref = f32[4,4,40]{2,1,0:T(4,128)S(1)} custom-call(bf16[2,160,128]{2,1,0:T(8,128)(2,1)S(1)} %get-tuple-element.43.refs_0_, bf16[2,128,512]{2,1,0:T(8,128)(2,1)S(1)} %get-tuple-element.40.first_ref.refs_1_, bf16[2,3,512,512]{3,2,1,0:T(8,128)(2,1)S(1)} %get-tuple-element.41.middle_ref.refs_2_, ...), custom_call_target="tpu_custom_call" | custom-call | tf_op jit(solution)/shard_map/pallas_call | solution.py:33
  23.9 1.8 %collective-permute-done.5.got_ref = f32[4,4,40]{2,1,0:T(4,128)S(1)} collective-permute-done((f32[4,4,40]{2,1,0:T(4,128)S(1)}, f32[4,4,40]{2,1,0:T(4,128)S(1)}, u32[]{:S(2)}, u32[]{:S(2)}) %collective-permute-start.5) | collective-permute-done | bytes 2592 | tf_op jit(solution)/shard_map/ppermute | solution.py:341
  25.6 3.9 %collective-permute-start.6 = (f32[4,4,40]{2,1,0:T(4,128)S(1)}, f32[4,4,40]{2,1,0:T(4,128)S(1)}, u32[]{:S(2)}, u32[]{:S(2)}) collective-permute-start(f32[4,4,40]{2,1,0:T(4,128)S(1)} %get-tuple-element.46), channel_id=1, source_target_pairs={{0,8},{4,12},{8,0},{12,4},{1,9},{5,13},{9,1},{13,5},{2,10},{6,14},... | collective-permute-start | bytes 7688 | tf_op jit(solution)/shard_map/ppermute | solution.py:341
  29.5 1.6 %collective-permute-done.6.got_ref = f32[4,4,40]{2,1,0:T(4,128)S(1)} collective-permute-done((f32[4,4,40]{2,1,0:T(4,128)S(1)}, f32[4,4,40]{2,1,0:T(4,128)S(1)}, u32[]{:S(2)}, u32[]{:S(2)}) %collective-permute-start.6) | collective-permute-done | bytes 2592 | tf_op jit(solution)/shard_map/ppermute | solution.py:341
  31.2 1.7 %collective-permute-start.7 = (f32[4,4,40]{2,1,0:T(4,128)S(1)}, f32[4,4,40]{2,1,0:T(4,128)S(1)}, u32[]{:S(2)}, u32[]{:S(2)}) collective-permute-start(f32[4,4,40]{2,1,0:T(4,128)S(1)} %get-tuple-element.48), channel_id=1, source_target_pairs={{0,4},{4,0},{8,12},{12,8},{1,5},{5,1},{9,13},{13,9},{2,6},{6,2},{1... | collective-permute-start | bytes 7688 | tf_op jit(solution)/shard_map/ppermute | solution.py:341
  32.9 1.9 %collective-permute-done.7.got_ref = f32[4,4,40]{2,1,0:T(4,128)S(1)} collective-permute-done((f32[4,4,40]{2,1,0:T(4,128)S(1)}, f32[4,4,40]{2,1,0:T(4,128)S(1)}, u32[]{:S(2)}, u32[]{:S(2)}) %collective-permute-start.7) | collective-permute-done | bytes 2592 | tf_op jit(solution)/shard_map/ppermute | solution.py:341
  34.8 0.7 %shard_map.90 = f32[4,320]{1,0:T(4,128)} custom-call(f32[4,4,40]{2,1,0:T(4,128)S(1)} %get-tuple-element.47.kept_ref, f32[4,4,40]{2,1,0:T(4,128)S(1)} %collective-permute-done.7.got_ref), custom_call_target="tpu_custom_call" | custom-call | tf_op jit(solution)/shard_map/pallas_call | solution.py:33
  (3 shorter events, 0.0 us)
Async XLA Ops:
  0.0 1.0 %copy-start = (bf16[64,4,8,128]{3,2,1,0:T(8,128)(2,1)S(1)}, bf16[64,4,8,128]{3,2,1,0:T(8,128)(2,1)}, u32[]{:S(2)}) copy-start(bf16[64,4,8,128]{3,2,1,0:T(8,128)(2,1)} %g_ref.1) | copy-start | bytes 1572868
  1.4 9.4 %collective-permute-start = (bf16[2,8,64,128]{3,2,1,0:T(8,128)(2,1)S(1)}, bf16[2,8,64,128]{3,2,1,0:T(8,128)(2,1)S(1)}, u32[]{:S(2)}, u32[]{:S(2)}) collective-permute-start(bf16[2,8,64,128]{3,2,1,0:T(8,128)(2,1)S(1)} %get-tuple-element.28), channel_id=1, source_target_pairs={{0,4},{1,5},{2,6},{3,7},{4,0},{5,1},{6,2},{7,3},{8,12},{9,13},{10,... | collective-permute-start | bytes 786440 | tf_op jit(solution)/shard_map/ppermute | solution.py:360
  4.5 6.3 %collective-permute-start.1 = (bf16[2,8,64,128]{3,2,1,0:T(8,128)(2,1)S(1)}, bf16[2,8,64,128]{3,2,1,0:T(8,128)(2,1)S(1)}, u32[]{:S(2)}, u32[]{:S(2)}) collective-permute-start(bf16[2,8,64,128]{3,2,1,0:T(8,128)(2,1)S(1)} %get-tuple-element.29), channel_id=1, source_target_pairs={{0,1},{1,0},{2,3},{3,2},{4,8},{5,9},{6,10},{7,11},{8,4},{9,5},{10,... | collective-permute-start | bytes 786440 | tf_op jit(solution)/shard_map/ppermute | solution.py:360
  10.9 6.8 %collective-permute-start.2 = (bf16[8,2,64,128]{3,2,1,0:T(8,128)(2,1)S(1)}, bf16[8,2,64,128]{3,2,1,0:T(8,128)(2,1)S(1)}, u32[]{:S(2)}, u32[]{:S(2)}) collective-permute-start(bf16[8,2,64,128]{3,2,1,0:T(8,128)(2,1)S(1)} %get-tuple-element.33), channel_id=1, source_target_pairs={{0,1},{1,0},{2,3},{3,2},{4,5},{5,4},{6,7},{7,6},{8,9},{9,8},{10,11... | collective-permute-start | bytes 786440 | tf_op jit(solution)/shard_map/ppermute | solution.py:341
  11.0 5.0 %collective-permute-start.3 = (bf16[4,2,64,128]{3,2,1,0:T(8,128)(2,1)S(1)}, bf16[4,2,64,128]{3,2,1,0:T(8,128)(2,1)S(1)}, u32[]{:S(2)}, u32[]{:S(2)}) collective-permute-start(bf16[4,2,64,128]{3,2,1,0:T(8,128)(2,1)S(1)} %get-tuple-element.34), channel_id=1, source_target_pairs={{0,16},{1,2},{2,1},{3,19},{4,20},{5,6},{6,5},{7,23},{8,24},{9,10},... | collective-permute-start | bytes 393224 | tf_op jit(solution)/shard_map/ppermute | solution.py:360
  12.7 5.0 %collective-permute-start.4 = (bf16[4,2,64,128]{3,2,1,0:T(8,128)(2,1)S(1)}, bf16[4,2,64,128]{3,2,1,0:T(8,128)(2,1)S(1)}, u32[]{:S(2)}, u32[]{:S(2)}) collective-permute-start(bf16[4,2,64,128]{3,2,1,0:T(8,128)(2,1)S(1)} %get-tuple-element.35), channel_id=1, source_target_pairs={{0,16},{1,2},{2,1},{3,19},{4,20},{5,6},{6,5},{7,23},{8,24},{9,10},... | collective-permute-start | bytes 393224 | tf_op jit(solution)/shard_map/ppermute | solution.py:360
  22.0 3.7 %collective-permute-start.5 = (f32[4,4,40]{2,1,0:T(4,128)S(1)}, f32[4,4,40]{2,1,0:T(4,128)S(1)}, u32[]{:S(2)}, u32[]{:S(2)}) collective-permute-start(f32[4,4,40]{2,1,0:T(4,128)S(1)} %get-tuple-element.44), channel_id=1, source_target_pairs={{0,2},{2,0},{1,3},{3,1},{4,6},{6,4},{5,7},{7,5},{8,10},{10,8},{9,1... | collective-permute-start | bytes 7688 | tf_op jit(solution)/shard_map/ppermute | solution.py:341
  25.6 5.5 %collective-permute-start.6 = (f32[4,4,40]{2,1,0:T(4,128)S(1)}, f32[4,4,40]{2,1,0:T(4,128)S(1)}, u32[]{:S(2)}, u32[]{:S(2)}) collective-permute-start(f32[4,4,40]{2,1,0:T(4,128)S(1)} %get-tuple-element.46), channel_id=1, source_target_pairs={{0,8},{4,12},{8,0},{12,4},{1,9},{5,13},{9,1},{13,5},{2,10},{6,14},... | collective-permute-start | bytes 7688 | tf_op jit(solution)/shard_map/ppermute | solution.py:341
  31.2 3.7 %collective-permute-start.7 = (f32[4,4,40]{2,1,0:T(4,128)S(1)}, f32[4,4,40]{2,1,0:T(4,128)S(1)}, u32[]{:S(2)}, u32[]{:S(2)}) collective-permute-start(f32[4,4,40]{2,1,0:T(4,128)S(1)} %get-tuple-element.48), channel_id=1, source_target_pairs={{0,4},{4,0},{8,12},{12,8},{1,5},{5,1},{9,13},{13,9},{2,6},{6,2},{1... | collective-permute-start | bytes 7688 | tf_op jit(solution)/shard_map/ppermute | solution.py:341

commit v7 on v6

--- a/solution.py
+++ b/solution.py
@@ -156,126 +156,130 @@
     return body
 
 
-def shifted_tiles(tile):
+def taps(tile, inside=True):
     span_z = tile.shape[1]
-    lane = iota(tile.shape, 1)
-    wide = tile.astype(F32)
-    lower = jnp.where(lane == 0, 0.0, pltpu.roll(wide, 1, 1)).astype(BF16)
-    upper = jnp.where(lane == span_z - 1, 0.0, pltpu.roll(wide, span_z - 1, 1)).astype(BF16)
-    return lower, tile, upper
-
-
-def layer_of(own_ref, before_ref, after_ref, x):
-    span_x = own_ref.shape[0]
-    if x < HALO:
-        return before_ref, x
-    if x >= HALO + span_x:
-        return after_ref, x - HALO - span_x
-    return own_ref, x - HALO
-
-
-def inner_body(
-    own_ref, before_ref, after_ref, kernel_ref, wz_ref, wxy_ref, total_ref, shifted, latent
-):
-    span_x, span_y, channels, span_z = own_ref.shape
-    group, pairs, step = 3 * channels, (span_y - 2) // 2, 2
-
-    def put(x):
-        ref, at = layer_of(own_ref, before_ref, after_ref, x)
-        for y in range(span_y):
-            for e, piece in enumerate(shifted_tiles(ref[at, y])):
-                base = x * group + e * channels
-                shifted[base : base + channels, y * span_z : (y + 1) * span_z] = piece
-
-    def lanes(y):
-        return slice(y * span_z, (y + 1) * span_z)
-
-    put(0)
-    put(1)
-    total = jnp.zeros(total_ref.shape, F32)
-    for x in range(0, span_x + 2, step):
-        layers = range(x, x + step)
-        for k in layers:
-            put(k + 2)
+    lane = iota((1, span_z), 1)
+    below, here, above = (
+        jnp.where(keep & inside, 1.0, 0.0).astype(BF16)
+        for keep in (lane > 0, lane >= 0, lane < span_z - 1)
+    )
+    pieces = (pltpu.roll(tile, 1, 1) * below, tile * here, pltpu.roll(tile, span_z - 1, 1) * above)
+    return jnp.concatenate(pieces, axis=0)
+
+
+def share(total, units, tap, weight, kernel_ref, wz_ref, wxy_ref):
+    channels, span_z = total.shape[0], wz_ref.shape[0]
+    for first in range(0, len(units), 4):
+        pair = units[first : first + 4]
         wide = jnp.concatenate(
             [
-                jnp.concatenate(
-                    [shifted[k * group : (k + 3) * group, lanes(2 * p + c)] for k in layers for p in range(pairs)],
-                    axis=1,
-                )
+                jnp.concatenate([tap(x + a, y + c) for x, y in pair], axis=1)
                 for c in range(4)
+                for a in range(3)
             ],
             axis=0,
         )
         part = jnp.dot(kernel_ref[...], wide, preferred_element_type=F32)
-        for k in layers:
-            ref, at = layer_of(own_ref, before_ref, after_ref, k + 1)
-            for y in range(2 * pairs):
-                response = part[
-                    (y % 2) * channels : (y % 2 + 1) * channels, lanes((k - x) * pairs + y // 2)
-                ]
-                base = ((k - x) * 2 * pairs + y) * channels
-                latent[base : base + channels, :] = (
-                    ref[at, y + 1].astype(F32) + gelu(response)
-                ).astype(BF16)
-        sampled = jnp.dot(latent[...], wz_ref[...], preferred_element_type=F32)
-        for k in layers:
-            for y in range(2 * pairs):
-                row = k * (span_y + 2) + y + 2
-                base = ((k - x) * 2 * pairs + y) * channels
-                total += sampled[base : base + channels] * wxy_ref[row : row + 1, :]
-    total_ref[...] = total
+        tiles, weights = [], []
+        for j in range(2):
+            centre = jnp.concatenate(
+                [tap(x + 1, y + j + 1)[channels : 2 * channels] for x, y in pair], axis=1
+            )
+            response = part[j * channels : (j + 1) * channels]
+            latent = (centre.astype(F32) + gelu(response)).astype(BF16)
+            for u, (x, y) in enumerate(pair):
+                tiles.append(latent[:, u * span_z : (u + 1) * span_z])
+                weights.append(weight(x, y + j))
+        sampled = jnp.dot(
+            jnp.concatenate(tiles, axis=0), wz_ref[...], preferred_element_type=F32
+        )
+        for k, w in enumerate(weights):
+            total += sampled[k * channels : (k + 1) * channels] * wxy_ref[pl.ds(w, 1), :]
+    return total
+
+
+def inner_units(layers, span_y):
+    return [(x, y) for x in layers for y in range(HALO, span_y, 2)]
+
+
+def block_body(own_ref, kernel_ref, wz_ref, wxy_ref, taps_ref, total_ref):
+    span_x, span_y = own_ref.shape[:2]
+    for x in range(span_x):
+        for y in range(span_y):
+            taps_ref[x, y] = taps(own_ref[x, y])
+    total_ref[...] = share(
+        jnp.zeros(total_ref.shape, F32),
+        inner_units(range(HALO, span_x), span_y),
+        lambda x, y: taps_ref[x - HALO, y - HALO],
+        lambda x, y: x * (span_y + 2) + y,
+        kernel_ref, wz_ref, wxy_ref,
+    )
+
+
+def tap_of(own_ref, halo_ref, x):
+    span_x = own_ref.shape[0]
+    if HALO <= x < HALO + span_x:
+        return own_ref.at[x - HALO]
+    return halo_ref.at[x if x < HALO else x - span_x]
+
+
+def inner_body(
+    own_ref, before_ref, after_ref, kernel_ref, wz_ref, wxy_ref, start_ref, halo_ref, total_ref
+):
+    span_x, span_y = own_ref.shape[:2]
+    for x in range(HALO):
+        for y in range(span_y):
+            halo_ref[x, y] = taps(before_ref[x, y])
+            halo_ref[HALO + x, y] = taps(after_ref[x, y])
+    total_ref[...] = share(
+        start_ref[...],
+        inner_units([*range(HALO), *range(span_x, span_x + 2)], span_y),
+        lambda x, y: tap_of(own_ref, halo_ref, x)[y - HALO],
+        lambda x, y: x * (span_y + 2) + y,
+        kernel_ref, wz_ref, wxy_ref,
+    )
+
+
+def side_share(total, on_left, inside, halo_tile, own_ref, halo_ref, side_ref, kernel_ref, wz_ref, wxy_ref):
+    span_x, span_y = own_ref.shape[:2]
+    near = jnp.where(on_left, 0, span_y - HALO)
+    for x in range(side_ref.shape[0]):
+        layer = tap_of(own_ref, halo_ref, x)
+        for j in range(HALO):
+            side_ref[x, jnp.where(on_left, HALO, 0) + j] = layer[near + j]
+            side_ref[x, jnp.where(on_left, 0, HALO) + j] = taps(halo_tile(x, j), inside)
+    base = jnp.where(on_left, 0, span_y)
+    return share(
+        total,
+        [(x, 0) for x in range(span_x + 2)],
+        lambda x, y: side_ref[x, y],
+        lambda x, y: x * (span_y + 2) + base + y,
+        kernel_ref, wz_ref, wxy_ref,
+    )
+
+
+def partner_body(
+    own_ref, halo_ref, partner_ref, kernel_ref, wz_ref, wxy_ref, start_ref, total_ref, side_ref
+):
+    total_ref[...] = side_share(
+        start_ref[...], lax.axis_index("slab") == 1, True, lambda x, j: partner_ref[x, j],
+        own_ref, halo_ref, side_ref, kernel_ref, wz_ref, wxy_ref,
+    )
 
 
 def outer_body(
-    own_ref, before_ref, after_ref, partner_ref, cross_ref, corner_ref, kernel_ref, total_ref,
-    pick_ref, wz_ref, wxy_ref, attr_ref, first_ref, middle_ref, last_ref,
-    value_ref, row_ref, shifted, latent,
+    own_ref, halo_ref, cross_ref, corner_ref, kernel_ref, wz_ref, wxy_ref, start_ref,
+    pick_ref, attr_ref, first_ref, middle_ref, last_ref,
+    value_ref, row_ref, side_ref,
 ):
-    span_x, span_y, channels, span_z = own_ref.shape
-    group = 3 * channels
-    left_chip = lax.axis_index("slab") == 0
     line = lax.axis_index(("sect", "slab"))
-    inside = (line > 0) & (line < lax.axis_size(("sect", "slab")) - 1)
-
-    def put(x):
-        ref, at = layer_of(own_ref, before_ref, after_ref, x)
-        far, near = layer_of(cross_ref, corner_ref, corner_ref.at[HALO:], x)
-        for j in range(2):
-            cross, partner = far[near, j].astype(F32), partner_ref[x, j].astype(F32)
-            cross = jnp.where(inside, cross, 0.0)
-            left = jnp.where(left_chip, cross, partner).astype(BF16)
-            right = jnp.where(left_chip, partner, cross).astype(BF16)
-            for side, column, tile in (
-                (0, j, left),
-                (0, j + HALO, ref[at, j]),
-                (1, j, ref[at, span_y - HALO + j]),
-                (1, j + HALO, right),
-            ):
-                for e, piece in enumerate(shifted_tiles(tile)):
-                    rows = slice(x * group + e * channels, x * group + (e + 1) * channels)
-                    shifted[column, rows, side * span_z : (side + 1) * span_z] = piece
-
-    put(0)
-    put(1)
-    total = total_ref[...]
-    for x in range(span_x + 2):
-        put(x + 2)
-        wide = jnp.concatenate([shifted[c, x * group : (x + 3) * group, :] for c in range(4)], axis=0)
-        part = jnp.dot(kernel_ref[...], wide, preferred_element_type=F32)
-        middle = slice((x + 1) * group + channels, (x + 1) * group + 2 * channels)
-        for y in range(2):
-            response = part[y * channels : (y + 1) * channels]
-            tiles = (shifted[y + 1, middle, :].astype(F32) + gelu(response)).astype(BF16)
-            for side in range(2):
-                base = (side * 2 + y) * channels
-                latent[base : base + channels, :] = tiles[:, side * span_z : (side + 1) * span_z]
-        sampled = jnp.dot(latent[...], wz_ref[...], preferred_element_type=F32)
-        for side in range(2):
-            for y in range(2):
-                base = (side * 2 + y) * channels
-                row = x * (span_y + 2) + side * span_y + y
-                total += sampled[base : base + channels] * wxy_ref[row : row + 1, :]
+    total = side_share(
+        start_ref[...],
+        lax.axis_index("slab") == 0,
+        (line > 0) & (line < lax.axis_size(("sect", "slab")) - 1),
+        lambda x, j: tap_of(cross_ref, corner_ref, x)[j],
+        own_ref, halo_ref, side_ref, kernel_ref, wz_ref, wxy_ref,
+    )
     table = jnp.concatenate([total.astype(BF16), attr_ref[...]], axis=0)
     row = lax.dot_general(
         pick_ref[...], table, (((1,), (1,)), ((), ())), preferred_element_type=F32
@@ -417,6 +421,10 @@
         n_hbm=7,
     )(point_place, destination.reshape(1, count), conv_kernels[0], point_attr.T, dense_first,
       dense_middle, dense_last)
+    features = jax.ShapeDtypeStruct((channels, count), F32)
+    own_taps, total = call(
+        block_body, [block(span_x, span_y, 3 * channels, span_z), features], [], 8
+    )(own, kernel, wz, wxy)
     before, after, to_partner, to_cross = call(
         edges_body,
         [
@@ -427,34 +435,24 @@
         ],
         [],
         4,
-    )(own, even, odd, wxy)
+    )(own, even, odd, total)
     partner = swap(to_partner, "slab", 1)
     corner = swap_pairs(to_cross, lines, 1, "case")
-    rows = (span_x + 2 * HALO) * 3 * channels
-    total = call(
-        inner_body,
-        jax.ShapeDtypeStruct((channels, count), F32),
-        [
-            pltpu.VMEM((rows, span_y * span_z), BF16),
-            pltpu.VMEM((2 * (span_y - 2) * channels, span_z), BF16),
-        ],
-        10,
-    )(own, before, after, kernel, wz, wxy)
+    halo_taps, total = call(
+        inner_body, [block(2 * HALO, span_y, 3 * channels, span_z), features], [], 8
+    )(own_taps, before, after, kernel, wz, wxy, total)
+    side = pltpu.VMEM((span_x + 2 * HALO, 2 * HALO, 3 * channels, span_z), BF16)
+    total = call(partner_body, features, [side], 8)(
+        own_taps, halo_taps, partner, kernel, wz, wxy, total
+    )
     blocks = bricks * sects // 2
 
     def values(number):
         return jax.ShapeDtypeStruct((number, outputs, capacity), F32)
 
     sent, table = call(
-        outer_body,
-        [values(blocks), block(2, slots // 2, point_attr.shape[1] + channels)],
-        [
-            pltpu.VMEM((4, rows, 2 * span_z), BF16),
-            pltpu.VMEM((4 * channels, span_z), BF16),
-        ],
-        12,
-    )(own, before, after, partner, cross, corner, kernel, total, pick, wz, wxy, attr, first, middle,
-      last)
+        outer_body, [values(blocks), block(2, slots // 2, point_attr.shape[1] + channels)], [side], 8
+    )(own_taps, halo_taps, cross, corner, kernel, wz, wxy, total, pick, attr, first, middle, last)
     got = swap(sent, "sect", sects // 2)
     kept = call(own_body, values(blocks), [], 8)(table, first, middle, last)
     labels = [list(range(blocks)), [blocks + q for q in range(blocks)]]

time: 35.6 us -> 34 us (0.955)
  waiting for transfers between devices: 11.2 us -> 9.77 us
    ppermute x4, waiting for transfers between devices: 5.92 us -> 4.46 us  [swap_pairs(): return lax.ppermute(array, everything, pairs)]
    pallas_call x9 -> x11, Pallas kernels: 11.5 us -> 11.2 us  [run(): pl.pallas_call(body, out_shape=outs, in_specs=[pl.BlockSpec(memory_space=...]
  transfers between devices with their start and end apart: 8 -> 8, of which waited for: 6 -> 5; matrix products, arithmetic and copies ran while one was open for 0% -> 0% of each run, Pallas kernels for 17% -> 22%
where the time goes in v7:
time: 34 us; the launch traced here: 33.8 us
  starting transfers between devices  11.7 us (34%)
  Pallas kernels  11.2 us (33%)
  waiting for transfers between devices  9.77 us (29%)
  local copies, waits for them, and re-layouts  1.04 us (3%)
    pallas_call x11, Pallas kernels, run(): pl.pallas_call(body, out_shape=outs, in_specs=[pl.BlockSpec(memory_space=...  11.2 us
    ppermute x4, starting transfers between devices, swap(): lax.ppermute(array, axis, [(i, i ^ step) for i in range(lax.axis_size(axi...  6.48 us
    ppermute x4, waiting for transfers between devices, swap(): lax.ppermute(array, axis, [(i, i ^ step) for i in range(lax.axis_size(axi...  5.31 us
    ppermute x4, starting transfers between devices, swap_pairs(): return lax.ppermute(array, everything, pairs)  5.21 us
    ppermute x4, waiting for transfers between devices, swap_pairs(): return lax.ppermute(array, everything, pairs)  4.46 us
    unnamed x2, local copies, waits for them, and re-layouts  1.04 us
  transfers between devices with their start and end apart: 8, of which 5 were waited for; matrix products, arithmetic and copies ran while one was open for 0% of the time, Pallas kernels for 22%

profile of v7, /device:TPU:0, one launch (start us, length us, event | category | flops | bytes accessed | tf_op | source)
XLA Modules:
  0.0 33.8 jit_solution(8434689947918906669)
XLA Ops:
  0.0 1.0 %copy-done = bf16[64,4,8,128]{3,2,1,0:T(8,128)(2,1)S(1)} copy-done((bf16[64,4,8,128]{3,2,1,0:T(8,128)(2,1)S(1)}, bf16[64,4,8,128]{3,2,1,0:T(8,128)(2,1)}, u32[]{:S(2)}) %copy-start) | copy-done | bytes 524312
  1.0 0.3 shard_map.82
  1.4 3.1 %collective-permute-start = (bf16[2,8,64,128]{3,2,1,0:T(8,128)(2,1)S(1)}, bf16[2,8,64,128]{3,2,1,0:T(8,128)(2,1)S(1)}, u32[]{:S(2)}, u32[]{:S(2)}) collective-permute-start(bf16[2,8,64,128]{3,2,1,0:T(8,128)(2,1)S(1)} %get-tuple-element.36), channel_id=1, source_target_pairs={{0,4},{1,5},{2,6},{3,7},{4,0},{5,1},{6,2},{7,3},{8,12},{9,13},{10,... | collective-permute-start | bytes 786440 | tf_op jit(solution)/shard_map/ppermute | solution.py:364
  4.5 0.0 collective-permute-start.1
  4.5 2.2 %shard_map.83 = (bf16[320,256]{1,0:T(8,128)(2,1)S(1)}, bf16[128,256]{1,0:T(8,128)(2,1)S(1)}, f32[60,256]{1,0:T(8,128)S(1)}, bf16[128,2304]{1,0:T(8,128)(2,1)S(1)...) custom-call(f32[3,256]{1,0:T(4,128)} %place_hbm.1, ...), custom_call_target="tpu_custom_call" | custom-call | tf_op jit(solution)/shard_map/pallas_call | solution.py:33
  6.7 1.1 %shard_map.84 = (bf16[4,8,192,128]{3,2,1,0:T(8,128)(2,1)S(1)}, f32[64,256]{1,0:T(8,128)S(1)}) custom-call(bf16[4,8,64,128]{3,2,1,0:T(8,128)(2,1)S(1)} %get-tuple-element.31.own_ref, bf16[128,2304]{1,0:T(8,128)(2,1)S(1)} %get-tuple-element.32.kernel_ref, bf16[128,256]{1,0:T(8,128)(2,1)S(1)} %get-tuple-element.33.wz_ref, f32[60,256]{1,0:T(8,128)S(1)} %get-tuple-element.34.wxy_ref), custom_call_target="tpu_custom_call" | custom-call | tf_op jit(solution)/shard_map/pallas_call | solution.py:33
  7.8 3.0 %collective-permute-done.even_ref = bf16[2,8,64,128]{3,2,1,0:T(8,128)(2,1)S(1)} collective-permute-done((bf16[2,8,64,128]{3,2,1,0:T(8,128)(2,1)S(1)}, bf16[2,8,64,128]{3,2,1,0:T(8,128)(2,1)S(1)}, u32[]{:S(2)}, u32[]{:S(2)}) %collective-permute-start) | collective-permute-done | bytes 262176 | tf_op jit(solution)/shard_map/ppermute | solution.py:364
  10.8 0.0 collective-permute-done.1.odd_ref
  10.8 0.1 shard_map.85
  10.9 0.1 collective-permute-start.4
  11.0 1.7 %collective-permute-start.2 = (bf16[4,2,64,128]{3,2,1,0:T(8,128)(2,1)S(1)}, bf16[4,2,64,128]{3,2,1,0:T(8,128)(2,1)S(1)}, u32[]{:S(2)}, u32[]{:S(2)}) collective-permute-start(bf16[4,2,64,128]{3,2,1,0:T(8,128)(2,1)S(1)} %get-tuple-element.42), channel_id=1, source_target_pairs={{0,16},{1,2},{2,1},{3,19},{4,20},{5,6},{6,5},{7,23},{8,24},{9,10},... | collective-permute-start | bytes 393224 | tf_op jit(solution)/shard_map/ppermute | solution.py:364
  12.7 0.3 %collective-permute-start.3 = (bf16[4,2,64,128]{3,2,1,0:T(8,128)(2,1)S(1)}, bf16[4,2,64,128]{3,2,1,0:T(8,128)(2,1)S(1)}, u32[]{:S(2)}, u32[]{:S(2)}) collective-permute-start(bf16[4,2,64,128]{3,2,1,0:T(8,128)(2,1)S(1)} %get-tuple-element.43), channel_id=1, source_target_pairs={{0,16},{1,2},{2,1},{3,19},{4,20},{5,6},{6,5},{7,23},{8,24},{9,10},... | collective-permute-start | bytes 393224 | tf_op jit(solution)/shard_map/ppermute | solution.py:364
  13.1 1.8 %shard_map.86 = (bf16[4,8,192,128]{3,2,1,0:T(8,128)(2,1)S(1)}, f32[64,256]{1,0:T(8,128)S(1)}) custom-call(bf16[4,8,192,128]{3,2,1,0:T(8,128)(2,1)S(1)} %get-tuple-element.35.own_ref, bf16[2,8,64,128]{3,2,1,0:T(8,128)(2,1)S(1)} %get-tuple-element.39.before_ref, bf16[2,8,64,128]{3,2,1,0:T(8,128)(2,1)S(1)} %get-tuple-element.40.after_ref, ...), custom_call_target="tpu_custom_call" | custom-call | tf_op jit(solution)/shard_map/pallas_call | solution.py:33
  14.9 1.3 %shard_map.87.start_ref = f32[64,256]{1,0:T(8,128)S(1)} custom-call(bf16[4,8,192,128]{3,2,1,0:T(8,128)(2,1)S(1)} %get-tuple-element.35.own_ref, bf16[4,8,192,128]{3,2,1,0:T(8,128)(2,1)S(1)} %get-tuple-element.41.halo_ref, bf16[8,2,64,128]{3,2,1,0:T(8,128)(2,1)S(1)} %collective-permute-done.4.partner_ref, bf16[128,2304]{1,0:T(8,128)(2,1)S(1)} %get-tuple-element.32.kernel_ref, ...), custom_call_target="tpu_custom_call" | custom-call | tf_op jit(solution)/shard_map/pallas_call | solution.py:33
  16.3 1.5 %collective-permute-done.3.corner_ref = bf16[4,2,64,128]{3,2,1,0:T(8,128)(2,1)S(1)} collective-permute-done((bf16[4,2,64,128]{3,2,1,0:T(8,128)(2,1)S(1)}, bf16[4,2,64,128]{3,2,1,0:T(8,128)(2,1)S(1)}, u32[]{:S(2)}, u32[]{:S(2)}) %collective-permute-start.3) | collective-permute-done | bytes 131104 | tf_op jit(solution)/shard_map/ppermute | solution.py:364
  17.7 2.6 %shard_map.88 = (f32[4,4,40]{2,1,0:T(4,128)S(1)}, bf16[2,160,128]{2,1,0:T(8,128)(2,1)S(1)}) custom-call(bf16[4,8,192,128]{3,2,1,0:T(8,128)(2,1)S(1)} %get-tuple-element.35.own_ref, bf16[4,8,192,128]{3,2,1,0:T(8,128)(2,1)S(1)} %get-tuple-element.41.halo_ref, bf16[4,2,64,128]{3,2,1,0:T(8,128)(2,1)S(1)} %collective-permute-done.2.cross_ref, ...), custom_call_target="tpu_custom_call" | custom-call | tf_op jit(solution)/shard_map/pallas_call | solution.py:33
  20.3 0.8 %collective-permute-start.5 = (f32[4,4,40]{2,1,0:T(4,128)S(1)}, f32[4,4,40]{2,1,0:T(4,128)S(1)}, u32[]{:S(2)}, u32[]{:S(2)}) collective-permute-start(f32[4,4,40]{2,1,0:T(4,128)S(1)} %get-tuple-element.52), channel_id=1, source_target_pairs={{0,2},{2,0},{1,3},{3,1},{4,6},{6,4},{5,7},{7,5},{8,10},{10,8},{9,1... | collective-permute-start | bytes 7688 | tf_op jit(solution)/shard_map/ppermute | solution.py:345
  21.1 1.1 %shard_map.89.kept_ref = f32[4,4,40]{2,1,0:T(4,128)S(1)} custom-call(bf16[2,160,128]{2,1,0:T(8,128)(2,1)S(1)} %get-tuple-element.51.refs_0_, bf16[2,128,512]{2,1,0:T(8,128)(2,1)S(1)} %get-tuple-element.48.first_ref.refs_1_, bf16[2,3,512,512]{3,2,1,0:T(8,128)(2,1)S(1)} %get-tuple-element.49.middle_ref.refs_2_, ...), custom_call_target="tpu_custom_call" | custom-call | tf_op jit(solution)/shard_map/pallas_call | solution.py:33
  22.2 1.8 %collective-permute-done.5.got_ref = f32[4,4,40]{2,1,0:T(4,128)S(1)} collective-permute-done((f32[4,4,40]{2,1,0:T(4,128)S(1)}, f32[4,4,40]{2,1,0:T(4,128)S(1)}, u32[]{:S(2)}, u32[]{:S(2)}) %collective-permute-start.5) | collective-permute-done | bytes 2592 | tf_op jit(solution)/shard_map/ppermute | solution.py:345
  24.0 3.9 %collective-permute-start.6 = (f32[4,4,40]{2,1,0:T(4,128)S(1)}, f32[4,4,40]{2,1,0:T(4,128)S(1)}, u32[]{:S(2)}, u32[]{:S(2)}) collective-permute-start(f32[4,4,40]{2,1,0:T(4,128)S(1)} %get-tuple-element.54), channel_id=1, source_target_pairs={{0,8},{4,12},{8,0},{12,4},{1,9},{5,13},{9,1},{13,5},{2,10},{6,14},... | collective-permute-start | bytes 7688 | tf_op jit(solution)/shard_map/ppermute | solution.py:345
  27.8 1.6 %collective-permute-done.6.got_ref = f32[4,4,40]{2,1,0:T(4,128)S(1)} collective-permute-done((f32[4,4,40]{2,1,0:T(4,128)S(1)}, f32[4,4,40]{2,1,0:T(4,128)S(1)}, u32[]{:S(2)}, u32[]{:S(2)}) %collective-permute-start.6) | collective-permute-done | bytes 2592 | tf_op jit(solution)/shard_map/ppermute | solution.py:345
  29.5 1.8 %collective-permute-start.7 = (f32[4,4,40]{2,1,0:T(4,128)S(1)}, f32[4,4,40]{2,1,0:T(4,128)S(1)}, u32[]{:S(2)}, u32[]{:S(2)}) collective-permute-start(f32[4,4,40]{2,1,0:T(4,128)S(1)} %get-tuple-element.56), channel_id=1, source_target_pairs={{0,4},{4,0},{8,12},{12,8},{1,5},{5,1},{9,13},{13,9},{2,6},{6,2},{1... | collective-permute-start | bytes 7688 | tf_op jit(solution)/shard_map/ppermute | solution.py:345
  31.2 1.9 %collective-permute-done.7.got_ref = f32[4,4,40]{2,1,0:T(4,128)S(1)} collective-permute-done((f32[4,4,40]{2,1,0:T(4,128)S(1)}, f32[4,4,40]{2,1,0:T(4,128)S(1)}, u32[]{:S(2)}, u32[]{:S(2)}) %collective-permute-start.7) | collective-permute-done | bytes 2592 | tf_op jit(solution)/shard_map/ppermute | solution.py:345
  33.1 0.7 %shard_map.92 = f32[4,320]{1,0:T(4,128)} custom-call(f32[4,4,40]{2,1,0:T(4,128)S(1)} %get-tuple-element.55.kept_ref, f32[4,4,40]{2,1,0:T(4,128)S(1)} %collective-permute-done.7.got_ref), custom_call_target="tpu_custom_call" | custom-call | tf_op jit(solution)/shard_map/pallas_call | solution.py:33
  (5 shorter events, 0.0 us)
Async XLA Ops:
  0.0 1.0 %copy-start = (bf16[64,4,8,128]{3,2,1,0:T(8,128)(2,1)S(1)}, bf16[64,4,8,128]{3,2,1,0:T(8,128)(2,1)}, u32[]{:S(2)}) copy-start(bf16[64,4,8,128]{3,2,1,0:T(8,128)(2,1)} %g_ref.1) | copy-start | bytes 1572868
  1.4 9.4 %collective-permute-start = (bf16[2,8,64,128]{3,2,1,0:T(8,128)(2,1)S(1)}, bf16[2,8,64,128]{3,2,1,0:T(8,128)(2,1)S(1)}, u32[]{:S(2)}, u32[]{:S(2)}) collective-permute-start(bf16[2,8,64,128]{3,2,1,0:T(8,128)(2,1)S(1)} %get-tuple-element.36), channel_id=1, source_target_pairs={{0,4},{1,5},{2,6},{3,7},{4,0},{5,1},{6,2},{7,3},{8,12},{9,13},{10,... | collective-permute-start | bytes 786440 | tf_op jit(solution)/shard_map/ppermute | solution.py:364
  4.5 6.3 %collective-permute-start.1 = (bf16[2,8,64,128]{3,2,1,0:T(8,128)(2,1)S(1)}, bf16[2,8,64,128]{3,2,1,0:T(8,128)(2,1)S(1)}, u32[]{:S(2)}, u32[]{:S(2)}) collective-permute-start(bf16[2,8,64,128]{3,2,1,0:T(8,128)(2,1)S(1)} %get-tuple-element.37), channel_id=1, source_target_pairs={{0,1},{1,0},{2,3},{3,2},{4,8},{5,9},{6,10},{7,11},{8,4},{9,5},{10,... | collective-permute-start | bytes 786440 | tf_op jit(solution)/shard_map/ppermute | solution.py:364
  10.9 4.0 %collective-permute-start.4 = (bf16[8,2,64,128]{3,2,1,0:T(8,128)(2,1)S(1)}, bf16[8,2,64,128]{3,2,1,0:T(8,128)(2,1)S(1)}, u32[]{:S(2)}, u32[]{:S(2)}) collective-permute-start(bf16[8,2,64,128]{3,2,1,0:T(8,128)(2,1)S(1)} %get-tuple-element.44), channel_id=1, source_target_pairs={{0,1},{1,0},{2,3},{3,2},{4,5},{5,4},{6,7},{7,6},{8,9},{9,8},{10,11... | collective-permute-start | bytes 786440 | tf_op jit(solution)/shard_map/ppermute | solution.py:345
  11.0 5.3 %collective-permute-start.2 = (bf16[4,2,64,128]{3,2,1,0:T(8,128)(2,1)S(1)}, bf16[4,2,64,128]{3,2,1,0:T(8,128)(2,1)S(1)}, u32[]{:S(2)}, u32[]{:S(2)}) collective-permute-start(bf16[4,2,64,128]{3,2,1,0:T(8,128)(2,1)S(1)} %get-tuple-element.42), channel_id=1, source_target_pairs={{0,16},{1,2},{2,1},{3,19},{4,20},{5,6},{6,5},{7,23},{8,24},{9,10},... | collective-permute-start | bytes 393224 | tf_op jit(solution)/shard_map/ppermute | solution.py:364
  12.7 5.0 %collective-permute-start.3 = (bf16[4,2,64,128]{3,2,1,0:T(8,128)(2,1)S(1)}, bf16[4,2,64,128]{3,2,1,0:T(8,128)(2,1)S(1)}, u32[]{:S(2)}, u32[]{:S(2)}) collective-permute-start(bf16[4,2,64,128]{3,2,1,0:T(8,128)(2,1)S(1)} %get-tuple-element.43), channel_id=1, source_target_pairs={{0,16},{1,2},{2,1},{3,19},{4,20},{5,6},{6,5},{7,23},{8,24},{9,10},... | collective-permute-start | bytes 393224 | tf_op jit(solution)/shard_map/ppermute | solution.py:364
  20.3 3.7 %collective-permute-start.5 = (f32[4,4,40]{2,1,0:T(4,128)S(1)}, f32[4,4,40]{2,1,0:T(4,128)S(1)}, u32[]{:S(2)}, u32[]{:S(2)}) collective-permute-start(f32[4,4,40]{2,1,0:T(4,128)S(1)} %get-tuple-element.52), channel_id=1, source_target_pairs={{0,2},{2,0},{1,3},{3,1},{4,6},{6,4},{5,7},{7,5},{8,10},{10,8},{9,1... | collective-permute-start | bytes 7688 | tf_op jit(solution)/shard_map/ppermute | solution.py:345
  24.0 5.5 %collective-permute-start.6 = (f32[4,4,40]{2,1,0:T(4,128)S(1)}, f32[4,4,40]{2,1,0:T(4,128)S(1)}, u32[]{:S(2)}, u32[]{:S(2)}) collective-permute-start(f32[4,4,40]{2,1,0:T(4,128)S(1)} %get-tuple-element.54), channel_id=1, source_target_pairs={{0,8},{4,12},{8,0},{12,4},{1,9},{5,13},{9,1},{13,5},{2,10},{6,14},... | collective-permute-start | bytes 7688 | tf_op jit(solution)/shard_map/ppermute | solution.py:345
  29.5 3.7 %collective-permute-start.7 = (f32[4,4,40]{2,1,0:T(4,128)S(1)}, f32[4,4,40]{2,1,0:T(4,128)S(1)}, u32[]{:S(2)}, u32[]{:S(2)}) collective-permute-start(f32[4,4,40]{2,1,0:T(4,128)S(1)} %get-tuple-element.56), channel_id=1, source_target_pairs={{0,4},{4,0},{8,12},{12,8},{1,5},{5,1},{9,13},{13,9},{2,6},{6,2},{1... | collective-permute-start | bytes 7688 | tf_op jit(solution)/shard_map/ppermute | solution.py:345

commit v8 on v7

--- a/solution.py
+++ b/solution.py
@@ -167,13 +167,13 @@
     return jnp.concatenate(pieces, axis=0)
 
 
-def share(total, units, tap, weight, kernel_ref, wz_ref, wxy_ref):
+def share(total, units, kernel_ref, wz_ref, wxy_ref):
     channels, span_z = total.shape[0], wz_ref.shape[0]
     for first in range(0, len(units), 4):
-        pair = units[first : first + 4]
+        group = units[first : first + 4]
         wide = jnp.concatenate(
             [
-                jnp.concatenate([tap(x + a, y + c) for x, y in pair], axis=1)
+                jnp.concatenate([tap(x + a, c) for tap, _, x in group], axis=1)
                 for c in range(4)
                 for a in range(3)
             ],
@@ -183,23 +183,31 @@
         tiles, weights = [], []
         for j in range(2):
             centre = jnp.concatenate(
-                [tap(x + 1, y + j + 1)[channels : 2 * channels] for x, y in pair], axis=1
+                [tap(x + 1, j + 1)[channels : 2 * channels] for tap, _, x in group], axis=1
             )
             response = part[j * channels : (j + 1) * channels]
             latent = (centre.astype(F32) + gelu(response)).astype(BF16)
-            for u, (x, y) in enumerate(pair):
+            for u, (_, row, x) in enumerate(group):
                 tiles.append(latent[:, u * span_z : (u + 1) * span_z])
-                weights.append(weight(x, y + j))
+                weights.append(wxy_ref[pl.ds(row(x) + j, 1), :])
         sampled = jnp.dot(
             jnp.concatenate(tiles, axis=0), wz_ref[...], preferred_element_type=F32
         )
         for k, w in enumerate(weights):
-            total += sampled[k * channels : (k + 1) * channels] * wxy_ref[pl.ds(w, 1), :]
+            total += sampled[k * channels : (k + 1) * channels] * w
     return total
 
 
-def inner_units(layers, span_y):
-    return [(x, y) for x in layers for y in range(HALO, span_y, 2)]
+def inner_units(layers, span_y, layer_taps):
+    return [
+        (
+            lambda x, c, y=y: layer_taps(x)[y - HALO + c],
+            lambda x, y=y: x * (span_y + 2) + y,
+            x,
+        )
+        for x in layers
+        for y in range(HALO, span_y, 2)
+    ]
 
 
 def block_body(own_ref, kernel_ref, wz_ref, wxy_ref, taps_ref, total_ref):
@@ -207,16 +215,12 @@
     for x in range(span_x):
         for y in range(span_y):
             taps_ref[x, y] = taps(own_ref[x, y])
-    total_ref[...] = share(
-        jnp.zeros(total_ref.shape, F32),
-        inner_units(range(HALO, span_x), span_y),
-        lambda x, y: taps_ref[x - HALO, y - HALO],
-        lambda x, y: x * (span_y + 2) + y,
-        kernel_ref, wz_ref, wxy_ref,
-    )
-
-
-def tap_of(own_ref, halo_ref, x):
+    units = inner_units(range(HALO, span_x), span_y, lambda x: taps_ref.at[x - HALO])
+    total = jnp.zeros(total_ref.shape, F32)
+    total_ref[...] = share(total, units, kernel_ref, wz_ref, wxy_ref)
+
+
+def layer_of(own_ref, halo_ref, x):
     span_x = own_ref.shape[0]
     if HALO <= x < HALO + span_x:
         return own_ref.at[x - HALO]
@@ -231,55 +235,53 @@
         for y in range(span_y):
             halo_ref[x, y] = taps(before_ref[x, y])
             halo_ref[HALO + x, y] = taps(after_ref[x, y])
-    total_ref[...] = share(
-        start_ref[...],
-        inner_units([*range(HALO), *range(span_x, span_x + 2)], span_y),
-        lambda x, y: tap_of(own_ref, halo_ref, x)[y - HALO],
-        lambda x, y: x * (span_y + 2) + y,
-        kernel_ref, wz_ref, wxy_ref,
-    )
-
-
-def side_share(total, on_left, inside, halo_tile, own_ref, halo_ref, side_ref, kernel_ref, wz_ref, wxy_ref):
-    span_x, span_y = own_ref.shape[:2]
+    layers = [*range(HALO), *range(span_x, span_x + 2)]
+    units = inner_units(layers, span_y, lambda x: layer_of(own_ref, halo_ref, x))
+    total_ref[...] = share(start_ref[...], units, kernel_ref, wz_ref, wxy_ref)
+
+
+def side_units(on_left, inside, layers, halo_tile, own_ref, halo_ref, side_ref):
+    _, span_y = own_ref.shape[:2]
     near = jnp.where(on_left, 0, span_y - HALO)
-    for x in range(side_ref.shape[0]):
-        layer = tap_of(own_ref, halo_ref, x)
+    for x in sorted({x + a for x in layers for a in range(3)}):
         for j in range(HALO):
-            side_ref[x, jnp.where(on_left, HALO, 0) + j] = layer[near + j]
-            side_ref[x, jnp.where(on_left, 0, HALO) + j] = taps(halo_tile(x, j), inside)
+            side_ref[x, jnp.where(on_left, HALO, 0) + j] = layer_of(own_ref, halo_ref, x)[near + j]
+            side_ref[x, jnp.where(on_left, 0, HALO) + j] = taps(halo_tile(x)[j], inside)
     base = jnp.where(on_left, 0, span_y)
-    return share(
-        total,
-        [(x, 0) for x in range(span_x + 2)],
-        lambda x, y: side_ref[x, y],
-        lambda x, y: x * (span_y + 2) + base + y,
-        kernel_ref, wz_ref, wxy_ref,
-    )
-
-
-def partner_body(
-    own_ref, halo_ref, partner_ref, kernel_ref, wz_ref, wxy_ref, start_ref, total_ref, side_ref
+    return [(lambda x, c: side_ref[x, c], lambda x: x * (span_y + 2) + base, x) for x in layers]
+
+
+def cross_units(layers, cross_ref, corner_ref, own_ref, halo_ref, side_ref):
+    line = lax.axis_index(("sect", "slab"))
+    inside = (line > 0) & (line < lax.axis_size(("sect", "slab")) - 1)
+    return side_units(
+        lax.axis_index("slab") == 0, inside, layers, lambda x: layer_of(cross_ref, corner_ref, x),
+        own_ref, halo_ref, side_ref,
+    )
+
+
+def beside_body(
+    own_ref, halo_ref, partner_ref, cross_ref, kernel_ref, wz_ref, wxy_ref, start_ref,
+    total_ref, partner_side, cross_side,
 ):
-    total_ref[...] = side_share(
-        start_ref[...], lax.axis_index("slab") == 1, True, lambda x, j: partner_ref[x, j],
-        own_ref, halo_ref, side_ref, kernel_ref, wz_ref, wxy_ref,
-    )
+    span_x = own_ref.shape[0]
+    units = side_units(
+        lax.axis_index("slab") == 1, True, range(span_x + 2), lambda x: partner_ref.at[x],
+        own_ref, halo_ref, partner_side,
+    )
+    units += cross_units(range(HALO, span_x), cross_ref, None, own_ref, halo_ref, cross_side)
+    total_ref[...] = share(start_ref[...], units, kernel_ref, wz_ref, wxy_ref)
 
 
 def outer_body(
     own_ref, halo_ref, cross_ref, corner_ref, kernel_ref, wz_ref, wxy_ref, start_ref,
     pick_ref, attr_ref, first_ref, middle_ref, last_ref,
-    value_ref, row_ref, side_ref,
+    value_ref, row_ref, cross_side,
 ):
-    line = lax.axis_index(("sect", "slab"))
-    total = side_share(
-        start_ref[...],
-        lax.axis_index("slab") == 0,
-        (line > 0) & (line < lax.axis_size(("sect", "slab")) - 1),
-        lambda x, j: tap_of(cross_ref, corner_ref, x)[j],
-        own_ref, halo_ref, side_ref, kernel_ref, wz_ref, wxy_ref,
-    )
+    span_x = own_ref.shape[0]
+    layers = [*range(HALO), *range(span_x, span_x + 2)]
+    units = cross_units(layers, cross_ref, corner_ref, own_ref, halo_ref, cross_side)
+    total = share(start_ref[...], units, kernel_ref, wz_ref, wxy_ref)
     table = jnp.concatenate([total.astype(BF16), attr_ref[...]], axis=0)
     row = lax.dot_general(
         pick_ref[...], table, (((1,), (1,)), ((), ())), preferred_element_type=F32
@@ -442,9 +444,7 @@
         inner_body, [block(2 * HALO, span_y, 3 * channels, span_z), features], [], 8
     )(own_taps, before, after, kernel, wz, wxy, total)
     side = pltpu.VMEM((span_x + 2 * HALO, 2 * HALO, 3 * channels, span_z), BF16)
-    total = call(partner_body, features, [side], 8)(
-        own_taps, halo_taps, partner, kernel, wz, wxy, total
-    )
+    total = call(beside_body, features, [side, side], 10)(own_taps, halo_taps, partner, cross, kernel, wz, wxy, total)
     blocks = bricks * sects // 2
 
     def values(number):

time: 34 us -> 33.8 us (level)
  waiting for transfers between devices: 9.77 us -> 9.2 us
  starting transfers between devices: 11.7 us -> 12.1 us
    ppermute x4, starting transfers between devices: 6.48 us -> 6.89 us  [swap(): lax.ppermute(array, axis, [(i, i ^ step) for i in range(lax.axis_size(axi...]
  transfers between devices with their start and end apart: 8 -> 8, of which waited for: 5 -> 5; matrix products, arithmetic and copies ran while one was open for 0% -> 0% of each run, Pallas kernels for 22% -> 23%
where the time goes in v8:
time: 33.8 us; the launch traced here: 33.6 us
  starting transfers between devices  12.1 us (36%)
  Pallas kernels  11.2 us (33%)
  waiting for transfers between devices  9.2 us (27%)
  local copies, waits for them, and re-layouts  1.04 us (3%)
    pallas_call x11, Pallas kernels, run(): pl.pallas_call(body, out_shape=outs, in_specs=[pl.BlockSpec(memory_space=...  11.2 us
    ppermute x4, starting transfers between devices, swap(): lax.ppermute(array, axis, [(i, i ^ step) for i in range(lax.axis_size(axi...  6.89 us
    ppermute x4, starting transfers between devices, swap_pairs(): return lax.ppermute(array, everything, pairs)  5.21 us
    ppermute x4, waiting for transfers between devices, swap(): lax.ppermute(array, axis, [(i, i ^ step) for i in range(lax.axis_size(axi...  5.06 us
    ppermute x4, waiting for transfers between devices, swap_pairs(): return lax.ppermute(array, everything, pairs)  4.14 us
    unnamed x2, local copies, waits for them, and re-layouts  1.04 us
  transfers between devices with their start and end apart: 8, of which 5 were waited for; matrix products, arithmetic and copies ran while one was open for 0% of the time, Pallas kernels for 23%

profile of v8, /device:TPU:0, one launch (start us, length us, event | category | flops | bytes accessed | tf_op | source)
XLA Modules:
  0.0 33.6 jit_solution(15370859897071741059)
XLA Ops:
  0.0 1.0 %copy-done = bf16[64,4,8,128]{3,2,1,0:T(8,128)(2,1)S(1)} copy-done((bf16[64,4,8,128]{3,2,1,0:T(8,128)(2,1)S(1)}, bf16[64,4,8,128]{3,2,1,0:T(8,128)(2,1)}, u32[]{:S(2)}) %copy-start) | copy-done | bytes 524312
  1.0 0.3 shard_map.82
  1.4 3.1 %collective-permute-start = (bf16[2,8,64,128]{3,2,1,0:T(8,128)(2,1)S(1)}, bf16[2,8,64,128]{3,2,1,0:T(8,128)(2,1)S(1)}, u32[]{:S(2)}, u32[]{:S(2)}) collective-permute-start(bf16[2,8,64,128]{3,2,1,0:T(8,128)(2,1)S(1)} %get-tuple-element.36), channel_id=1, source_target_pairs={{0,4},{1,5},{2,6},{3,7},{4,0},{5,1},{6,2},{7,3},{8,12},{9,13},{10,... | collective-permute-start | bytes 786440 | tf_op jit(solution)/shard_map/ppermute | solution.py:366
  4.5 0.0 collective-permute-start.1
  4.5 2.2 %shard_map.83 = (bf16[320,256]{1,0:T(8,128)(2,1)S(1)}, bf16[128,256]{1,0:T(8,128)(2,1)S(1)}, f32[60,256]{1,0:T(8,128)S(1)}, bf16[128,2304]{1,0:T(8,128)(2,1)S(1)...) custom-call(f32[3,256]{1,0:T(4,128)} %place_hbm.1, ...), custom_call_target="tpu_custom_call" | custom-call | tf_op jit(solution)/shard_map/pallas_call | solution.py:33
  6.7 1.1 %shard_map.84 = (bf16[4,8,192,128]{3,2,1,0:T(8,128)(2,1)S(1)}, f32[64,256]{1,0:T(8,128)S(1)}) custom-call(bf16[4,8,64,128]{3,2,1,0:T(8,128)(2,1)S(1)} %get-tuple-element.31.own_ref, bf16[128,2304]{1,0:T(8,128)(2,1)S(1)} %get-tuple-element.32.kernel_ref, bf16[128,256]{1,0:T(8,128)(2,1)S(1)} %get-tuple-element.33.wz_ref, f32[60,256]{1,0:T(8,128)S(1)} %get-tuple-element.34.wxy_ref), custom_call_target="tpu_custom_call" | custom-call | tf_op jit(solution)/shard_map/pallas_call | solution.py:33
  7.8 3.0 %collective-permute-done.even_ref = bf16[2,8,64,128]{3,2,1,0:T(8,128)(2,1)S(1)} collective-permute-done((bf16[2,8,64,128]{3,2,1,0:T(8,128)(2,1)S(1)}, bf16[2,8,64,128]{3,2,1,0:T(8,128)(2,1)S(1)}, u32[]{:S(2)}, u32[]{:S(2)}) %collective-permute-start) | collective-permute-done | bytes 262176 | tf_op jit(solution)/shard_map/ppermute | solution.py:366
  10.8 0.1 shard_map.85
  10.9 0.1 collective-permute-start.4
  11.0 1.7 %collective-permute-start.2 = (bf16[4,2,64,128]{3,2,1,0:T(8,128)(2,1)S(1)}, bf16[4,2,64,128]{3,2,1,0:T(8,128)(2,1)S(1)}, u32[]{:S(2)}, u32[]{:S(2)}) collective-permute-start(bf16[4,2,64,128]{3,2,1,0:T(8,128)(2,1)S(1)} %get-tuple-element.42), channel_id=1, source_target_pairs={{0,16},{1,2},{2,1},{3,19},{4,20},{5,6},{6,5},{7,23},{8,24},{9,10},... | collective-permute-start | bytes 393224 | tf_op jit(solution)/shard_map/ppermute | solution.py:366
  12.7 0.3 %collective-permute-start.3 = (bf16[4,2,64,128]{3,2,1,0:T(8,128)(2,1)S(1)}, bf16[4,2,64,128]{3,2,1,0:T(8,128)(2,1)S(1)}, u32[]{:S(2)}, u32[]{:S(2)}) collective-permute-start(bf16[4,2,64,128]{3,2,1,0:T(8,128)(2,1)S(1)} %get-tuple-element.43), channel_id=1, source_target_pairs={{0,16},{1,2},{2,1},{3,19},{4,20},{5,6},{6,5},{7,23},{8,24},{9,10},... | collective-permute-start | bytes 393224 | tf_op jit(solution)/shard_map/ppermute | solution.py:366
  13.1 1.8 %shard_map.86 = (bf16[4,8,192,128]{3,2,1,0:T(8,128)(2,1)S(1)}, f32[64,256]{1,0:T(8,128)S(1)}) custom-call(bf16[4,8,192,128]{3,2,1,0:T(8,128)(2,1)S(1)} %get-tuple-element.35.own_ref, bf16[2,8,64,128]{3,2,1,0:T(8,128)(2,1)S(1)} %get-tuple-element.39.before_ref, bf16[2,8,64,128]{3,2,1,0:T(8,128)(2,1)S(1)} %get-tuple-element.40.after_ref, ...), custom_call_target="tpu_custom_call" | custom-call | tf_op jit(solution)/shard_map/pallas_call | solution.py:33
  14.9 1.1 %collective-permute-done.2.cross_ref = bf16[4,2,64,128]{3,2,1,0:T(8,128)(2,1)S(1)} collective-permute-done((bf16[4,2,64,128]{3,2,1,0:T(8,128)(2,1)S(1)}, bf16[4,2,64,128]{3,2,1,0:T(8,128)(2,1)S(1)}, u32[]{:S(2)}, u32[]{:S(2)}) %collective-permute-start.2) | collective-permute-done | bytes 131104 | tf_op jit(solution)/shard_map/ppermute | solution.py:366
  16.0 1.6 %shard_map.87.start_ref = f32[64,256]{1,0:T(8,128)S(1)} custom-call(bf16[4,8,192,128]{3,2,1,0:T(8,128)(2,1)S(1)} %get-tuple-element.35.own_ref, bf16[4,8,192,128]{3,2,1,0:T(8,128)(2,1)S(1)} %get-tuple-element.41.halo_ref, bf16[8,2,64,128]{3,2,1,0:T(8,128)(2,1)S(1)} %collective-permute-done.4.partner_ref, ...), custom_call_target="tpu_custom_call" | custom-call | tf_op jit(solution)/shard_map/pallas_call | solution.py:33
  17.7 0.0 collective-permute-done.3.corner_ref
  17.7 2.3 %shard_map.88 = (f32[4,4,40]{2,1,0:T(4,128)S(1)}, bf16[2,160,128]{2,1,0:T(8,128)(2,1)S(1)}) custom-call(bf16[4,8,192,128]{3,2,1,0:T(8,128)(2,1)S(1)} %get-tuple-element.35.own_ref, bf16[4,8,192,128]{3,2,1,0:T(8,128)(2,1)S(1)} %get-tuple-element.41.halo_ref, bf16[4,2,64,128]{3,2,1,0:T(8,128)(2,1)S(1)} %collective-permute-done.2.cross_ref, ...), custom_call_target="tpu_custom_call" | custom-call | tf_op jit(solution)/shard_map/pallas_call | solution.py:33
  20.0 1.1 %collective-permute-start.5 = (f32[4,4,40]{2,1,0:T(4,128)S(1)}, f32[4,4,40]{2,1,0:T(4,128)S(1)}, u32[]{:S(2)}, u32[]{:S(2)}) collective-permute-start(f32[4,4,40]{2,1,0:T(4,128)S(1)} %get-tuple-element.52), channel_id=1, source_target_pairs={{0,2},{2,0},{1,3},{3,1},{4,6},{6,4},{5,7},{7,5},{8,10},{10,8},{9,1... | collective-permute-start | bytes 7688 | tf_op jit(solution)/shard_map/ppermute | solution.py:347
  21.1 1.1 %shard_map.89.kept_ref = f32[4,4,40]{2,1,0:T(4,128)S(1)} custom-call(bf16[2,160,128]{2,1,0:T(8,128)(2,1)S(1)} %get-tuple-element.51.refs_0_, bf16[2,128,512]{2,1,0:T(8,128)(2,1)S(1)} %get-tuple-element.48.first_ref.refs_1_, bf16[2,3,512,512]{3,2,1,0:T(8,128)(2,1)S(1)} %get-tuple-element.49.middle_ref.refs_2_, ...), custom_call_target="tpu_custom_call" | custom-call | tf_op jit(solution)/shard_map/pallas_call | solution.py:33
  22.1 1.5 %collective-permute-done.5.got_ref = f32[4,4,40]{2,1,0:T(4,128)S(1)} collective-permute-done((f32[4,4,40]{2,1,0:T(4,128)S(1)}, f32[4,4,40]{2,1,0:T(4,128)S(1)}, u32[]{:S(2)}, u32[]{:S(2)}) %collective-permute-start.5) | collective-permute-done | bytes 2592 | tf_op jit(solution)/shard_map/ppermute | solution.py:347
  23.7 4.0 %collective-permute-start.6 = (f32[4,4,40]{2,1,0:T(4,128)S(1)}, f32[4,4,40]{2,1,0:T(4,128)S(1)}, u32[]{:S(2)}, u32[]{:S(2)}) collective-permute-start(f32[4,4,40]{2,1,0:T(4,128)S(1)} %get-tuple-element.54), channel_id=1, source_target_pairs={{0,8},{4,12},{8,0},{12,4},{1,9},{5,13},{9,1},{13,5},{2,10},{6,14},... | collective-permute-start | bytes 7688 | tf_op jit(solution)/shard_map/ppermute | solution.py:347
  27.7 1.6 %collective-permute-done.6.got_ref = f32[4,4,40]{2,1,0:T(4,128)S(1)} collective-permute-done((f32[4,4,40]{2,1,0:T(4,128)S(1)}, f32[4,4,40]{2,1,0:T(4,128)S(1)}, u32[]{:S(2)}, u32[]{:S(2)}) %collective-permute-start.6) | collective-permute-done | bytes 2592 | tf_op jit(solution)/shard_map/ppermute | solution.py:347
  29.3 1.7 %collective-permute-start.7 = (f32[4,4,40]{2,1,0:T(4,128)S(1)}, f32[4,4,40]{2,1,0:T(4,128)S(1)}, u32[]{:S(2)}, u32[]{:S(2)}) collective-permute-start(f32[4,4,40]{2,1,0:T(4,128)S(1)} %get-tuple-element.56), channel_id=1, source_target_pairs={{0,4},{4,0},{8,12},{12,8},{1,5},{5,1},{9,13},{13,9},{2,6},{6,2},{1... | collective-permute-start | bytes 7688 | tf_op jit(solution)/shard_map/ppermute | solution.py:347
  31.1 1.9 %collective-permute-done.7.got_ref = f32[4,4,40]{2,1,0:T(4,128)S(1)} collective-permute-done((f32[4,4,40]{2,1,0:T(4,128)S(1)}, f32[4,4,40]{2,1,0:T(4,128)S(1)}, u32[]{:S(2)}, u32[]{:S(2)}) %collective-permute-start.7) | collective-permute-done | bytes 2592 | tf_op jit(solution)/shard_map/ppermute | solution.py:347
  33.0 0.7 %shard_map.92 = f32[4,320]{1,0:T(4,128)} custom-call(f32[4,4,40]{2,1,0:T(4,128)S(1)} %get-tuple-element.55.kept_ref, f32[4,4,40]{2,1,0:T(4,128)S(1)} %collective-permute-done.7.got_ref), custom_call_target="tpu_custom_call" | custom-call | tf_op jit(solution)/shard_map/pallas_call | solution.py:33
  (5 shorter events, 0.0 us)
Async XLA Ops:
  0.0 1.0 %copy-start = (bf16[64,4,8,128]{3,2,1,0:T(8,128)(2,1)S(1)}, bf16[64,4,8,128]{3,2,1,0:T(8,128)(2,1)}, u32[]{:S(2)}) copy-start(bf16[64,4,8,128]{3,2,1,0:T(8,128)(2,1)} %g_ref.1) | copy-start | bytes 1572868
  1.4 9.4 %collective-permute-start = (bf16[2,8,64,128]{3,2,1,0:T(8,128)(2,1)S(1)}, bf16[2,8,64,128]{3,2,1,0:T(8,128)(2,1)S(1)}, u32[]{:S(2)}, u32[]{:S(2)}) collective-permute-start(bf16[2,8,64,128]{3,2,1,0:T(8,128)(2,1)S(1)} %get-tuple-element.36), channel_id=1, source_target_pairs={{0,4},{1,5},{2,6},{3,7},{4,0},{5,1},{6,2},{7,3},{8,12},{9,13},{10,... | collective-permute-start | bytes 786440 | tf_op jit(solution)/shard_map/ppermute | solution.py:366
  4.5 6.3 %collective-permute-start.1 = (bf16[2,8,64,128]{3,2,1,0:T(8,128)(2,1)S(1)}, bf16[2,8,64,128]{3,2,1,0:T(8,128)(2,1)S(1)}, u32[]{:S(2)}, u32[]{:S(2)}) collective-permute-start(bf16[2,8,64,128]{3,2,1,0:T(8,128)(2,1)S(1)} %get-tuple-element.37), channel_id=1, source_target_pairs={{0,1},{1,0},{2,3},{3,2},{4,8},{5,9},{6,10},{7,11},{8,4},{9,5},{10,... | collective-permute-start | bytes 786440 | tf_op jit(solution)/shard_map/ppermute | solution.py:366
  10.9 5.1 %collective-permute-start.4 = (bf16[8,2,64,128]{3,2,1,0:T(8,128)(2,1)S(1)}, bf16[8,2,64,128]{3,2,1,0:T(8,128)(2,1)S(1)}, u32[]{:S(2)}, u32[]{:S(2)}) collective-permute-start(bf16[8,2,64,128]{3,2,1,0:T(8,128)(2,1)S(1)} %get-tuple-element.44), channel_id=1, source_target_pairs={{0,1},{1,0},{2,3},{3,2},{4,5},{5,4},{6,7},{7,6},{8,9},{9,8},{10,11... | collective-permute-start | bytes 786440 | tf_op jit(solution)/shard_map/ppermute | solution.py:347
  11.0 5.0 %collective-permute-start.2 = (bf16[4,2,64,128]{3,2,1,0:T(8,128)(2,1)S(1)}, bf16[4,2,64,128]{3,2,1,0:T(8,128)(2,1)S(1)}, u32[]{:S(2)}, u32[]{:S(2)}) collective-permute-start(bf16[4,2,64,128]{3,2,1,0:T(8,128)(2,1)S(1)} %get-tuple-element.42), channel_id=1, source_target_pairs={{0,16},{1,2},{2,1},{3,19},{4,20},{5,6},{6,5},{7,23},{8,24},{9,10},... | collective-permute-start | bytes 393224 | tf_op jit(solution)/shard_map/ppermute | solution.py:366
  12.7 5.0 %collective-permute-start.3 = (bf16[4,2,64,128]{3,2,1,0:T(8,128)(2,1)S(1)}, bf16[4,2,64,128]{3,2,1,0:T(8,128)(2,1)S(1)}, u32[]{:S(2)}, u32[]{:S(2)}) collective-permute-start(bf16[4,2,64,128]{3,2,1,0:T(8,128)(2,1)S(1)} %get-tuple-element.43), channel_id=1, source_target_pairs={{0,16},{1,2},{2,1},{3,19},{4,20},{5,6},{6,5},{7,23},{8,24},{9,10},... | collective-permute-start | bytes 393224 | tf_op jit(solution)/shard_map/ppermute | solution.py:366
  20.0 3.7 %collective-permute-start.5 = (f32[4,4,40]{2,1,0:T(4,128)S(1)}, f32[4,4,40]{2,1,0:T(4,128)S(1)}, u32[]{:S(2)}, u32[]{:S(2)}) collective-permute-start(f32[4,4,40]{2,1,0:T(4,128)S(1)} %get-tuple-element.52), channel_id=1, source_target_pairs={{0,2},{2,0},{1,3},{3,1},{4,6},{6,4},{5,7},{7,5},{8,10},{10,8},{9,1... | collective-permute-start | bytes 7688 | tf_op jit(solution)/shard_map/ppermute | solution.py:347
  23.7 5.6 %collective-permute-start.6 = (f32[4,4,40]{2,1,0:T(4,128)S(1)}, f32[4,4,40]{2,1,0:T(4,128)S(1)}, u32[]{:S(2)}, u32[]{:S(2)}) collective-permute-start(f32[4,4,40]{2,1,0:T(4,128)S(1)} %get-tuple-element.54), channel_id=1, source_target_pairs={{0,8},{4,12},{8,0},{12,4},{1,9},{5,13},{9,1},{13,5},{2,10},{6,14},... | collective-permute-start | bytes 7688 | tf_op jit(solution)/shard_map/ppermute | solution.py:347
  29.3 3.7 %collective-permute-start.7 = (f32[4,4,40]{2,1,0:T(4,128)S(1)}, f32[4,4,40]{2,1,0:T(4,128)S(1)}, u32[]{:S(2)}, u32[]{:S(2)}) collective-permute-start(f32[4,4,40]{2,1,0:T(4,128)S(1)} %get-tuple-element.56), channel_id=1, source_target_pairs={{0,4},{4,0},{8,12},{12,8},{1,5},{5,1},{9,13},{13,9},{2,6},{6,2},{1... | collective-permute-start | bytes 7688 | tf_op jit(solution)/shard_map/ppermute | solution.py:347

commit v9 on v8

--- a/solution.py
+++ b/solution.py
@@ -46,7 +46,7 @@
     span_x, span_y = g_ref.shape[1:3]
     parity, slab = lax.axis_index("brick") % 2, lax.axis_index("slab")
     for x in range(span_x):
-        own_ref[x] = jnp.swapaxes(g_ref[:, x].astype(F32), 0, 1).astype(BF16)
+        own_ref[x] = jnp.swapaxes(g_ref[:, x], 0, 1)
     for side in range(2):
 
         @pl.when(parity == side)
@@ -65,12 +65,13 @@
 
         @pl.when(lax.axis_index("brick") % 2 == side)
         def _(before=(odd_ref, even_ref)[side], after=(even_ref, odd_ref)[side]):
-            brick = lax.axis_index("brick")
-            outside = jnp.zeros(before_ref.shape, F32)
-            inside = before[...].astype(F32)
-            before_ref[...] = jnp.where(brick > 0, inside, outside).astype(BF16)
-            inside = after[...].astype(F32)
-            after_ref[...] = jnp.where(brick < lax.axis_size("brick") - 1, inside, outside).astype(BF16)
+            brick, last = lax.axis_index("brick"), lax.axis_size("brick") - 1
+            for ref, source, inside in (
+                (before_ref, before, brick > 0),
+                (after_ref, after, brick < last),
+            ):
+                keep = jnp.where(inside, jnp.ones((1, 1, 1, source.shape[3]), F32), 0.0).astype(BF16)
+                ref[...] = source[...] * keep
 
     for slab in range(2):
 

time: 33.8 us -> 33.7 us (level)
  no operation moved by 1% of the time
where the time goes in v9:
time: 33.7 us; the launch traced here: 33.5 us
  starting transfers between devices  12.1 us (36%)
  Pallas kernels  11.1 us (33%)
  waiting for transfers between devices  9.19 us (27%)
  local copies, waits for them, and re-layouts  1.04 us (3%)
    pallas_call x11, Pallas kernels, run(): pl.pallas_call(body, out_shape=outs, in_specs=[pl.BlockSpec(memory_space=...  11.1 us
    ppermute x4, starting transfers between devices, swap(): lax.ppermute(array, axis, [(i, i ^ step) for i in range(lax.axis_size(axi...  6.9 us
    ppermute x4, starting transfers between devices, swap_pairs(): return lax.ppermute(array, everything, pairs)  5.21 us
    ppermute x4, waiting for transfers between devices, swap(): lax.ppermute(array, axis, [(i, i ^ step) for i in range(lax.axis_size(axi...  5.05 us
    ppermute x4, waiting for transfers between devices, swap_pairs(): return lax.ppermute(array, everything, pairs)  4.14 us
    unnamed x2, local copies, waits for them, and re-layouts  1.04 us
  transfers between devices with their start and end apart: 8, of which 5 were waited for; matrix products, arithmetic and copies ran while one was open for 0% of the time, Pallas kernels for 23%

profile of v9, /device:TPU:0, one launch (start us, length us, event | category | flops | bytes accessed | tf_op | source)
XLA Modules:
  0.0 33.5 jit_solution(2054428708770553863)
XLA Ops:
  0.0 1.0 %copy-done = bf16[64,4,8,128]{3,2,1,0:T(8,128)(2,1)S(1)} copy-done((bf16[64,4,8,128]{3,2,1,0:T(8,128)(2,1)S(1)}, bf16[64,4,8,128]{3,2,1,0:T(8,128)(2,1)}, u32[]{:S(2)}) %copy-start) | copy-done | bytes 524312
  1.0 0.2 shard_map.82
  1.3 3.1 %collective-permute-start = (bf16[2,8,64,128]{3,2,1,0:T(8,128)(2,1)S(1)}, bf16[2,8,64,128]{3,2,1,0:T(8,128)(2,1)S(1)}, u32[]{:S(2)}, u32[]{:S(2)}) collective-permute-start(bf16[2,8,64,128]{3,2,1,0:T(8,128)(2,1)S(1)} %get-tuple-element.36), channel_id=1, source_target_pairs={{0,4},{1,5},{2,6},{3,7},{4,0},{5,1},{6,2},{7,3},{8,12},{9,13},{10,... | collective-permute-start | bytes 786440 | tf_op jit(solution)/shard_map/ppermute | solution.py:367
  4.4 0.0 collective-permute-start.1
  4.4 2.2 %shard_map.83 = (bf16[320,256]{1,0:T(8,128)(2,1)S(1)}, bf16[128,256]{1,0:T(8,128)(2,1)S(1)}, f32[60,256]{1,0:T(8,128)S(1)}, bf16[128,2304]{1,0:T(8,128)(2,1)S(1)...) custom-call(f32[3,256]{1,0:T(4,128)} %place_hbm.1, ...), custom_call_target="tpu_custom_call" | custom-call | tf_op jit(solution)/shard_map/pallas_call | solution.py:33
  6.6 1.1 %shard_map.84 = (bf16[4,8,192,128]{3,2,1,0:T(8,128)(2,1)S(1)}, f32[64,256]{1,0:T(8,128)S(1)}) custom-call(bf16[4,8,64,128]{3,2,1,0:T(8,128)(2,1)S(1)} %get-tuple-element.31.own_ref, bf16[128,2304]{1,0:T(8,128)(2,1)S(1)} %get-tuple-element.32.kernel_ref, bf16[128,256]{1,0:T(8,128)(2,1)S(1)} %get-tuple-element.33.wz_ref, f32[60,256]{1,0:T(8,128)S(1)} %get-tuple-element.34.wxy_ref), custom_call_target="tpu_custom_call" | custom-call | tf_op jit(solution)/shard_map/pallas_call | solution.py:33
  7.7 3.0 %collective-permute-done.even_ref = bf16[2,8,64,128]{3,2,1,0:T(8,128)(2,1)S(1)} collective-permute-done((bf16[2,8,64,128]{3,2,1,0:T(8,128)(2,1)S(1)}, bf16[2,8,64,128]{3,2,1,0:T(8,128)(2,1)S(1)}, u32[]{:S(2)}, u32[]{:S(2)}) %collective-permute-start) | collective-permute-done | bytes 262176 | tf_op jit(solution)/shard_map/ppermute | solution.py:367
  10.7 0.1 shard_map.85
  10.8 0.1 collective-permute-start.4
  10.9 1.7 %collective-permute-start.2 = (bf16[4,2,64,128]{3,2,1,0:T(8,128)(2,1)S(1)}, bf16[4,2,64,128]{3,2,1,0:T(8,128)(2,1)S(1)}, u32[]{:S(2)}, u32[]{:S(2)}) collective-permute-start(bf16[4,2,64,128]{3,2,1,0:T(8,128)(2,1)S(1)} %get-tuple-element.42), channel_id=1, source_target_pairs={{0,16},{1,2},{2,1},{3,19},{4,20},{5,6},{6,5},{7,23},{8,24},{9,10},... | collective-permute-start | bytes 393224 | tf_op jit(solution)/shard_map/ppermute | solution.py:367
  12.6 0.3 %collective-permute-start.3 = (bf16[4,2,64,128]{3,2,1,0:T(8,128)(2,1)S(1)}, bf16[4,2,64,128]{3,2,1,0:T(8,128)(2,1)S(1)}, u32[]{:S(2)}, u32[]{:S(2)}) collective-permute-start(bf16[4,2,64,128]{3,2,1,0:T(8,128)(2,1)S(1)} %get-tuple-element.43), channel_id=1, source_target_pairs={{0,16},{1,2},{2,1},{3,19},{4,20},{5,6},{6,5},{7,23},{8,24},{9,10},... | collective-permute-start | bytes 393224 | tf_op jit(solution)/shard_map/ppermute | solution.py:367
  13.0 1.8 %shard_map.86 = (bf16[4,8,192,128]{3,2,1,0:T(8,128)(2,1)S(1)}, f32[64,256]{1,0:T(8,128)S(1)}) custom-call(bf16[4,8,192,128]{3,2,1,0:T(8,128)(2,1)S(1)} %get-tuple-element.35.own_ref, bf16[2,8,64,128]{3,2,1,0:T(8,128)(2,1)S(1)} %get-tuple-element.39.before_ref, bf16[2,8,64,128]{3,2,1,0:T(8,128)(2,1)S(1)} %get-tuple-element.40.after_ref, ...), custom_call_target="tpu_custom_call" | custom-call | tf_op jit(solution)/shard_map/pallas_call | solution.py:33
  14.8 1.1 %collective-permute-done.2.cross_ref = bf16[4,2,64,128]{3,2,1,0:T(8,128)(2,1)S(1)} collective-permute-done((bf16[4,2,64,128]{3,2,1,0:T(8,128)(2,1)S(1)}, bf16[4,2,64,128]{3,2,1,0:T(8,128)(2,1)S(1)}, u32[]{:S(2)}, u32[]{:S(2)}) %collective-permute-start.2) | collective-permute-done | bytes 131104 | tf_op jit(solution)/shard_map/ppermute | solution.py:367
  15.9 1.6 %shard_map.87.start_ref = f32[64,256]{1,0:T(8,128)S(1)} custom-call(bf16[4,8,192,128]{3,2,1,0:T(8,128)(2,1)S(1)} %get-tuple-element.35.own_ref, bf16[4,8,192,128]{3,2,1,0:T(8,128)(2,1)S(1)} %get-tuple-element.41.halo_ref, bf16[8,2,64,128]{3,2,1,0:T(8,128)(2,1)S(1)} %collective-permute-done.4.partner_ref, ...), custom_call_target="tpu_custom_call" | custom-call | tf_op jit(solution)/shard_map/pallas_call | solution.py:33
  17.6 0.0 collective-permute-done.3.corner_ref
  17.6 2.3 %shard_map.88 = (f32[4,4,40]{2,1,0:T(4,128)S(1)}, bf16[2,160,128]{2,1,0:T(8,128)(2,1)S(1)}) custom-call(bf16[4,8,192,128]{3,2,1,0:T(8,128)(2,1)S(1)} %get-tuple-element.35.own_ref, bf16[4,8,192,128]{3,2,1,0:T(8,128)(2,1)S(1)} %get-tuple-element.41.halo_ref, bf16[4,2,64,128]{3,2,1,0:T(8,128)(2,1)S(1)} %collective-permute-done.2.cross_ref, ...), custom_call_target="tpu_custom_call" | custom-call | tf_op jit(solution)/shard_map/pallas_call | solution.py:33
  19.9 1.1 %collective-permute-start.5 = (f32[4,4,40]{2,1,0:T(4,128)S(1)}, f32[4,4,40]{2,1,0:T(4,128)S(1)}, u32[]{:S(2)}, u32[]{:S(2)}) collective-permute-start(f32[4,4,40]{2,1,0:T(4,128)S(1)} %get-tuple-element.52), channel_id=1, source_target_pairs={{0,2},{2,0},{1,3},{3,1},{4,6},{6,4},{5,7},{7,5},{8,10},{10,8},{9,1... | collective-permute-start | bytes 7688 | tf_op jit(solution)/shard_map/ppermute | solution.py:348
  21.0 1.1 %shard_map.89.kept_ref = f32[4,4,40]{2,1,0:T(4,128)S(1)} custom-call(bf16[2,160,128]{2,1,0:T(8,128)(2,1)S(1)} %get-tuple-element.51.refs_0_, bf16[2,128,512]{2,1,0:T(8,128)(2,1)S(1)} %get-tuple-element.48.first_ref.refs_1_, bf16[2,3,512,512]{3,2,1,0:T(8,128)(2,1)S(1)} %get-tuple-element.49.middle_ref.refs_2_, ...), custom_call_target="tpu_custom_call" | custom-call | tf_op jit(solution)/shard_map/pallas_call | solution.py:33
  22.0 1.5 %collective-permute-done.5.got_ref = f32[4,4,40]{2,1,0:T(4,128)S(1)} collective-permute-done((f32[4,4,40]{2,1,0:T(4,128)S(1)}, f32[4,4,40]{2,1,0:T(4,128)S(1)}, u32[]{:S(2)}, u32[]{:S(2)}) %collective-permute-start.5) | collective-permute-done | bytes 2592 | tf_op jit(solution)/shard_map/ppermute | solution.py:348
  23.6 4.0 %collective-permute-start.6 = (f32[4,4,40]{2,1,0:T(4,128)S(1)}, f32[4,4,40]{2,1,0:T(4,128)S(1)}, u32[]{:S(2)}, u32[]{:S(2)}) collective-permute-start(f32[4,4,40]{2,1,0:T(4,128)S(1)} %get-tuple-element.54), channel_id=1, source_target_pairs={{0,8},{4,12},{8,0},{12,4},{1,9},{5,13},{9,1},{13,5},{2,10},{6,14},... | collective-permute-start | bytes 7688 | tf_op jit(solution)/shard_map/ppermute | solution.py:348
  27.6 1.6 %collective-permute-done.6.got_ref = f32[4,4,40]{2,1,0:T(4,128)S(1)} collective-permute-done((f32[4,4,40]{2,1,0:T(4,128)S(1)}, f32[4,4,40]{2,1,0:T(4,128)S(1)}, u32[]{:S(2)}, u32[]{:S(2)}) %collective-permute-start.6) | collective-permute-done | bytes 2592 | tf_op jit(solution)/shard_map/ppermute | solution.py:348
  29.2 1.7 %collective-permute-start.7 = (f32[4,4,40]{2,1,0:T(4,128)S(1)}, f32[4,4,40]{2,1,0:T(4,128)S(1)}, u32[]{:S(2)}, u32[]{:S(2)}) collective-permute-start(f32[4,4,40]{2,1,0:T(4,128)S(1)} %get-tuple-element.56), channel_id=1, source_target_pairs={{0,4},{4,0},{8,12},{12,8},{1,5},{5,1},{9,13},{13,9},{2,6},{6,2},{1... | collective-permute-start | bytes 7688 | tf_op jit(solution)/shard_map/ppermute | solution.py:348
  31.0 1.9 %collective-permute-done.7.got_ref = f32[4,4,40]{2,1,0:T(4,128)S(1)} collective-permute-done((f32[4,4,40]{2,1,0:T(4,128)S(1)}, f32[4,4,40]{2,1,0:T(4,128)S(1)}, u32[]{:S(2)}, u32[]{:S(2)}) %collective-permute-start.7) | collective-permute-done | bytes 2592 | tf_op jit(solution)/shard_map/ppermute | solution.py:348
  32.9 0.7 %shard_map.92 = f32[4,320]{1,0:T(4,128)} custom-call(f32[4,4,40]{2,1,0:T(4,128)S(1)} %get-tuple-element.55.kept_ref, f32[4,4,40]{2,1,0:T(4,128)S(1)} %collective-permute-done.7.got_ref), custom_call_target="tpu_custom_call" | custom-call | tf_op jit(solution)/shard_map/pallas_call | solution.py:33
  (5 shorter events, 0.0 us)
Async XLA Ops:
  0.0 1.0 %copy-start = (bf16[64,4,8,128]{3,2,1,0:T(8,128)(2,1)S(1)}, bf16[64,4,8,128]{3,2,1,0:T(8,128)(2,1)}, u32[]{:S(2)}) copy-start(bf16[64,4,8,128]{3,2,1,0:T(8,128)(2,1)} %g_ref.1) | copy-start | bytes 1572868
  1.3 9.4 %collective-permute-start = (bf16[2,8,64,128]{3,2,1,0:T(8,128)(2,1)S(1)}, bf16[2,8,64,128]{3,2,1,0:T(8,128)(2,1)S(1)}, u32[]{:S(2)}, u32[]{:S(2)}) collective-permute-start(bf16[2,8,64,128]{3,2,1,0:T(8,128)(2,1)S(1)} %get-tuple-element.36), channel_id=1, source_target_pairs={{0,4},{1,5},{2,6},{3,7},{4,0},{5,1},{6,2},{7,3},{8,12},{9,13},{10,... | collective-permute-start | bytes 786440 | tf_op jit(solution)/shard_map/ppermute | solution.py:367
  4.4 6.3 %collective-permute-start.1 = (bf16[2,8,64,128]{3,2,1,0:T(8,128)(2,1)S(1)}, bf16[2,8,64,128]{3,2,1,0:T(8,128)(2,1)S(1)}, u32[]{:S(2)}, u32[]{:S(2)}) collective-permute-start(bf16[2,8,64,128]{3,2,1,0:T(8,128)(2,1)S(1)} %get-tuple-element.37), channel_id=1, source_target_pairs={{0,1},{1,0},{2,3},{3,2},{4,8},{5,9},{6,10},{7,11},{8,4},{9,5},{10,... | collective-permute-start | bytes 786440 | tf_op jit(solution)/shard_map/ppermute | solution.py:367
  10.8 5.1 %collective-permute-start.4 = (bf16[8,2,64,128]{3,2,1,0:T(8,128)(2,1)S(1)}, bf16[8,2,64,128]{3,2,1,0:T(8,128)(2,1)S(1)}, u32[]{:S(2)}, u32[]{:S(2)}) collective-permute-start(bf16[8,2,64,128]{3,2,1,0:T(8,128)(2,1)S(1)} %get-tuple-element.44), channel_id=1, source_target_pairs={{0,1},{1,0},{2,3},{3,2},{4,5},{5,4},{6,7},{7,6},{8,9},{9,8},{10,11... | collective-permute-start | bytes 786440 | tf_op jit(solution)/shard_map/ppermute | solution.py:348
  10.9 5.0 %collective-permute-start.2 = (bf16[4,2,64,128]{3,2,1,0:T(8,128)(2,1)S(1)}, bf16[4,2,64,128]{3,2,1,0:T(8,128)(2,1)S(1)}, u32[]{:S(2)}, u32[]{:S(2)}) collective-permute-start(bf16[4,2,64,128]{3,2,1,0:T(8,128)(2,1)S(1)} %get-tuple-element.42), channel_id=1, source_target_pairs={{0,16},{1,2},{2,1},{3,19},{4,20},{5,6},{6,5},{7,23},{8,24},{9,10},... | collective-permute-start | bytes 393224 | tf_op jit(solution)/shard_map/ppermute | solution.py:367
  12.6 5.0 %collective-permute-start.3 = (bf16[4,2,64,128]{3,2,1,0:T(8,128)(2,1)S(1)}, bf16[4,2,64,128]{3,2,1,0:T(8,128)(2,1)S(1)}, u32[]{:S(2)}, u32[]{:S(2)}) collective-permute-start(bf16[4,2,64,128]{3,2,1,0:T(8,128)(2,1)S(1)} %get-tuple-element.43), channel_id=1, source_target_pairs={{0,16},{1,2},{2,1},{3,19},{4,20},{5,6},{6,5},{7,23},{8,24},{9,10},... | collective-permute-start | bytes 393224 | tf_op jit(solution)/shard_map/ppermute | solution.py:367
  19.9 3.7 %collective-permute-start.5 = (f32[4,4,40]{2,1,0:T(4,128)S(1)}, f32[4,4,40]{2,1,0:T(4,128)S(1)}, u32[]{:S(2)}, u32[]{:S(2)}) collective-permute-start(f32[4,4,40]{2,1,0:T(4,128)S(1)} %get-tuple-element.52), channel_id=1, source_target_pairs={{0,2},{2,0},{1,3},{3,1},{4,6},{6,4},{5,7},{7,5},{8,10},{10,8},{9,1... | collective-permute-start | bytes 7688 | tf_op jit(solution)/shard_map/ppermute | solution.py:348
  23.6 5.7 %collective-permute-start.6 = (f32[4,4,40]{2,1,0:T(4,128)S(1)}, f32[4,4,40]{2,1,0:T(4,128)S(1)}, u32[]{:S(2)}, u32[]{:S(2)}) collective-permute-start(f32[4,4,40]{2,1,0:T(4,128)S(1)} %get-tuple-element.54), channel_id=1, source_target_pairs={{0,8},{4,12},{8,0},{12,4},{1,9},{5,13},{9,1},{13,5},{2,10},{6,14},... | collective-permute-start | bytes 7688 | tf_op jit(solution)/shard_map/ppermute | solution.py:348
  29.2 3.7 %collective-permute-start.7 = (f32[4,4,40]{2,1,0:T(4,128)S(1)}, f32[4,4,40]{2,1,0:T(4,128)S(1)}, u32[]{:S(2)}, u32[]{:S(2)}) collective-permute-start(f32[4,4,40]{2,1,0:T(4,128)S(1)} %get-tuple-element.56), channel_id=1, source_target_pairs={{0,4},{4,0},{8,12},{12,8},{1,5},{5,1},{9,13},{13,9},{2,6},{6,2},{1... | collective-permute-start | bytes 7688 | tf_op jit(solution)/shard_map/ppermute | solution.py:348

commit v10 on v9

--- a/solution.py
+++ b/solution.py
@@ -106,6 +106,7 @@
         slots = pick_ref.shape[0]
         brick, line = lax.axis_index("brick"), lax.axis_index(("sect", "slab"))
         last_brick, last_line = lax.axis_size("brick") - 1, lax.axis_size(("sect", "slab")) - 1
+        half = slots // 2
         local_x = place_ref[0:1, :] * span_x
         local_y = place_ref[1:2, :] * span_y
         local_z = place_ref[2:3, :] * span_z
@@ -241,47 +242,68 @@
     total_ref[...] = share(start_ref[...], units, kernel_ref, wz_ref, wxy_ref)
 
 
-def side_units(on_left, inside, layers, halo_tile, own_ref, halo_ref, side_ref):
-    _, span_y = own_ref.shape[:2]
+class Shifted:
+    def __init__(self, ref, base):
+        self.ref, self.base = ref, base
+
+    def __getitem__(self, at):
+        return self.ref[at[0] - self.base, at[1]]
+
+    def __setitem__(self, at, value):
+        self.ref[at[0] - self.base, at[1]] = value
+
+
+def side_units(on_left, inside, layers, halo_tile, own_ref, halo_ref, side_ref, ready_ref=None):
+    span_x, span_y = own_ref.shape[:2]
     near = jnp.where(on_left, 0, span_y - HALO)
+
+    def ready(x):
+        return ready_ref is not None and HALO <= x < HALO + span_x
+
     for x in sorted({x + a for x in layers for a in range(3)}):
+        if ready(x):
+            continue
         for j in range(HALO):
             side_ref[x, jnp.where(on_left, HALO, 0) + j] = layer_of(own_ref, halo_ref, x)[near + j]
             side_ref[x, jnp.where(on_left, 0, HALO) + j] = taps(halo_tile(x)[j], inside)
     base = jnp.where(on_left, 0, span_y)
-    return [(lambda x, c: side_ref[x, c], lambda x: x * (span_y + 2) + base, x) for x in layers]
-
-
-def cross_units(layers, cross_ref, corner_ref, own_ref, halo_ref, side_ref):
+
+    def tap(x, c):
+        return ready_ref[x - HALO, c] if ready(x) else side_ref[x, c]
+
+    return [(tap, lambda x: x * (span_y + 2) + base, x) for x in layers]
+
+
+def cross_units(layers, cross_ref, corner_ref, own_ref, halo_ref, side_ref, ready_ref=None):
     line = lax.axis_index(("sect", "slab"))
     inside = (line > 0) & (line < lax.axis_size(("sect", "slab")) - 1)
     return side_units(
         lax.axis_index("slab") == 0, inside, layers, lambda x: layer_of(cross_ref, corner_ref, x),
-        own_ref, halo_ref, side_ref,
+        own_ref, halo_ref, side_ref, ready_ref,
     )
 
 
 def beside_body(
     own_ref, halo_ref, partner_ref, cross_ref, kernel_ref, wz_ref, wxy_ref, start_ref,
-    total_ref, partner_side, cross_side,
+    total_ref, ready_ref, partner_side,
 ):
     span_x = own_ref.shape[0]
     units = side_units(
         lax.axis_index("slab") == 1, True, range(span_x + 2), lambda x: partner_ref.at[x],
         own_ref, halo_ref, partner_side,
     )
-    units += cross_units(range(HALO, span_x), cross_ref, None, own_ref, halo_ref, cross_side)
+    units += cross_units(range(HALO, span_x), cross_ref, None, own_ref, halo_ref, Shifted(ready_ref, HALO))
     total_ref[...] = share(start_ref[...], units, kernel_ref, wz_ref, wxy_ref)
 
 
 def outer_body(
-    own_ref, halo_ref, cross_ref, corner_ref, kernel_ref, wz_ref, wxy_ref, start_ref,
+    own_ref, halo_ref, cross_ref, corner_ref, ready_ref, kernel_ref, wz_ref, wxy_ref, start_ref,
     pick_ref, attr_ref, first_ref, middle_ref, last_ref,
     value_ref, row_ref, cross_side,
 ):
     span_x = own_ref.shape[0]
     layers = [*range(HALO), *range(span_x, span_x + 2)]
-    units = cross_units(layers, cross_ref, corner_ref, own_ref, halo_ref, cross_side)
+    units = cross_units(layers, cross_ref, corner_ref, own_ref, halo_ref, cross_side, ready_ref)
     total = share(start_ref[...], units, kernel_ref, wz_ref, wxy_ref)
     table = jnp.concatenate([total.astype(BF16), attr_ref[...]], axis=0)
     row = lax.dot_general(
@@ -445,7 +467,10 @@
         inner_body, [block(2 * HALO, span_y, 3 * channels, span_z), features], [], 8
     )(own_taps, before, after, kernel, wz, wxy, total)
     side = pltpu.VMEM((span_x + 2 * HALO, 2 * HALO, 3 * channels, span_z), BF16)
-    total = call(beside_body, features, [side, side], 10)(own_taps, halo_taps, partner, cross, kernel, wz, wxy, total)
+    ready = block(span_x, 2 * HALO, 3 * channels, span_z)
+    total, ready = call(beside_body, [features, ready], [side], 10)(
+        own_taps, halo_taps, partner, cross, kernel, wz, wxy, total
+    )
     blocks = bricks * sects // 2
 
     def values(number):
@@ -453,7 +478,7 @@
 
     sent, table = call(
         outer_body, [values(blocks), block(2, slots // 2, point_attr.shape[1] + channels)], [side], 8
-    )(own_taps, halo_taps, cross, corner, kernel, wz, wxy, total, pick, attr, first, middle, last)
+    )(own_taps, halo_taps, cross, corner, ready, kernel, wz, wxy, total, pick, attr, first, middle, last)
     got = swap(sent, "sect", sects // 2)
     kept = call(own_body, values(blocks), [], 8)(table, first, middle, last)
     labels = [list(range(blocks)), [blocks + q for q in range(blocks)]]

time: 33.7 us -> 33.6 us (level)
  transfers between devices with their start and end apart: 8 -> 8, of which waited for: 5 -> 5; matrix products, arithmetic and copies ran while one was open for 0% -> 0% of each run, Pallas kernels for 23% -> 24%
where the time goes in v10:
time: 33.6 us; the launch traced here: 33.4 us
  starting transfers between devices  12.1 us (36%)
  Pallas kernels  11 us (33%)
  waiting for transfers between devices  9.16 us (27%)
  local copies, waits for them, and re-layouts  1.04 us (3%)
    pallas_call x11, Pallas kernels, run(): pl.pallas_call(body, out_shape=outs, in_specs=[pl.BlockSpec(memory_space=...  11 us
    ppermute x4, starting transfers between devices, swap(): lax.ppermute(array, axis, [(i, i ^ step) for i in range(lax.axis_size(axi...  6.92 us
    ppermute x4, starting transfers between devices, swap_pairs(): return lax.ppermute(array, everything, pairs)  5.21 us
    ppermute x4, waiting for transfers between devices, swap(): lax.ppermute(array, axis, [(i, i ^ step) for i in range(lax.axis_size(axi...  5.04 us
    ppermute x4, waiting for transfers between devices, swap_pairs(): return lax.ppermute(array, everything, pairs)  4.12 us
    unnamed x2, local copies, waits for them, and re-layouts  1.04 us
  transfers between devices with their start and end apart: 8, of which 5 were waited for; matrix products, arithmetic and copies ran while one was open for 0% of the time, Pallas kernels for 24%

profile of v10, /device:TPU:0, one launch (start us, length us, event | category | flops | bytes accessed | tf_op | source)
XLA Modules:
  0.0 33.4 jit_solution(8577980401014892596)
XLA Ops:
  0.0 1.0 %copy-done = bf16[64,4,8,128]{3,2,1,0:T(8,128)(2,1)S(1)} copy-done((bf16[64,4,8,128]{3,2,1,0:T(8,128)(2,1)S(1)}, bf16[64,4,8,128]{3,2,1,0:T(8,128)(2,1)}, u32[]{:S(2)}) %copy-start) | copy-done | bytes 524312
  1.0 0.2 shard_map.82
  1.3 3.1 %collective-permute-start = (bf16[2,8,64,128]{3,2,1,0:T(8,128)(2,1)S(1)}, bf16[2,8,64,128]{3,2,1,0:T(8,128)(2,1)S(1)}, u32[]{:S(2)}, u32[]{:S(2)}) collective-permute-start(bf16[2,8,64,128]{3,2,1,0:T(8,128)(2,1)S(1)} %get-tuple-element.38), channel_id=1, source_target_pairs={{0,4},{1,5},{2,6},{3,7},{4,0},{5,1},{6,2},{7,3},{8,12},{9,13},{10,... | collective-permute-start | bytes 786440 | tf_op jit(solution)/shard_map/ppermute | solution.py:389
  4.4 0.0 collective-permute-start.1
  4.4 2.2 %shard_map.83 = (bf16[320,256]{1,0:T(8,128)(2,1)S(1)}, bf16[128,256]{1,0:T(8,128)(2,1)S(1)}, f32[60,256]{1,0:T(8,128)S(1)}, bf16[128,2304]{1,0:T(8,128)(2,1)S(1)...) custom-call(f32[3,256]{1,0:T(4,128)} %place_hbm.1, ...), custom_call_target="tpu_custom_call" | custom-call | tf_op jit(solution)/shard_map/pallas_call | solution.py:33
  6.6 1.1 %shard_map.84 = (bf16[4,8,192,128]{3,2,1,0:T(8,128)(2,1)S(1)}, f32[64,256]{1,0:T(8,128)S(1)}) custom-call(bf16[4,8,64,128]{3,2,1,0:T(8,128)(2,1)S(1)} %get-tuple-element.33.own_ref, bf16[128,2304]{1,0:T(8,128)(2,1)S(1)} %get-tuple-element.34.kernel_ref, bf16[128,256]{1,0:T(8,128)(2,1)S(1)} %get-tuple-element.35.wz_ref, f32[60,256]{1,0:T(8,128)S(1)} %get-tuple-element.36.wxy_ref), custom_call_target="tpu_custom_call" | custom-call | tf_op jit(solution)/shard_map/pallas_call | solution.py:33
  7.7 3.0 %collective-permute-done.even_ref = bf16[2,8,64,128]{3,2,1,0:T(8,128)(2,1)S(1)} collective-permute-done((bf16[2,8,64,128]{3,2,1,0:T(8,128)(2,1)S(1)}, bf16[2,8,64,128]{3,2,1,0:T(8,128)(2,1)S(1)}, u32[]{:S(2)}, u32[]{:S(2)}) %collective-permute-start) | collective-permute-done | bytes 262176 | tf_op jit(solution)/shard_map/ppermute | solution.py:389
  10.7 0.1 shard_map.85
  10.8 0.1 collective-permute-start.4
  10.9 1.7 %collective-permute-start.2 = (bf16[4,2,64,128]{3,2,1,0:T(8,128)(2,1)S(1)}, bf16[4,2,64,128]{3,2,1,0:T(8,128)(2,1)S(1)}, u32[]{:S(2)}, u32[]{:S(2)}) collective-permute-start(bf16[4,2,64,128]{3,2,1,0:T(8,128)(2,1)S(1)} %get-tuple-element.44), channel_id=1, source_target_pairs={{0,16},{1,2},{2,1},{3,19},{4,20},{5,6},{6,5},{7,23},{8,24},{9,10},... | collective-permute-start | bytes 393224 | tf_op jit(solution)/shard_map/ppermute | solution.py:389
  12.6 0.3 %collective-permute-start.3 = (bf16[4,2,64,128]{3,2,1,0:T(8,128)(2,1)S(1)}, bf16[4,2,64,128]{3,2,1,0:T(8,128)(2,1)S(1)}, u32[]{:S(2)}, u32[]{:S(2)}) collective-permute-start(bf16[4,2,64,128]{3,2,1,0:T(8,128)(2,1)S(1)} %get-tuple-element.45), channel_id=1, source_target_pairs={{0,16},{1,2},{2,1},{3,19},{4,20},{5,6},{6,5},{7,23},{8,24},{9,10},... | collective-permute-start | bytes 393224 | tf_op jit(solution)/shard_map/ppermute | solution.py:389
  13.0 1.8 %shard_map.86 = (bf16[4,8,192,128]{3,2,1,0:T(8,128)(2,1)S(1)}, f32[64,256]{1,0:T(8,128)S(1)}) custom-call(bf16[4,8,192,128]{3,2,1,0:T(8,128)(2,1)S(1)} %get-tuple-element.37.own_ref, bf16[2,8,64,128]{3,2,1,0:T(8,128)(2,1)S(1)} %get-tuple-element.41.before_ref, bf16[2,8,64,128]{3,2,1,0:T(8,128)(2,1)S(1)} %get-tuple-element.42.after_ref, ...), custom_call_target="tpu_custom_call" | custom-call | tf_op jit(solution)/shard_map/pallas_call | solution.py:33
  14.8 1.1 %collective-permute-done.2.cross_ref = bf16[4,2,64,128]{3,2,1,0:T(8,128)(2,1)S(1)} collective-permute-done((bf16[4,2,64,128]{3,2,1,0:T(8,128)(2,1)S(1)}, bf16[4,2,64,128]{3,2,1,0:T(8,128)(2,1)S(1)}, u32[]{:S(2)}, u32[]{:S(2)}) %collective-permute-start.2) | collective-permute-done | bytes 131104 | tf_op jit(solution)/shard_map/ppermute | solution.py:389
  15.9 1.7 %shard_map.87 = (f32[64,256]{1,0:T(8,128)S(1)}, bf16[4,4,192,128]{3,2,1,0:T(8,128)(2,1)S(1)}) custom-call(bf16[4,8,192,128]{3,2,1,0:T(8,128)(2,1)S(1)} %get-tuple-element.37.own_ref, bf16[4,8,192,128]{3,2,1,0:T(8,128)(2,1)S(1)} %get-tuple-element.43.halo_ref, bf16[8,2,64,128]{3,2,1,0:T(8,128)(2,1)S(1)} %collective-permute-done.4.partner_ref, ...), custom_call_target="tpu_custom_call" | custom-call | tf_op jit(solution)/shard_map/pallas_call | solution.py:33
  17.6 0.0 collective-permute-done.3.corner_ref
  17.6 2.1 %shard_map.88 = (f32[4,4,40]{2,1,0:T(4,128)S(1)}, bf16[2,160,128]{2,1,0:T(8,128)(2,1)S(1)}) custom-call(bf16[4,8,192,128]{3,2,1,0:T(8,128)(2,1)S(1)} %get-tuple-element.37.own_ref, bf16[4,8,192,128]{3,2,1,0:T(8,128)(2,1)S(1)} %get-tuple-element.43.halo_ref, bf16[4,2,64,128]{3,2,1,0:T(8,128)(2,1)S(1)} %collective-permute-done.2.cross_ref, ...), custom_call_target="tpu_custom_call" | custom-call | tf_op jit(solution)/shard_map/pallas_call | solution.py:33
  19.7 1.1 %collective-permute-start.5 = (f32[4,4,40]{2,1,0:T(4,128)S(1)}, f32[4,4,40]{2,1,0:T(4,128)S(1)}, u32[]{:S(2)}, u32[]{:S(2)}) collective-permute-start(f32[4,4,40]{2,1,0:T(4,128)S(1)} %get-tuple-element.56), channel_id=1, source_target_pairs={{0,2},{2,0},{1,3},{3,1},{4,6},{6,4},{5,7},{7,5},{8,10},{10,8},{9,1... | collective-permute-start | bytes 7688 | tf_op jit(solution)/shard_map/ppermute | solution.py:370
  20.8 1.1 %shard_map.89.kept_ref = f32[4,4,40]{2,1,0:T(4,128)S(1)} custom-call(bf16[2,160,128]{2,1,0:T(8,128)(2,1)S(1)} %get-tuple-element.55.refs_0_, bf16[2,128,512]{2,1,0:T(8,128)(2,1)S(1)} %get-tuple-element.52.first_ref.refs_1_, bf16[2,3,512,512]{3,2,1,0:T(8,128)(2,1)S(1)} %get-tuple-element.53.middle_ref.refs_2_, ...), custom_call_target="tpu_custom_call" | custom-call | tf_op jit(solution)/shard_map/pallas_call | solution.py:33
  21.9 1.5 %collective-permute-done.5.got_ref = f32[4,4,40]{2,1,0:T(4,128)S(1)} collective-permute-done((f32[4,4,40]{2,1,0:T(4,128)S(1)}, f32[4,4,40]{2,1,0:T(4,128)S(1)}, u32[]{:S(2)}, u32[]{:S(2)}) %collective-permute-start.5) | collective-permute-done | bytes 2592 | tf_op jit(solution)/shard_map/ppermute | solution.py:370
  23.4 4.0 %collective-permute-start.6 = (f32[4,4,40]{2,1,0:T(4,128)S(1)}, f32[4,4,40]{2,1,0:T(4,128)S(1)}, u32[]{:S(2)}, u32[]{:S(2)}) collective-permute-start(f32[4,4,40]{2,1,0:T(4,128)S(1)} %get-tuple-element.58), channel_id=1, source_target_pairs={{0,8},{4,12},{8,0},{12,4},{1,9},{5,13},{9,1},{13,5},{2,10},{6,14},... | collective-permute-start | bytes 7688 | tf_op jit(solution)/shard_map/ppermute | solution.py:370
  27.4 1.6 %collective-permute-done.6.got_ref = f32[4,4,40]{2,1,0:T(4,128)S(1)} collective-permute-done((f32[4,4,40]{2,1,0:T(4,128)S(1)}, f32[4,4,40]{2,1,0:T(4,128)S(1)}, u32[]{:S(2)}, u32[]{:S(2)}) %collective-permute-start.6) | collective-permute-done | bytes 2592 | tf_op jit(solution)/shard_map/ppermute | solution.py:370
  29.1 1.7 %collective-permute-start.7 = (f32[4,4,40]{2,1,0:T(4,128)S(1)}, f32[4,4,40]{2,1,0:T(4,128)S(1)}, u32[]{:S(2)}, u32[]{:S(2)}) collective-permute-start(f32[4,4,40]{2,1,0:T(4,128)S(1)} %get-tuple-element.60), channel_id=1, source_target_pairs={{0,4},{4,0},{8,12},{12,8},{1,5},{5,1},{9,13},{13,9},{2,6},{6,2},{1... | collective-permute-start | bytes 7688 | tf_op jit(solution)/shard_map/ppermute | solution.py:370
  30.8 1.9 %collective-permute-done.7.got_ref = f32[4,4,40]{2,1,0:T(4,128)S(1)} collective-permute-done((f32[4,4,40]{2,1,0:T(4,128)S(1)}, f32[4,4,40]{2,1,0:T(4,128)S(1)}, u32[]{:S(2)}, u32[]{:S(2)}) %collective-permute-start.7) | collective-permute-done | bytes 2592 | tf_op jit(solution)/shard_map/ppermute | solution.py:370
  32.7 0.7 %shard_map.92 = f32[4,320]{1,0:T(4,128)} custom-call(f32[4,4,40]{2,1,0:T(4,128)S(1)} %get-tuple-element.59.kept_ref, f32[4,4,40]{2,1,0:T(4,128)S(1)} %collective-permute-done.7.got_ref), custom_call_target="tpu_custom_call" | custom-call | tf_op jit(solution)/shard_map/pallas_call | solution.py:33
  (5 shorter events, 0.0 us)
Async XLA Ops:
  0.0 1.0 %copy-start = (bf16[64,4,8,128]{3,2,1,0:T(8,128)(2,1)S(1)}, bf16[64,4,8,128]{3,2,1,0:T(8,128)(2,1)}, u32[]{:S(2)}) copy-start(bf16[64,4,8,128]{3,2,1,0:T(8,128)(2,1)} %g_ref.1) | copy-start | bytes 1572868
  1.3 9.4 %collective-permute-start = (bf16[2,8,64,128]{3,2,1,0:T(8,128)(2,1)S(1)}, bf16[2,8,64,128]{3,2,1,0:T(8,128)(2,1)S(1)}, u32[]{:S(2)}, u32[]{:S(2)}) collective-permute-start(bf16[2,8,64,128]{3,2,1,0:T(8,128)(2,1)S(1)} %get-tuple-element.38), channel_id=1, source_target_pairs={{0,4},{1,5},{2,6},{3,7},{4,0},{5,1},{6,2},{7,3},{8,12},{9,13},{10,... | collective-permute-start | bytes 786440 | tf_op jit(solution)/shard_map/ppermute | solution.py:389
  4.4 6.3 %collective-permute-start.1 = (bf16[2,8,64,128]{3,2,1,0:T(8,128)(2,1)S(1)}, bf16[2,8,64,128]{3,2,1,0:T(8,128)(2,1)S(1)}, u32[]{:S(2)}, u32[]{:S(2)}) collective-permute-start(bf16[2,8,64,128]{3,2,1,0:T(8,128)(2,1)S(1)} %get-tuple-element.39), channel_id=1, source_target_pairs={{0,1},{1,0},{2,3},{3,2},{4,8},{5,9},{6,10},{7,11},{8,4},{9,5},{10,... | collective-permute-start | bytes 786440 | tf_op jit(solution)/shard_map/ppermute | solution.py:389
  10.8 5.1 %collective-permute-start.4 = (bf16[8,2,64,128]{3,2,1,0:T(8,128)(2,1)S(1)}, bf16[8,2,64,128]{3,2,1,0:T(8,128)(2,1)S(1)}, u32[]{:S(2)}, u32[]{:S(2)}) collective-permute-start(bf16[8,2,64,128]{3,2,1,0:T(8,128)(2,1)S(1)} %get-tuple-element.46), channel_id=1, source_target_pairs={{0,1},{1,0},{2,3},{3,2},{4,5},{5,4},{6,7},{7,6},{8,9},{9,8},{10,11... | collective-permute-start | bytes 786440 | tf_op jit(solution)/shard_map/ppermute | solution.py:370
  10.9 5.0 %collective-permute-start.2 = (bf16[4,2,64,128]{3,2,1,0:T(8,128)(2,1)S(1)}, bf16[4,2,64,128]{3,2,1,0:T(8,128)(2,1)S(1)}, u32[]{:S(2)}, u32[]{:S(2)}) collective-permute-start(bf16[4,2,64,128]{3,2,1,0:T(8,128)(2,1)S(1)} %get-tuple-element.44), channel_id=1, source_target_pairs={{0,16},{1,2},{2,1},{3,19},{4,20},{5,6},{6,5},{7,23},{8,24},{9,10},... | collective-permute-start | bytes 393224 | tf_op jit(solution)/shard_map/ppermute | solution.py:389
  12.6 5.0 %collective-permute-start.3 = (bf16[4,2,64,128]{3,2,1,0:T(8,128)(2,1)S(1)}, bf16[4,2,64,128]{3,2,1,0:T(8,128)(2,1)S(1)}, u32[]{:S(2)}, u32[]{:S(2)}) collective-permute-start(bf16[4,2,64,128]{3,2,1,0:T(8,128)(2,1)S(1)} %get-tuple-element.45), channel_id=1, source_target_pairs={{0,16},{1,2},{2,1},{3,19},{4,20},{5,6},{6,5},{7,23},{8,24},{9,10},... | collective-permute-start | bytes 393224 | tf_op jit(solution)/shard_map/ppermute | solution.py:389
  19.7 3.7 %collective-permute-start.5 = (f32[4,4,40]{2,1,0:T(4,128)S(1)}, f32[4,4,40]{2,1,0:T(4,128)S(1)}, u32[]{:S(2)}, u32[]{:S(2)}) collective-permute-start(f32[4,4,40]{2,1,0:T(4,128)S(1)} %get-tuple-element.56), channel_id=1, source_target_pairs={{0,2},{2,0},{1,3},{3,1},{4,6},{6,4},{5,7},{7,5},{8,10},{10,8},{9,1... | collective-permute-start | bytes 7688 | tf_op jit(solution)/shard_map/ppermute | solution.py:370
  23.4 5.7 %collective-permute-start.6 = (f32[4,4,40]{2,1,0:T(4,128)S(1)}, f32[4,4,40]{2,1,0:T(4,128)S(1)}, u32[]{:S(2)}, u32[]{:S(2)}) collective-permute-start(f32[4,4,40]{2,1,0:T(4,128)S(1)} %get-tuple-element.58), channel_id=1, source_target_pairs={{0,8},{4,12},{8,0},{12,4},{1,9},{5,13},{9,1},{13,5},{2,10},{6,14},... | collective-permute-start | bytes 7688 | tf_op jit(solution)/shard_map/ppermute | solution.py:370
  29.1 3.7 %collective-permute-start.7 = (f32[4,4,40]{2,1,0:T(4,128)S(1)}, f32[4,4,40]{2,1,0:T(4,128)S(1)}, u32[]{:S(2)}, u32[]{:S(2)}) collective-permute-start(f32[4,4,40]{2,1,0:T(4,128)S(1)} %get-tuple-element.60), channel_id=1, source_target_pairs={{0,4},{4,0},{8,12},{12,8},{1,5},{5,1},{9,13},{13,9},{2,6},{6,2},{1... | collective-permute-start | bytes 7688 | tf_op jit(solution)/shard_map/ppermute | solution.py:370

commit v11 on v10

--- a/solution.py
+++ b/solution.py
@@ -103,7 +103,7 @@
         copies[0].wait()
         count = place_ref.shape[1]
         span_z = wz_ref.shape[0]
-        slots = pick_ref.shape[0]
+        slots = 2 * pick_ref.shape[1]
         brick, line = lax.axis_index("brick"), lax.axis_index(("sect", "slab"))
         last_brick, last_line = lax.axis_size("brick") - 1, lax.axis_size(("sect", "slab")) - 1
         half = slots // 2
@@ -139,7 +139,9 @@
         target = row.astype(jnp.int32)
         slot = ((target % sects) * bricks + target // sects) * capacity + arrival
         pick = jnp.where(iota((slots, count), 0) == slot, 1.0, 0.0).astype(BF16)
-        pick_ref[...] = pick
+        half = slots // 2
+        for s in range(2):
+            pick_ref[s] = pick[s * half : (s + 1) * half]
         copies[2].wait()
         channels = conv_ref.shape[-1]
         group = 9 * channels
@@ -299,20 +301,16 @@
 def outer_body(
     own_ref, halo_ref, cross_ref, corner_ref, ready_ref, kernel_ref, wz_ref, wxy_ref, start_ref,
     pick_ref, attr_ref, first_ref, middle_ref, last_ref,
-    value_ref, row_ref, cross_side,
+    value_ref, table_ref, cross_side,
 ):
     span_x = own_ref.shape[0]
     layers = [*range(HALO), *range(span_x, span_x + 2)]
     units = cross_units(layers, cross_ref, corner_ref, own_ref, halo_ref, cross_side, ready_ref)
     total = share(start_ref[...], units, kernel_ref, wz_ref, wxy_ref)
-    table = jnp.concatenate([total.astype(BF16), attr_ref[...]], axis=0)
-    row = lax.dot_general(
-        pick_ref[...], table, (((1,), (1,)), ((), ())), preferred_element_type=F32
-    ).astype(BF16)
-    half = row.shape[0] // 2
-    for s in range(2):
-        row_ref[s] = row[s * half : (s + 1) * half]
-    network(1 - own_section(), row_ref, first_ref, middle_ref, last_ref, value_ref)
+    table_ref[...] = jnp.concatenate([total.astype(BF16), attr_ref[...]], axis=0)
+    network(
+        1 - own_section(), pick_ref, table_ref, first_ref, middle_ref, last_ref, value_ref
+    )
 
 
 def own_section():
@@ -326,8 +324,11 @@
     )
 
 
-def network(s, row_ref, first_ref, middle_ref, last_ref, value_ref):
-    act = gelu(jnp.dot(row_ref[s], first_ref[s], preferred_element_type=F32)).astype(BF16)
+def network(s, pick_ref, table_ref, first_ref, middle_ref, last_ref, value_ref):
+    row = lax.dot_general(
+        pick_ref[s], table_ref[...], (((1,), (1,)), ((), ())), preferred_element_type=F32
+    ).astype(BF16)
+    act = gelu(jnp.dot(row, first_ref[s], preferred_element_type=F32)).astype(BF16)
     for i in range(middle_ref.shape[1]):
         act = gelu(jnp.dot(act, middle_ref[s, i], preferred_element_type=F32)).astype(BF16)
     value = lax.dot_general(
@@ -427,7 +428,7 @@
     pick, wz, wxy, kernel, attr, first, middle, last = call(
         make_points_body(span_x, span_y, bricks, sects, capacity),
         [
-            block(slots, count),
+            block(2, slots // 2, count),
             block(span_z, count),
             jax.ShapeDtypeStruct(((span_x + 2) * (span_y + 2), count), F32),
             block(2 * channels, 36 * channels),
@@ -477,10 +478,10 @@
         return jax.ShapeDtypeStruct((number, outputs, capacity), F32)
 
     sent, table = call(
-        outer_body, [values(blocks), block(2, slots // 2, point_attr.shape[1] + channels)], [side], 8
+        outer_body, [values(blocks), block(channels + point_attr.shape[1], count)], [side], 8
     )(own_taps, halo_taps, cross, corner, ready, kernel, wz, wxy, total, pick, attr, first, middle, last)
     got = swap(sent, "sect", sects // 2)
-    kept = call(own_body, values(blocks), [], 8)(table, first, middle, last)
+    kept = call(own_body, values(blocks), [], 8)(pick, table, first, middle, last)
     labels = [list(range(blocks)), [blocks + q for q in range(blocks)]]
     step = blocks // 2
     while step:

time: 33.6 us -> 33.5 us (level)
  no operation moved by 1% of the time
where the time goes in v11:
time: 33.5 us; the launch traced here: 33.3 us
  starting transfers between devices  12.1 us (36%)
  Pallas kernels  11 us (33%)
  waiting for transfers between devices  9.05 us (27%)
  local copies, waits for them, and re-layouts  1.04 us (3%)
    pallas_call x11, Pallas kernels, run(): pl.pallas_call(body, out_shape=outs, in_specs=[pl.BlockSpec(memory_space=...  11 us
    ppermute x4, starting transfers between devices, swap(): lax.ppermute(array, axis, [(i, i ^ step) for i in range(lax.axis_size(axi...  6.94 us
    ppermute x4, starting transfers between devices, swap_pairs(): return lax.ppermute(array, everything, pairs)  5.21 us
    ppermute x4, waiting for transfers between devices, swap(): lax.ppermute(array, axis, [(i, i ^ step) for i in range(lax.axis_size(axi...  4.93 us
    ppermute x4, waiting for transfers between devices, swap_pairs(): return lax.ppermute(array, everything, pairs)  4.12 us
    unnamed x2, local copies, waits for them, and re-layouts  1.04 us
  transfers between devices with their start and end apart: 8, of which 5 were waited for; matrix products, arithmetic and copies ran while one was open for 0% of the time, Pallas kernels for 24%

profile of v11, /device:TPU:0, one launch (start us, length us, event | category | flops | bytes accessed | tf_op | source)
XLA Modules:
  0.0 33.3 jit_solution(10285741608385997143)
XLA Ops:
  0.0 1.0 %copy-done = bf16[64,4,8,128]{3,2,1,0:T(8,128)(2,1)S(1)} copy-done((bf16[64,4,8,128]{3,2,1,0:T(8,128)(2,1)S(1)}, bf16[64,4,8,128]{3,2,1,0:T(8,128)(2,1)}, u32[]{:S(2)}) %copy-start) | copy-done | bytes 524312
  1.0 0.2 shard_map.83
  1.3 3.1 %collective-permute-start = (bf16[2,8,64,128]{3,2,1,0:T(8,128)(2,1)S(1)}, bf16[2,8,64,128]{3,2,1,0:T(8,128)(2,1)S(1)}, u32[]{:S(2)}, u32[]{:S(2)}) collective-permute-start(bf16[2,8,64,128]{3,2,1,0:T(8,128)(2,1)S(1)} %get-tuple-element.39), channel_id=1, source_target_pairs={{0,4},{1,5},{2,6},{3,7},{4,0},{5,1},{6,2},{7,3},{8,12},{9,13},{10,... | collective-permute-start | bytes 786440 | tf_op jit(solution)/shard_map/ppermute | solution.py:390
  4.4 0.0 collective-permute-start.1
  4.4 2.2 %shard_map.82 = (bf16[2,160,256]{2,1,0:T(8,128)(2,1)S(1)}, bf16[128,256]{1,0:T(8,128)(2,1)S(1)}, f32[60,256]{1,0:T(8,128)S(1)}, bf16[128,2304]{1,0:T(8,128)(2,1)...) custom-call(f32[3,256]{1,0:T(4,128)} %place_hbm.1, ...), custom_call_target="tpu_custom_call" | custom-call | tf_op jit(solution)/shard_map/pallas_call | solution.py:33
  6.6 1.1 %shard_map.84 = (bf16[4,8,192,128]{3,2,1,0:T(8,128)(2,1)S(1)}, f32[64,256]{1,0:T(8,128)S(1)}) custom-call(bf16[4,8,64,128]{3,2,1,0:T(8,128)(2,1)S(1)} %get-tuple-element.34.own_ref, bf16[128,2304]{1,0:T(8,128)(2,1)S(1)} %get-tuple-element.35.kernel_ref, bf16[128,256]{1,0:T(8,128)(2,1)S(1)} %get-tuple-element.36.wz_ref, f32[60,256]{1,0:T(8,128)S(1)} %get-tuple-element.37.wxy_ref), custom_call_target="tpu_custom_call" | custom-call | tf_op jit(solution)/shard_map/pallas_call | solution.py:33
  7.7 3.0 %collective-permute-done.even_ref = bf16[2,8,64,128]{3,2,1,0:T(8,128)(2,1)S(1)} collective-permute-done((bf16[2,8,64,128]{3,2,1,0:T(8,128)(2,1)S(1)}, bf16[2,8,64,128]{3,2,1,0:T(8,128)(2,1)S(1)}, u32[]{:S(2)}, u32[]{:S(2)}) %collective-permute-start) | collective-permute-done | bytes 262176 | tf_op jit(solution)/shard_map/ppermute | solution.py:390
  10.7 0.1 shard_map.85
  10.8 0.1 collective-permute-start.4
  10.9 1.7 %collective-permute-start.2 = (bf16[4,2,64,128]{3,2,1,0:T(8,128)(2,1)S(1)}, bf16[4,2,64,128]{3,2,1,0:T(8,128)(2,1)S(1)}, u32[]{:S(2)}, u32[]{:S(2)}) collective-permute-start(bf16[4,2,64,128]{3,2,1,0:T(8,128)(2,1)S(1)} %get-tuple-element.45), channel_id=1, source_target_pairs={{0,16},{1,2},{2,1},{3,19},{4,20},{5,6},{6,5},{7,23},{8,24},{9,10},... | collective-permute-start | bytes 393224 | tf_op jit(solution)/shard_map/ppermute | solution.py:390
  12.6 0.3 %collective-permute-start.3 = (bf16[4,2,64,128]{3,2,1,0:T(8,128)(2,1)S(1)}, bf16[4,2,64,128]{3,2,1,0:T(8,128)(2,1)S(1)}, u32[]{:S(2)}, u32[]{:S(2)}) collective-permute-start(bf16[4,2,64,128]{3,2,1,0:T(8,128)(2,1)S(1)} %get-tuple-element.46), channel_id=1, source_target_pairs={{0,16},{1,2},{2,1},{3,19},{4,20},{5,6},{6,5},{7,23},{8,24},{9,10},... | collective-permute-start | bytes 393224 | tf_op jit(solution)/shard_map/ppermute | solution.py:390
  13.0 1.8 %shard_map.86 = (bf16[4,8,192,128]{3,2,1,0:T(8,128)(2,1)S(1)}, f32[64,256]{1,0:T(8,128)S(1)}) custom-call(bf16[4,8,192,128]{3,2,1,0:T(8,128)(2,1)S(1)} %get-tuple-element.38.own_ref, bf16[2,8,64,128]{3,2,1,0:T(8,128)(2,1)S(1)} %get-tuple-element.42.before_ref, bf16[2,8,64,128]{3,2,1,0:T(8,128)(2,1)S(1)} %get-tuple-element.43.after_ref, ...), custom_call_target="tpu_custom_call" | custom-call | tf_op jit(solution)/shard_map/pallas_call | solution.py:33
  14.8 1.1 %collective-permute-done.2.cross_ref = bf16[4,2,64,128]{3,2,1,0:T(8,128)(2,1)S(1)} collective-permute-done((bf16[4,2,64,128]{3,2,1,0:T(8,128)(2,1)S(1)}, bf16[4,2,64,128]{3,2,1,0:T(8,128)(2,1)S(1)}, u32[]{:S(2)}, u32[]{:S(2)}) %collective-permute-start.2) | collective-permute-done | bytes 131104 | tf_op jit(solution)/shard_map/ppermute | solution.py:390
  15.9 1.7 %shard_map.87 = (f32[64,256]{1,0:T(8,128)S(1)}, bf16[4,4,192,128]{3,2,1,0:T(8,128)(2,1)S(1)}) custom-call(bf16[4,8,192,128]{3,2,1,0:T(8,128)(2,1)S(1)} %get-tuple-element.38.own_ref, bf16[4,8,192,128]{3,2,1,0:T(8,128)(2,1)S(1)} %get-tuple-element.44.halo_ref, bf16[8,2,64,128]{3,2,1,0:T(8,128)(2,1)S(1)} %collective-permute-done.4.partner_ref, ...), custom_call_target="tpu_custom_call" | custom-call | tf_op jit(solution)/shard_map/pallas_call | solution.py:33
  17.6 0.0 collective-permute-done.3.corner_ref
  17.6 2.1 %shard_map.88 = (f32[4,4,40]{2,1,0:T(4,128)S(1)}, bf16[128,256]{1,0:T(8,128)(2,1)S(1)}) custom-call(bf16[4,8,192,128]{3,2,1,0:T(8,128)(2,1)S(1)} %get-tuple-element.38.own_ref, bf16[4,8,192,128]{3,2,1,0:T(8,128)(2,1)S(1)} %get-tuple-element.44.halo_ref, bf16[4,2,64,128]{3,2,1,0:T(8,128)(2,1)S(1)} %collective-permute-done.2.cross_ref, ...), custom_call_target="tpu_custom_call" | custom-call | tf_op jit(solution)/shard_map/pallas_call | solution.py:33
  19.7 1.1 %collective-permute-start.5 = (f32[4,4,40]{2,1,0:T(4,128)S(1)}, f32[4,4,40]{2,1,0:T(4,128)S(1)}, u32[]{:S(2)}, u32[]{:S(2)}) collective-permute-start(f32[4,4,40]{2,1,0:T(4,128)S(1)} %get-tuple-element.56), channel_id=1, source_target_pairs={{0,2},{2,0},{1,3},{3,1},{4,6},{6,4},{5,7},{7,5},{8,10},{10,8},{9,1... | collective-permute-start | bytes 7688 | tf_op jit(solution)/shard_map/ppermute | solution.py:371
  20.8 1.2 %shard_map.89.kept_ref = f32[4,4,40]{2,1,0:T(4,128)S(1)} custom-call(bf16[2,160,256]{2,1,0:T(8,128)(2,1)S(1)} %get-tuple-element.33.pick_ref.refs_0_, bf16[128,256]{1,0:T(8,128)(2,1)S(1)} %get-tuple-element.55.refs_1_, bf16[2,128,512]{2,1,0:T(8,128)(2,1)S(1)} %get-tuple-element.52.first_ref.refs_2_, ...), custom_call_target="tpu_custom_call" | custom-call | tf_op jit(solution)/shard_map/pallas_call | solution.py:33
  21.9 1.4 %collective-permute-done.5.got_ref = f32[4,4,40]{2,1,0:T(4,128)S(1)} collective-permute-done((f32[4,4,40]{2,1,0:T(4,128)S(1)}, f32[4,4,40]{2,1,0:T(4,128)S(1)}, u32[]{:S(2)}, u32[]{:S(2)}) %collective-permute-start.5) | collective-permute-done | bytes 2592 | tf_op jit(solution)/shard_map/ppermute | solution.py:371
  23.3 4.0 %collective-permute-start.6 = (f32[4,4,40]{2,1,0:T(4,128)S(1)}, f32[4,4,40]{2,1,0:T(4,128)S(1)}, u32[]{:S(2)}, u32[]{:S(2)}) collective-permute-start(f32[4,4,40]{2,1,0:T(4,128)S(1)} %get-tuple-element.58), channel_id=1, source_target_pairs={{0,8},{4,12},{8,0},{12,4},{1,9},{5,13},{9,1},{13,5},{2,10},{6,14},... | collective-permute-start | bytes 7688 | tf_op jit(solution)/shard_map/ppermute | solution.py:371
  27.4 1.6 %collective-permute-done.6.got_ref = f32[4,4,40]{2,1,0:T(4,128)S(1)} collective-permute-done((f32[4,4,40]{2,1,0:T(4,128)S(1)}, f32[4,4,40]{2,1,0:T(4,128)S(1)}, u32[]{:S(2)}, u32[]{:S(2)}) %collective-permute-start.6) | collective-permute-done | bytes 2592 | tf_op jit(solution)/shard_map/ppermute | solution.py:371
  29.0 1.7 %collective-permute-start.7 = (f32[4,4,40]{2,1,0:T(4,128)S(1)}, f32[4,4,40]{2,1,0:T(4,128)S(1)}, u32[]{:S(2)}, u32[]{:S(2)}) collective-permute-start(f32[4,4,40]{2,1,0:T(4,128)S(1)} %get-tuple-element.60), channel_id=1, source_target_pairs={{0,4},{4,0},{8,12},{12,8},{1,5},{5,1},{9,13},{13,9},{2,6},{6,2},{1... | collective-permute-start | bytes 7688 | tf_op jit(solution)/shard_map/ppermute | solution.py:371
  30.7 1.9 %collective-permute-done.7.got_ref = f32[4,4,40]{2,1,0:T(4,128)S(1)} collective-permute-done((f32[4,4,40]{2,1,0:T(4,128)S(1)}, f32[4,4,40]{2,1,0:T(4,128)S(1)}, u32[]{:S(2)}, u32[]{:S(2)}) %collective-permute-start.7) | collective-permute-done | bytes 2592 | tf_op jit(solution)/shard_map/ppermute | solution.py:371
  32.7 0.7 %shard_map.92 = f32[4,320]{1,0:T(4,128)} custom-call(f32[4,4,40]{2,1,0:T(4,128)S(1)} %get-tuple-element.59.kept_ref, f32[4,4,40]{2,1,0:T(4,128)S(1)} %collective-permute-done.7.got_ref), custom_call_target="tpu_custom_call" | custom-call | tf_op jit(solution)/shard_map/pallas_call | solution.py:33
  (5 shorter events, 0.0 us)
Async XLA Ops:
  0.0 1.0 %copy-start = (bf16[64,4,8,128]{3,2,1,0:T(8,128)(2,1)S(1)}, bf16[64,4,8,128]{3,2,1,0:T(8,128)(2,1)}, u32[]{:S(2)}) copy-start(bf16[64,4,8,128]{3,2,1,0:T(8,128)(2,1)} %g_ref.1) | copy-start | bytes 1572868
  1.3 9.4 %collective-permute-start = (bf16[2,8,64,128]{3,2,1,0:T(8,128)(2,1)S(1)}, bf16[2,8,64,128]{3,2,1,0:T(8,128)(2,1)S(1)}, u32[]{:S(2)}, u32[]{:S(2)}) collective-permute-start(bf16[2,8,64,128]{3,2,1,0:T(8,128)(2,1)S(1)} %get-tuple-element.39), channel_id=1, source_target_pairs={{0,4},{1,5},{2,6},{3,7},{4,0},{5,1},{6,2},{7,3},{8,12},{9,13},{10,... | collective-permute-start | bytes 786440 | tf_op jit(solution)/shard_map/ppermute | solution.py:390
  4.4 6.3 %collective-permute-start.1 = (bf16[2,8,64,128]{3,2,1,0:T(8,128)(2,1)S(1)}, bf16[2,8,64,128]{3,2,1,0:T(8,128)(2,1)S(1)}, u32[]{:S(2)}, u32[]{:S(2)}) collective-permute-start(bf16[2,8,64,128]{3,2,1,0:T(8,128)(2,1)S(1)} %get-tuple-element.40), channel_id=1, source_target_pairs={{0,1},{1,0},{2,3},{3,2},{4,8},{5,9},{6,10},{7,11},{8,4},{9,5},{10,... | collective-permute-start | bytes 786440 | tf_op jit(solution)/shard_map/ppermute | solution.py:390
  10.8 5.1 %collective-permute-start.4 = (bf16[8,2,64,128]{3,2,1,0:T(8,128)(2,1)S(1)}, bf16[8,2,64,128]{3,2,1,0:T(8,128)(2,1)S(1)}, u32[]{:S(2)}, u32[]{:S(2)}) collective-permute-start(bf16[8,2,64,128]{3,2,1,0:T(8,128)(2,1)S(1)} %get-tuple-element.47), channel_id=1, source_target_pairs={{0,1},{1,0},{2,3},{3,2},{4,5},{5,4},{6,7},{7,6},{8,9},{9,8},{10,11... | collective-permute-start | bytes 786440 | tf_op jit(solution)/shard_map/ppermute | solution.py:371
  10.9 5.0 %collective-permute-start.2 = (bf16[4,2,64,128]{3,2,1,0:T(8,128)(2,1)S(1)}, bf16[4,2,64,128]{3,2,1,0:T(8,128)(2,1)S(1)}, u32[]{:S(2)}, u32[]{:S(2)}) collective-permute-start(bf16[4,2,64,128]{3,2,1,0:T(8,128)(2,1)S(1)} %get-tuple-element.45), channel_id=1, source_target_pairs={{0,16},{1,2},{2,1},{3,19},{4,20},{5,6},{6,5},{7,23},{8,24},{9,10},... | collective-permute-start | bytes 393224 | tf_op jit(solution)/shard_map/ppermute | solution.py:390
  12.6 5.0 %collective-permute-start.3 = (bf16[4,2,64,128]{3,2,1,0:T(8,128)(2,1)S(1)}, bf16[4,2,64,128]{3,2,1,0:T(8,128)(2,1)S(1)}, u32[]{:S(2)}, u32[]{:S(2)}) collective-permute-start(bf16[4,2,64,128]{3,2,1,0:T(8,128)(2,1)S(1)} %get-tuple-element.46), channel_id=1, source_target_pairs={{0,16},{1,2},{2,1},{3,19},{4,20},{5,6},{6,5},{7,23},{8,24},{9,10},... | collective-permute-start | bytes 393224 | tf_op jit(solution)/shard_map/ppermute | solution.py:390
  19.7 3.7 %collective-permute-start.5 = (f32[4,4,40]{2,1,0:T(4,128)S(1)}, f32[4,4,40]{2,1,0:T(4,128)S(1)}, u32[]{:S(2)}, u32[]{:S(2)}) collective-permute-start(f32[4,4,40]{2,1,0:T(4,128)S(1)} %get-tuple-element.56), channel_id=1, source_target_pairs={{0,2},{2,0},{1,3},{3,1},{4,6},{6,4},{5,7},{7,5},{8,10},{10,8},{9,1... | collective-permute-start | bytes 7688 | tf_op jit(solution)/shard_map/ppermute | solution.py:371
  23.3 5.7 %collective-permute-start.6 = (f32[4,4,40]{2,1,0:T(4,128)S(1)}, f32[4,4,40]{2,1,0:T(4,128)S(1)}, u32[]{:S(2)}, u32[]{:S(2)}) collective-permute-start(f32[4,4,40]{2,1,0:T(4,128)S(1)} %get-tuple-element.58), channel_id=1, source_target_pairs={{0,8},{4,12},{8,0},{12,4},{1,9},{5,13},{9,1},{13,5},{2,10},{6,14},... | collective-permute-start | bytes 7688 | tf_op jit(solution)/shard_map/ppermute | solution.py:371
  29.0 3.7 %collective-permute-start.7 = (f32[4,4,40]{2,1,0:T(4,128)S(1)}, f32[4,4,40]{2,1,0:T(4,128)S(1)}, u32[]{:S(2)}, u32[]{:S(2)}) collective-permute-start(f32[4,4,40]{2,1,0:T(4,128)S(1)} %get-tuple-element.60), channel_id=1, source_target_pairs={{0,4},{4,0},{8,12},{12,8},{1,5},{5,1},{9,13},{13,9},{2,6},{6,2},{1... | collective-permute-start | bytes 7688 | tf_op jit(solution)/shard_map/ppermute | solution.py:371

commit v12 on v11

--- a/solution.py
+++ b/solution.py
@@ -167,7 +167,7 @@
         jnp.where(keep & inside, 1.0, 0.0).astype(BF16)
         for keep in (lane > 0, lane >= 0, lane < span_z - 1)
     )
-    pieces = (pltpu.roll(tile, 1, 1) * below, tile * here, pltpu.roll(tile, span_z - 1, 1) * above)
+    pieces = (pltpu.roll(tile, 1, 1) * below, tile if inside is True else tile * here, pltpu.roll(tile, span_z - 1, 1) * above)
     return jnp.concatenate(pieces, axis=0)
 
 
@@ -328,11 +328,17 @@
     row = lax.dot_general(
         pick_ref[s], table_ref[...], (((1,), (1,)), ((), ())), preferred_element_type=F32
     ).astype(BF16)
-    act = gelu(jnp.dot(row, first_ref[s], preferred_element_type=F32)).astype(BF16)
-    for i in range(middle_ref.shape[1]):
-        act = gelu(jnp.dot(act, middle_ref[s, i], preferred_element_type=F32)).astype(BF16)
+    half = row.shape[0] // 2
+    acts = [row[:half], row[half:]]
+    for weights in [first_ref[s]] + [middle_ref[s, i] for i in range(middle_ref.shape[1])]:
+        acts = [
+            gelu(jnp.dot(act, weights, preferred_element_type=F32)).astype(BF16) for act in acts
+        ]
     value = lax.dot_general(
-        last_ref[s], act, (((1,), (1,)), ((), ())), preferred_element_type=F32
+        last_ref[s],
+        jnp.concatenate(acts, axis=0),
+        (((1,), (1,)), ((), ())),
+        preferred_element_type=F32,
     )
     blocks, _, capacity = value_ref.shape
     place = own_place()

time: 33.5 us -> 33.5 us (level)
  no operation moved by 1% of the time
where the time goes in v12:
time: 33.5 us; the launch traced here: 33.3 us
  starting transfers between devices  12.1 us (36%)
  Pallas kernels  11 us (33%)
  waiting for transfers between devices  9.05 us (27%)
  local copies, waits for them, and re-layouts  1.04 us (3%)
    pallas_call x11, Pallas kernels, run(): pl.pallas_call(body, out_shape=outs, in_specs=[pl.BlockSpec(memory_space=...  11 us
    ppermute x4, starting transfers between devices, swap(): lax.ppermute(array, axis, [(i, i ^ step) for i in range(lax.axis_size(axi...  6.94 us
    ppermute x4, starting transfers between devices, swap_pairs(): return lax.ppermute(array, everything, pairs)  5.21 us
    ppermute x4, waiting for transfers between devices, swap(): lax.ppermute(array, axis, [(i, i ^ step) for i in range(lax.axis_size(axi...  4.95 us
    ppermute x4, waiting for transfers between devices, swap_pairs(): return lax.ppermute(array, everything, pairs)  4.11 us
    unnamed x2, local copies, waits for them, and re-layouts  1.04 us
  transfers between devices with their start and end apart: 8, of which 5 were waited for; matrix products, arithmetic and copies ran while one was open for 0% of the time, Pallas kernels for 24%

profile of v12, /device:TPU:0, one launch (start us, length us, event | category | flops | bytes accessed | tf_op | source)
XLA Modules:
  0.0 33.3 jit_solution(6768286585413123435)
XLA Ops:
  0.0 1.0 %copy-done = bf16[64,4,8,128]{3,2,1,0:T(8,128)(2,1)S(1)} copy-done((bf16[64,4,8,128]{3,2,1,0:T(8,128)(2,1)S(1)}, bf16[64,4,8,128]{3,2,1,0:T(8,128)(2,1)}, u32[]{:S(2)}) %copy-start) | copy-done | bytes 524312
  1.0 0.2 shard_map.83
  1.3 3.1 %collective-permute-start = (bf16[2,8,64,128]{3,2,1,0:T(8,128)(2,1)S(1)}, bf16[2,8,64,128]{3,2,1,0:T(8,128)(2,1)S(1)}, u32[]{:S(2)}, u32[]{:S(2)}) collective-permute-start(bf16[2,8,64,128]{3,2,1,0:T(8,128)(2,1)S(1)} %get-tuple-element.39), channel_id=1, source_target_pairs={{0,4},{1,5},{2,6},{3,7},{4,0},{5,1},{6,2},{7,3},{8,12},{9,13},{10,... | collective-permute-start | bytes 786440 | tf_op jit(solution)/shard_map/ppermute | solution.py:396
  4.4 0.0 collective-permute-start.1
  4.4 2.2 %shard_map.82 = (bf16[2,160,256]{2,1,0:T(8,128)(2,1)S(1)}, bf16[128,256]{1,0:T(8,128)(2,1)S(1)}, f32[60,256]{1,0:T(8,128)S(1)}, bf16[128,2304]{1,0:T(8,128)(2,1)...) custom-call(f32[3,256]{1,0:T(4,128)} %place_hbm.1, ...), custom_call_target="tpu_custom_call" | custom-call | tf_op jit(solution)/shard_map/pallas_call | solution.py:33
  6.6 1.1 %shard_map.84 = (bf16[4,8,192,128]{3,2,1,0:T(8,128)(2,1)S(1)}, f32[64,256]{1,0:T(8,128)S(1)}) custom-call(bf16[4,8,64,128]{3,2,1,0:T(8,128)(2,1)S(1)} %get-tuple-element.34.own_ref, bf16[128,2304]{1,0:T(8,128)(2,1)S(1)} %get-tuple-element.35.kernel_ref, bf16[128,256]{1,0:T(8,128)(2,1)S(1)} %get-tuple-element.36.wz_ref, f32[60,256]{1,0:T(8,128)S(1)} %get-tuple-element.37.wxy_ref), custom_call_target="tpu_custom_call" | custom-call | tf_op jit(solution)/shard_map/pallas_call | solution.py:33
  7.7 3.0 %collective-permute-done.even_ref = bf16[2,8,64,128]{3,2,1,0:T(8,128)(2,1)S(1)} collective-permute-done((bf16[2,8,64,128]{3,2,1,0:T(8,128)(2,1)S(1)}, bf16[2,8,64,128]{3,2,1,0:T(8,128)(2,1)S(1)}, u32[]{:S(2)}, u32[]{:S(2)}) %collective-permute-start) | collective-permute-done | bytes 262176 | tf_op jit(solution)/shard_map/ppermute | solution.py:396
  10.7 0.1 shard_map.85
  10.8 0.1 collective-permute-start.4
  10.9 1.7 %collective-permute-start.2 = (bf16[4,2,64,128]{3,2,1,0:T(8,128)(2,1)S(1)}, bf16[4,2,64,128]{3,2,1,0:T(8,128)(2,1)S(1)}, u32[]{:S(2)}, u32[]{:S(2)}) collective-permute-start(bf16[4,2,64,128]{3,2,1,0:T(8,128)(2,1)S(1)} %get-tuple-element.45), channel_id=1, source_target_pairs={{0,16},{1,2},{2,1},{3,19},{4,20},{5,6},{6,5},{7,23},{8,24},{9,10},... | collective-permute-start | bytes 393224 | tf_op jit(solution)/shard_map/ppermute | solution.py:396
  12.6 0.3 %collective-permute-start.3 = (bf16[4,2,64,128]{3,2,1,0:T(8,128)(2,1)S(1)}, bf16[4,2,64,128]{3,2,1,0:T(8,128)(2,1)S(1)}, u32[]{:S(2)}, u32[]{:S(2)}) collective-permute-start(bf16[4,2,64,128]{3,2,1,0:T(8,128)(2,1)S(1)} %get-tuple-element.46), channel_id=1, source_target_pairs={{0,16},{1,2},{2,1},{3,19},{4,20},{5,6},{6,5},{7,23},{8,24},{9,10},... | collective-permute-start | bytes 393224 | tf_op jit(solution)/shard_map/ppermute | solution.py:396
  13.0 1.8 %shard_map.86 = (bf16[4,8,192,128]{3,2,1,0:T(8,128)(2,1)S(1)}, f32[64,256]{1,0:T(8,128)S(1)}) custom-call(bf16[4,8,192,128]{3,2,1,0:T(8,128)(2,1)S(1)} %get-tuple-element.38.own_ref, bf16[2,8,64,128]{3,2,1,0:T(8,128)(2,1)S(1)} %get-tuple-element.42.before_ref, bf16[2,8,64,128]{3,2,1,0:T(8,128)(2,1)S(1)} %get-tuple-element.43.after_ref, ...), custom_call_target="tpu_custom_call" | custom-call | tf_op jit(solution)/shard_map/pallas_call | solution.py:33
  14.8 1.1 %collective-permute-done.2.cross_ref = bf16[4,2,64,128]{3,2,1,0:T(8,128)(2,1)S(1)} collective-permute-done((bf16[4,2,64,128]{3,2,1,0:T(8,128)(2,1)S(1)}, bf16[4,2,64,128]{3,2,1,0:T(8,128)(2,1)S(1)}, u32[]{:S(2)}, u32[]{:S(2)}) %collective-permute-start.2) | collective-permute-done | bytes 131104 | tf_op jit(solution)/shard_map/ppermute | solution.py:396
  15.9 1.7 %shard_map.87 = (f32[64,256]{1,0:T(8,128)S(1)}, bf16[4,4,192,128]{3,2,1,0:T(8,128)(2,1)S(1)}) custom-call(bf16[4,8,192,128]{3,2,1,0:T(8,128)(2,1)S(1)} %get-tuple-element.38.own_ref, bf16[4,8,192,128]{3,2,1,0:T(8,128)(2,1)S(1)} %get-tuple-element.44.halo_ref, bf16[8,2,64,128]{3,2,1,0:T(8,128)(2,1)S(1)} %collective-permute-done.4.partner_ref, ...), custom_call_target="tpu_custom_call" | custom-call | tf_op jit(solution)/shard_map/pallas_call | solution.py:33
  17.6 0.0 collective-permute-done.3.corner_ref
  17.6 2.0 %shard_map.88 = (f32[4,4,40]{2,1,0:T(4,128)S(1)}, bf16[128,256]{1,0:T(8,128)(2,1)S(1)}) custom-call(bf16[4,8,192,128]{3,2,1,0:T(8,128)(2,1)S(1)} %get-tuple-element.38.own_ref, bf16[4,8,192,128]{3,2,1,0:T(8,128)(2,1)S(1)} %get-tuple-element.44.halo_ref, bf16[4,2,64,128]{3,2,1,0:T(8,128)(2,1)S(1)} %collective-permute-done.2.cross_ref, ...), custom_call_target="tpu_custom_call" | custom-call | tf_op jit(solution)/shard_map/pallas_call | solution.py:33
  19.6 1.1 %collective-permute-start.5 = (f32[4,4,40]{2,1,0:T(4,128)S(1)}, f32[4,4,40]{2,1,0:T(4,128)S(1)}, u32[]{:S(2)}, u32[]{:S(2)}) collective-permute-start(f32[4,4,40]{2,1,0:T(4,128)S(1)} %get-tuple-element.56), channel_id=1, source_target_pairs={{0,2},{2,0},{1,3},{3,1},{4,6},{6,4},{5,7},{7,5},{8,10},{10,8},{9,1... | collective-permute-start | bytes 7688 | tf_op jit(solution)/shard_map/ppermute | solution.py:377
  20.7 1.2 %shard_map.89.kept_ref = f32[4,4,40]{2,1,0:T(4,128)S(1)} custom-call(bf16[2,160,256]{2,1,0:T(8,128)(2,1)S(1)} %get-tuple-element.33.pick_ref.refs_0_, bf16[128,256]{1,0:T(8,128)(2,1)S(1)} %get-tuple-element.55.refs_1_, bf16[2,128,512]{2,1,0:T(8,128)(2,1)S(1)} %get-tuple-element.52.first_ref.refs_2_, ...), custom_call_target="tpu_custom_call" | custom-call | tf_op jit(solution)/shard_map/pallas_call | solution.py:33
  21.9 1.4 %collective-permute-done.5.got_ref = f32[4,4,40]{2,1,0:T(4,128)S(1)} collective-permute-done((f32[4,4,40]{2,1,0:T(4,128)S(1)}, f32[4,4,40]{2,1,0:T(4,128)S(1)}, u32[]{:S(2)}, u32[]{:S(2)}) %collective-permute-start.5) | collective-permute-done | bytes 2592 | tf_op jit(solution)/shard_map/ppermute | solution.py:377
  23.3 4.0 %collective-permute-start.6 = (f32[4,4,40]{2,1,0:T(4,128)S(1)}, f32[4,4,40]{2,1,0:T(4,128)S(1)}, u32[]{:S(2)}, u32[]{:S(2)}) collective-permute-start(f32[4,4,40]{2,1,0:T(4,128)S(1)} %get-tuple-element.58), channel_id=1, source_target_pairs={{0,8},{4,12},{8,0},{12,4},{1,9},{5,13},{9,1},{13,5},{2,10},{6,14},... | collective-permute-start | bytes 7688 | tf_op jit(solution)/shard_map/ppermute | solution.py:377
  27.3 1.6 %collective-permute-done.6.got_ref = f32[4,4,40]{2,1,0:T(4,128)S(1)} collective-permute-done((f32[4,4,40]{2,1,0:T(4,128)S(1)}, f32[4,4,40]{2,1,0:T(4,128)S(1)}, u32[]{:S(2)}, u32[]{:S(2)}) %collective-permute-start.6) | collective-permute-done | bytes 2592 | tf_op jit(solution)/shard_map/ppermute | solution.py:377
  29.0 1.7 %collective-permute-start.7 = (f32[4,4,40]{2,1,0:T(4,128)S(1)}, f32[4,4,40]{2,1,0:T(4,128)S(1)}, u32[]{:S(2)}, u32[]{:S(2)}) collective-permute-start(f32[4,4,40]{2,1,0:T(4,128)S(1)} %get-tuple-element.60), channel_id=1, source_target_pairs={{0,4},{4,0},{8,12},{12,8},{1,5},{5,1},{9,13},{13,9},{2,6},{6,2},{1... | collective-permute-start | bytes 7688 | tf_op jit(solution)/shard_map/ppermute | solution.py:377
  30.7 1.9 %collective-permute-done.7.got_ref = f32[4,4,40]{2,1,0:T(4,128)S(1)} collective-permute-done((f32[4,4,40]{2,1,0:T(4,128)S(1)}, f32[4,4,40]{2,1,0:T(4,128)S(1)}, u32[]{:S(2)}, u32[]{:S(2)}) %collective-permute-start.7) | collective-permute-done | bytes 2592 | tf_op jit(solution)/shard_map/ppermute | solution.py:377
  32.6 0.7 %shard_map.92 = f32[4,320]{1,0:T(4,128)} custom-call(f32[4,4,40]{2,1,0:T(4,128)S(1)} %get-tuple-element.59.kept_ref, f32[4,4,40]{2,1,0:T(4,128)S(1)} %collective-permute-done.7.got_ref), custom_call_target="tpu_custom_call" | custom-call | tf_op jit(solution)/shard_map/pallas_call | solution.py:33
  (5 shorter events, 0.0 us)
Async XLA Ops:
  0.0 1.0 %copy-start = (bf16[64,4,8,128]{3,2,1,0:T(8,128)(2,1)S(1)}, bf16[64,4,8,128]{3,2,1,0:T(8,128)(2,1)}, u32[]{:S(2)}) copy-start(bf16[64,4,8,128]{3,2,1,0:T(8,128)(2,1)} %g_ref.1) | copy-start | bytes 1572868
  1.3 9.4 %collective-permute-start = (bf16[2,8,64,128]{3,2,1,0:T(8,128)(2,1)S(1)}, bf16[2,8,64,128]{3,2,1,0:T(8,128)(2,1)S(1)}, u32[]{:S(2)}, u32[]{:S(2)}) collective-permute-start(bf16[2,8,64,128]{3,2,1,0:T(8,128)(2,1)S(1)} %get-tuple-element.39), channel_id=1, source_target_pairs={{0,4},{1,5},{2,6},{3,7},{4,0},{5,1},{6,2},{7,3},{8,12},{9,13},{10,... | collective-permute-start | bytes 786440 | tf_op jit(solution)/shard_map/ppermute | solution.py:396
  4.4 6.3 %collective-permute-start.1 = (bf16[2,8,64,128]{3,2,1,0:T(8,128)(2,1)S(1)}, bf16[2,8,64,128]{3,2,1,0:T(8,128)(2,1)S(1)}, u32[]{:S(2)}, u32[]{:S(2)}) collective-permute-start(bf16[2,8,64,128]{3,2,1,0:T(8,128)(2,1)S(1)} %get-tuple-element.40), channel_id=1, source_target_pairs={{0,1},{1,0},{2,3},{3,2},{4,8},{5,9},{6,10},{7,11},{8,4},{9,5},{10,... | collective-permute-start | bytes 786440 | tf_op jit(solution)/shard_map/ppermute | solution.py:396
  10.8 5.1 %collective-permute-start.4 = (bf16[8,2,64,128]{3,2,1,0:T(8,128)(2,1)S(1)}, bf16[8,2,64,128]{3,2,1,0:T(8,128)(2,1)S(1)}, u32[]{:S(2)}, u32[]{:S(2)}) collective-permute-start(bf16[8,2,64,128]{3,2,1,0:T(8,128)(2,1)S(1)} %get-tuple-element.47), channel_id=1, source_target_pairs={{0,1},{1,0},{2,3},{3,2},{4,5},{5,4},{6,7},{7,6},{8,9},{9,8},{10,11... | collective-permute-start | bytes 786440 | tf_op jit(solution)/shard_map/ppermute | solution.py:377
  10.9 5.0 %collective-permute-start.2 = (bf16[4,2,64,128]{3,2,1,0:T(8,128)(2,1)S(1)}, bf16[4,2,64,128]{3,2,1,0:T(8,128)(2,1)S(1)}, u32[]{:S(2)}, u32[]{:S(2)}) collective-permute-start(bf16[4,2,64,128]{3,2,1,0:T(8,128)(2,1)S(1)} %get-tuple-element.45), channel_id=1, source_target_pairs={{0,16},{1,2},{2,1},{3,19},{4,20},{5,6},{6,5},{7,23},{8,24},{9,10},... | collective-permute-start | bytes 393224 | tf_op jit(solution)/shard_map/ppermute | solution.py:396
  12.6 5.0 %collective-permute-start.3 = (bf16[4,2,64,128]{3,2,1,0:T(8,128)(2,1)S(1)}, bf16[4,2,64,128]{3,2,1,0:T(8,128)(2,1)S(1)}, u32[]{:S(2)}, u32[]{:S(2)}) collective-permute-start(bf16[4,2,64,128]{3,2,1,0:T(8,128)(2,1)S(1)} %get-tuple-element.46), channel_id=1, source_target_pairs={{0,16},{1,2},{2,1},{3,19},{4,20},{5,6},{6,5},{7,23},{8,24},{9,10},... | collective-permute-start | bytes 393224 | tf_op jit(solution)/shard_map/ppermute | solution.py:396
  19.6 3.7 %collective-permute-start.5 = (f32[4,4,40]{2,1,0:T(4,128)S(1)}, f32[4,4,40]{2,1,0:T(4,128)S(1)}, u32[]{:S(2)}, u32[]{:S(2)}) collective-permute-start(f32[4,4,40]{2,1,0:T(4,128)S(1)} %get-tuple-element.56), channel_id=1, source_target_pairs={{0,2},{2,0},{1,3},{3,1},{4,6},{6,4},{5,7},{7,5},{8,10},{10,8},{9,1... | collective-permute-start | bytes 7688 | tf_op jit(solution)/shard_map/ppermute | solution.py:377
  23.3 5.7 %collective-permute-start.6 = (f32[4,4,40]{2,1,0:T(4,128)S(1)}, f32[4,4,40]{2,1,0:T(4,128)S(1)}, u32[]{:S(2)}, u32[]{:S(2)}) collective-permute-start(f32[4,4,40]{2,1,0:T(4,128)S(1)} %get-tuple-element.58), channel_id=1, source_target_pairs={{0,8},{4,12},{8,0},{12,4},{1,9},{5,13},{9,1},{13,5},{2,10},{6,14},... | collective-permute-start | bytes 7688 | tf_op jit(solution)/shard_map/ppermute | solution.py:377
  29.0 3.7 %collective-permute-start.7 = (f32[4,4,40]{2,1,0:T(4,128)S(1)}, f32[4,4,40]{2,1,0:T(4,128)S(1)}, u32[]{:S(2)}, u32[]{:S(2)}) collective-permute-start(f32[4,4,40]{2,1,0:T(4,128)S(1)} %get-tuple-element.60), channel_id=1, source_target_pairs={{0,4},{4,0},{8,12},{12,8},{1,5},{5,1},{9,13},{13,9},{2,6},{6,2},{1... | collective-permute-start | bytes 7688 | tf_op jit(solution)/shard_map/ppermute | solution.py:377
